TPU v7x, 128 devices: a whole 4x4x4 slice. The times are simulated.
128 devices in a mesh: row: 4 (over z_lo, core), col: 16 (over y, x), filt: 2 (over z_hi).
Axes of the slice: x: 4, y: 4, z: 4 (z_hi: 2, z_lo: 2; z = z_hi * 2 + z_lo), core: 2. Of those that a mesh axis runs over, the one named last changes fastest.
Arguments:
- grad_out: bfloat16 [16, 128, 256, 256], P(None, 'row', 'col', 'filt'), may hold values from -6 to 6
- pre_act: bfloat16 [16, 128, 256, 256], P(None, 'row', 'col', 'filt'), may hold values from -6 to 6
- weight_one: bfloat16 [3, 3, 256, 256], replicated, may hold values from -0.125 to 0.125
- weight_two: bfloat16 [3, 3, 256, 256], replicated, may hold values from -0.125 to 0.125
Outputs:
- grad_in: bfloat16 [16, 128, 256, 256], P(None, 'row', 'col', 'filt')
All inputs are finite; a program needn't handle non-finite values.
Results may differ from a plain program's by a relative error of at most 0.0049.
Values may be sent and summed in bfloat16 or wider, within the bound.
No kernel may reach another device: no remote copies, remote signals or barrier semaphores. Data moves between devices by JAX's collectives and lax.ppermute only.
A program may use at most 192 MiB of HBM per device.

v0:
```python
import jax
import jax.numpy as jnp
from jax import lax
from jax.sharding import PartitionSpec as P


def padded_2(cells, sides, width):
    for axis, dim in sides:
        count = lax.axis_size(axis)
        ends = count - 1
        head = lax.slice_in_dim(cells, 0, width, axis=dim)
        tail = lax.slice_in_dim(cells, cells.shape[dim] - width, cells.shape[dim], axis=dim)
        cells = jnp.concatenate(
            [
                lax.ppermute(tail, axis, [(i, (i + 1) % count) for i in range(ends)]),
                cells,
                lax.ppermute(head, axis, [((i + 1) % count, i) for i in range(ends)]),
            ],
            axis=dim,
        )
    return cells


def tap_sum(padded, weight, spacing, rows, cols):
    total = None
    for tap_row in range(3):
        for tap_col in range(3):
            top = spacing * (2 - tap_row)
            left = spacing * (2 - tap_col)
            piece = padded[:, top : top + rows, left : left + cols, :]
            term = jnp.einsum(
                "bhwo,io->bhwi", piece, weight[tap_row, tap_col], preferred_element_type=jnp.float32
            )
            total = term if total is None else total + term
    return total


def per_device(grad_out, pre_act, weight_one, weight_two):
    rows = grad_out.shape[1]
    cols = grad_out.shape[2]
    own_width = grad_out.shape[3]
    first_channel = lax.axis_index("filt") * own_width
    outer = padded_2(grad_out, (("row", 1), ("col", 2)), 4)
    cols_two = lax.dynamic_slice_in_dim(weight_two, first_channel, own_width, 3)
    grad_a = lax.psum_scatter(
        tap_sum(outer, cols_two, 4, rows, cols), "filt", scatter_dimension=3, tiled=True
    )
    grad_h = jnp.where(pre_act > 0, grad_a, jnp.float32(0.0)).astype(jnp.bfloat16)
    inner = padded_2(grad_h, (("row", 1), ("col", 2)), 2)
    cols_one = lax.dynamic_slice_in_dim(weight_one, first_channel, own_width, 3)
    grad_in = lax.psum_scatter(
        tap_sum(inner, cols_one, 2, rows, cols), "filt", scatter_dimension=3, tiled=True
    )
    return grad_in.astype(jnp.bfloat16)


def solution(mesh):
    placed = (P(None, "row", "col", "filt"), P(None, "row", "col", "filt"), P(), P())
    return jax.shard_map(
        per_device,
        mesh=mesh,
        in_specs=placed,
        out_specs=P(None, "row", "col", "filt"),
        check_vma=False,
    )
```

profile of v0, /device:TPU:9, one launch (start us, length us, event | category | flops | bytes accessed | tf_op | source)
XLA Modules:
  0.0 400.0 jit_solution(17624767567661599678)
XLA Ops:
  6.5 1.9 fusion.82
  8.4 4.1 %collective-permute-start = (bf16[16,4,16,128]{3,2,1,0:T(8,128)(2,1)S(1)}, bf16[16,4,16,128]{3,2,1,0:T(8,128)(2,1)S(1)}, u32[]{:S(2)}, u32[]{:S(2)}) collective-permute-start(bf16[16,4,16,128]{3,2,1,0:T(8,128)(2,1)S(1)} %get-tuple-element.14), channel_id=1, source_target_pairs={{0,32},{32,64},{64,96},{1,33},{33,65},{65,97},{2,34},{34,66},{66,9... | collective-permute-start | bytes 786440 | tf_op jit(solution)/shard_map/ppermute | solution.py:15
  12.5 1.9 collective-permute-start.1
  14.4 1.4 collective-permute-done
  15.8 0.0 copy-start.4
  15.8 2.3 constant_dynamic-update-slice_fusion.1
  18.2 2.3 collective-permute-done.1
  20.5 1.0 constant_dynamic-update-slice_fusion
  21.5 1.5 copy-done.2
  23.0 1.6 fusion.80
  24.6 3.1 collective-permute-start.3
  27.7 4.5 %fusion.51 = f32[256,16,32,16]{0,3,2,1:T(8,128)} fusion(bf16[16,32,16,128]{3,2,1,0:T(8,128)(2,1)S(1)} %copy-done.4, bf16[3,3,256,256]{3,2,1,0:T(8,128)(2,1)S(1)} %copy-done, s32[]{:T(128)S(6)} %add.73, s32[]{:T(128)S(6)} %select_n.8), kind=kOutput, calls=%fused_computation.77 | convolution fusion | flops 536870912 | bytes 10551304 | tf_op jit(solution)/shard_map/bhwo,io->bhwi/dot_general | solution.py:31
  32.2 4.4 %collective-permute-start.2 = (bf16[16,40,4,128]{3,2,1,0:T(4,128)(2,1)}, bf16[16,40,4,128]{3,2,1,0:T(4,128)(2,1)S(1)}, u32[]{:S(2)}, u32[]{:S(2)}) collective-permute-start(bf16[16,40,4,128]{3,2,1,0:T(4,128)(2,1)} %get-tuple-element.6), channel_id=1, source_target_pairs={{2,0},{4,2},{6,4},{8,6},{10,8},{12,10},{14,12},{16,14},{18,16},{20... | collective-permute-start | bytes 1966088 | tf_op jit(solution)/shard_map/ppermute | solution.py:17
  36.7 5.4 %fusion.4 = f32[16,32,16,256]{3,2,1,0:T(8,128)} fusion(bf16[16,4,16,128]{3,2,1,0:T(8,128)(2,1)} %collective-permute-done.1, bf16[16,32,16,128]{3,2,1,0:T(8,128)(2,1)S(1)} %copy-done.4, bf16[3,3,256,256]{3,2,1,0:T(8,128)(2,1)S(1)} %copy-done, s32[]{:T(128)S(6)} %add.73, s32[]{:T(128)S(6)} %select_n.8), kind=kOutput, calls=%fused_computation.17 | convolution fusion | flops 541589504 | bytes 10813448 | tf_op jit(solution)/shard_map/bhwo,io->bhwi/dot_general | solution.py:31
  42.1 4.5 %fusion.8 = f32[16,32,16,256]{3,2,1,0:T(8,128)} fusion(bf16[16,32,16,128]{3,2,1,0:T(8,128)(2,1)S(1)} %copy-done.4, bf16[16,4,16,128]{3,2,1,0:T(8,128)(2,1)S(1)} %collective-permute-done, bf16[3,3,256,256]{3,2,1,0:T(8,128)(2,1)S(1)} %copy-done, s32[]{:T(128)S(6)} %add.74, s32[]{:T(128)S(6)} %add.73, s32[]{:T(128)S(6)} %select_n.8), kind=kOutput, calls=%fused_computation.21 | convolution fusion | flops 541589504 | bytes 10813452 | tf_op jit(solution)/shard_map/bhwo,io->bhwi/dot_general | solution.py:31
  46.6 0.0 collective-permute-done.3
  46.6 5.6 %fusion.21 = f32[16,32,16,256]{3,2,1,0:T(8,128)} fusion(bf16[16,40,16,128]{3,2,1,0:T(8,128)(2,1)S(1)} %copy-done.3, bf16[16,40,4,128]{3,2,1,0:T(4,128)(2,1)} %collective-permute-done.3, bf16[3,3,256,256]{3,2,1,0:T(8,128)(2,1)S(1)} %copy-done, s32[]{:T(128)S(6)} %add.73, s32[]{:T(128)S(6)} %add.74, s32[]{:T(128)S(6)} %select_n.8), kind=kOutput, calls=%fused_computation.34 | convolution fusion | flops 541065216 | bytes 11730956 | tf_op jit(solution)/shard_map/bhwo,io->bhwi/dot_general | solution.py:31
  52.2 5.6 %fusion.24 = f32[16,32,16,256]{3,2,1,0:T(8,128)} fusion(bf16[16,40,16,128]{3,2,1,0:T(8,128)(2,1)S(1)} %copy-done.3, bf16[16,40,4,128]{3,2,1,0:T(4,128)(2,1)} %collective-permute-done.3, bf16[3,3,256,256]{3,2,1,0:T(8,128)(2,1)S(1)} %copy-done, s32[]{:T(128)S(6)} %add.74, s32[]{:T(128)S(6)} %select_n.8), kind=kOutput, calls=%fused_computation.36 | convolution fusion | flops 541065216 | bytes 11730952 | tf_op jit(solution)/shard_map/bhwo,io->bhwi/dot_general | solution.py:31
  57.7 0.0 collective-permute-done.2
  57.8 4.5 %fusion.27 = f32[16,32,16,256]{3,2,1,0:T(8,128)} fusion(bf16[16,40,16,128]{3,2,1,0:T(8,128)(2,1)S(1)} %copy-done.3, bf16[16,40,4,128]{3,2,1,0:T(4,128)(2,1)S(1)} %collective-permute-done.2, bf16[3,3,256,256]{3,2,1,0:T(8,128)(2,1)S(1)} %copy-done, s32[]{:T(128)S(6)} %add.73, s32[]{:T(128)S(6)} %select_n.8), kind=kOutput, calls=%fused_computation.38 | convolution fusion | flops 541065216 | bytes 11730952 | tf_op jit(solution)/shard_map/bhwo,io->bhwi/dot_general | solution.py:31
  62.2 4.5 %fusion.48 = f32[16,32,16,256]{3,2,1,0:T(8,128)} fusion(bf16[16,40,4,128]{3,2,1,0:T(4,128)(2,1)S(1)} %collective-permute-done.2, bf16[16,40,16,128]{3,2,1,0:T(8,128)(2,1)S(1)} %copy-done.3, bf16[3,3,256,256]{3,2,1,0:T(8,128)(2,1)S(1)} %copy-done, s32[]{:T(128)S(6)} %add.74, s32[]{:T(128)S(6)} %select_n.8), kind=kOutput, calls=%fused_computation.57 | convolution fusion | flops 541065216 | bytes 11730952 | tf_op jit(solution)/shard_map/bhwo,io->bhwi/dot_general | solution.py:31
  66.8 4.5 %fusion.30 = f32[16,32,16,256]{3,2,1,0:T(8,128)} fusion(bf16[16,40,16,128]{3,2,1,0:T(8,128)(2,1)S(1)} %copy-done.3, bf16[16,40,4,128]{3,2,1,0:T(4,128)(2,1)S(1)} %collective-permute-done.2, bf16[3,3,256,256]{3,2,1,0:T(8,128)(2,1)S(1)} %copy-done, s32[]{:T(128)S(6)} %select_n.8), kind=kOutput, calls=%fused_computation.40 | convolution fusion | flops 541065216 | bytes 11730948 | tf_op jit(solution)/shard_map/bhwo,io->bhwi/dot_general | solution.py:31
  71.3 26.0 %fusion.3 = f32[16,32,16,256]{3,2,1,0:T(8,128)} fusion(f32[16,32,16,256]{3,2,1,0:T(8,128)} %fusion.8, f32[16,32,16,256]{3,2,1,0:T(8,128)} %fusion.48, f32[16,32,16,256]{3,2,1,0:T(8,128)} %fusion.21, f32[256,16,32,16]{0,3,2,1:T(8,128)} %fusion.51, f32[16,32,16,256]{3,2,1,0:T(8,128)} %fusion.27, f32[16,32,16,256]{3,2,1,0:T(8,128)} %fusion.24, ...), kind=kOutput, calls=%fused_computation.4 | convolution fusion | flops 557842432 | bytes 78839816 | tf_op jit(solution)/shard_map/bhwo,io->bhwi/dot_general | solution.py:31
  97.2 0.0 reduce-scatter.3.cloned.1.call-update
  97.2 0.0 reduce-scatter.5.cloned.1.call-start
  97.3 102.6 %reduce-scatter.3.cloned.1.call-done = f32[16,32,16,128]{3,2,1,0:T(8,128)} async-done(((f32[16,32,16,256]{3,2,1,0:T(8,128)}), f32[16,32,16,128]{3,2,1,0:T(8,128)}) %reduce-scatter.3.cloned.1.call-update) | async-done | bytes 4194320 | tf_op jit(solution)/shard_map/reduce_scatter | solution.py:45
  199.9 2.8 select_convert_fusion
  202.7 2.8 collective-permute-start.5
  205.5 2.8 collective-permute-start.4
  208.3 5.3 %fusion.50 = f32[16,32,16,256]{3,2,1,0:T(8,128)} fusion(bf16[16,32,16,128]{3,2,1,0:T(8,128)(2,1)S(1)} %select_convert_fusion, bf16[3,3,256,256]{3,2,1,0:T(8,128)(2,1)} %param.6, s32[]{:T(128)S(6)} %add.73, s32[]{:T(128)S(6)} %select_n.8), kind=kOutput, calls=%fused_computation.67 | convolution fusion | flops 536870912 | bytes 10551304 | tf_op jit(solution)/shard_map/bhwo,io->bhwi/dot_general | solution.py:31
  213.7 0.0 collective-permute-done.4
  213.7 0.5 pad_maximum_fusion.7
  214.1 4.5 %collective-permute-start.6 = (bf16[16,36,2,128]{3,2,1,0:T(2,128)(2,1)S(1)}, bf16[16,36,2,128]{3,2,1,0:T(2,128)(2,1)S(1)}, u32[]{:S(2)}, u32[]{:S(2)}) collective-permute-start(bf16[16,36,2,128]{3,2,1,0:T(2,128)(2,1)S(1)} %get-tuple-element.10), channel_id=1, source_target_pairs={{2,0},{4,2},{6,4},{8,6},{10,8},{12,10},{14,12},{16,14},{18,16},{20... | collective-permute-start | bytes 884744 | tf_op jit(solution)/shard_map/ppermute | solution.py:17
  218.7 1.9 collective-permute-start.7
  220.6 5.3 %fusion.12 = f32[16,32,16,256]{3,2,1,0:T(8,128)} fusion(bf16[16,2,16,128]{3,2,1,0:T(8,128)(2,1)S(1)} %collective-permute-done.5, bf16[16,32,16,128]{3,2,1,0:T(8,128)(2,1)S(1)} %select_convert_fusion, bf16[3,3,256,256]{3,2,1,0:T(8,128)(2,1)} %param.6, s32[]{:T(128)S(6)} %add.73, s32[]{:T(128)S(6)} %select_n.8), kind=kOutput, calls=%fused_computation.25 | convolution fusion | flops 541327360 | bytes 10682376 | tf_op jit(solution)/shard_map/bhwo,io->bhwi/dot_general | solution.py:31
  225.9 5.3 %fusion.16 = f32[16,32,16,256]{3,2,1,0:T(8,128)} fusion(bf16[16,32,16,128]{3,2,1,0:T(8,128)(2,1)S(1)} %select_convert_fusion, bf16[16,2,16,128]{3,2,1,0:T(8,128)(2,1)S(1)} %collective-permute-done.4, bf16[3,3,256,256]{3,2,1,0:T(8,128)(2,1)} %param.6, s32[]{:T(128)S(6)} %add.74, s32[]{:T(128)S(6)} %add.73, s32[]{:T(128)S(6)} %select_n.8), kind=kOutput, calls=%fused_computation.29 | convolution fusion | flops 541327360 | bytes 10682380 | tf_op jit(solution)/shard_map/bhwo,io->bhwi/dot_general | solution.py:31
  231.2 0.1 collective-permute-done.7
  231.4 2.3 maximum_maximum_fusion
  233.7 5.4 %fusion.38 = f32[16,32,16,256]{3,2,1,0:T(8,128)} fusion(bf16[16,36,18,128]{3,2,1,0:T(8,128)(2,1)S(1)} %get-tuple-element.7, bf16[3,3,256,256]{3,2,1,0:T(8,128)(2,1)} %param.6, s32[]{:T(128)S(6)} %add.73, s32[]{:T(128)S(6)} %add.74, s32[]{:T(128)S(6)} %select_n.8), kind=kOutput, calls=%fused_computation.45 | convolution fusion | flops 536870912 | bytes 10551308 | tf_op jit(solution)/shard_map/bhwo,io->bhwi/dot_general | solution.py:31
  239.1 5.3 %fusion.42 = f32[16,32,16,256]{3,2,1,0:T(8,128)} fusion(bf16[16,36,18,128]{3,2,1,0:T(8,128)(2,1)S(1)} %get-tuple-element.7, bf16[3,3,256,256]{3,2,1,0:T(8,128)(2,1)} %param.6, s32[]{:T(128)S(6)} %add.74, s32[]{:T(128)S(6)} %select_n.8), kind=kOutput, calls=%fused_computation.49 | convolution fusion | flops 536870912 | bytes 10551304 | tf_op jit(solution)/shard_map/bhwo,io->bhwi/dot_general | solution.py:31
  244.4 5.3 %fusion.40 = f32[16,32,16,256]{3,2,1,0:T(8,128)} fusion(bf16[16,36,18,128]{3,2,1,0:T(8,128)(2,1)S(1)} %get-tuple-element.8, bf16[3,3,256,256]{3,2,1,0:T(8,128)(2,1)} %param.6, s32[]{:T(128)S(6)} %add.73, s32[]{:T(128)S(6)} %select_n.8), kind=kOutput, calls=%fused_computation.47 | convolution fusion | flops 536870912 | bytes 10551304 | tf_op jit(solution)/shard_map/bhwo,io->bhwi/dot_general | solution.py:31
  249.8 5.3 %fusion.44 = f32[16,32,16,256]{3,2,1,0:T(8,128)} fusion(bf16[16,36,18,128]{3,2,1,0:T(8,128)(2,1)S(1)} %get-tuple-element.8, bf16[3,3,256,256]{3,2,1,0:T(8,128)(2,1)} %param.6, s32[]{:T(128)S(6)} %select_n.8), kind=kOutput, calls=%fused_computation.51 | convolution fusion | flops 536870912 | bytes 10551300 | tf_op jit(solution)/shard_map/bhwo,io->bhwi/dot_general | solution.py:31
  255.1 5.3 %fusion.36 = f32[16,32,16,256]{3,2,1,0:T(8,128)} fusion(bf16[16,36,18,128]{3,2,1,0:T(8,128)(2,1)S(1)} %get-tuple-element.8, bf16[3,3,256,256]{3,2,1,0:T(8,128)(2,1)} %param.6, s32[]{:T(128)S(6)} %add.74, s32[]{:T(128)S(6)} %select_n.8), kind=kOutput, calls=%fused_computation.43 | convolution fusion | flops 536870912 | bytes 10551304 | tf_op jit(solution)/shard_map/bhwo,io->bhwi/dot_general | solution.py:31
  260.4 25.7 %add_add_fusion = f32[16,32,16,256]{3,2,1,0:T(8,128)} fusion(f32[16,32,16,256]{3,2,1,0:T(8,128)} %fusion.16, f32[16,32,16,256]{3,2,1,0:T(8,128)} %fusion.36, f32[16,32,16,256]{3,2,1,0:T(8,128)} %fusion.38, f32[16,32,16,256]{3,2,1,0:T(8,128)} %fusion.50, f32[16,32,16,256]{3,2,1,0:T(8,128)} %fusion.40, f32[16,32,16,256]{3,2,1,0:T(8,128)} %fusion.42, ...), kind=kOutput, calls=%fused_computation.5 | convolution fusion | flops 553648128 | bytes 77660168 | tf_op jit(solution)/shard_map/bhwo,io->bhwi/dot_general | solution.py:31
  286.2 0.0 reduce-scatter.5.cloned.1.call-update
  286.2 0.0 copy-start.1
  286.2 103.1 %reduce-scatter.5.cloned.1.call-done = f32[16,32,16,128]{3,2,1,0:T(8,128)} async-done(((f32[16,32,16,256]{3,2,1,0:T(8,128)}), f32[16,32,16,128]{3,2,1,0:T(8,128)}) %reduce-scatter.5.cloned.1.call-update) | async-done | bytes 4194320 | tf_op jit(solution)/shard_map/reduce_scatter | solution.py:51
  389.3 3.8 convert_element_type.7
  (16 shorter events, 0.1 us)
Async XLA Ops:
  6.5 21.2 %copy-start = (bf16[3,3,256,256]{3,2,1,0:T(8,128)(2,1)S(1)}, bf16[3,3,256,256]{3,2,1,0:T(8,128)(2,1)}, u32[]{:S(2)}) copy-start(bf16[3,3,256,256]{3,2,1,0:T(8,128)(2,1)} %param.7) | copy-start | bytes 3538948
  6.5 193.4 %reduce-scatter.3.cloned.1.call-start = ((), (), s32[]{:S(2)}) async-start(), calls=%async_computation.2 | async-start | bytes 12582912 | tf_op jit(solution)/shard_map/reduce_scatter | solution.py:45
  8.4 7.4 %collective-permute-start = (bf16[16,4,16,128]{3,2,1,0:T(8,128)(2,1)S(1)}, bf16[16,4,16,128]{3,2,1,0:T(8,128)(2,1)S(1)}, u32[]{:S(2)}, u32[]{:S(2)}) collective-permute-start(bf16[16,4,16,128]{3,2,1,0:T(8,128)(2,1)S(1)} %get-tuple-element.14), channel_id=1, source_target_pairs={{0,32},{32,64},{64,96},{1,33},{33,65},{65,97},{2,34},{34,66},{66,9... | collective-permute-start | bytes 786440 | tf_op jit(solution)/shard_map/ppermute | solution.py:15
  12.5 8.0 %collective-permute-start.1 = (bf16[16,4,16,128]{3,2,1,0:T(8,128)(2,1)}, bf16[16,4,16,128]{3,2,1,0:T(8,128)(2,1)}, u32[]{:S(2)}, u32[]{:S(2)}) collective-permute-start(bf16[16,4,16,128]{3,2,1,0:T(8,128)(2,1)} %get-tuple-element.13), channel_id=1, source_target_pairs={{32,0},{64,32},{96,64},{33,1},{65,33},{97,65},{34,2},{66,34},{98,6... | collective-permute-start | bytes 786440 | tf_op jit(solution)/shard_map/ppermute | solution.py:17
  15.8 11.9 %copy-start.4 = (bf16[16,32,16,128]{3,2,1,0:T(8,128)(2,1)S(1)}, bf16[16,32,16,128]{3,2,1,0:T(8,128)(2,1)}, u32[]{:S(2)}) copy-start(bf16[16,32,16,128]{3,2,1,0:T(8,128)(2,1)} %param.4) | copy-start | bytes 6291460
  21.5 1.5 copy-start.2
  24.6 22.0 %collective-permute-start.3 = (bf16[16,40,4,128]{3,2,1,0:T(4,128)(2,1)}, bf16[16,40,4,128]{3,2,1,0:T(4,128)(2,1)}, u32[]{:S(2)}, u32[]{:S(2)}) collective-permute-start(bf16[16,40,4,128]{3,2,1,0:T(4,128)(2,1)} %get-tuple-element.5), channel_id=1, source_target_pairs={{0,2},{2,4},{4,6},{6,8},{8,10},{10,12},{12,14},{14,16},{16,18},{18... | collective-permute-start | bytes 1966088 | tf_op jit(solution)/shard_map/ppermute | solution.py:15
  32.2 25.5 %collective-permute-start.2 = (bf16[16,40,4,128]{3,2,1,0:T(4,128)(2,1)}, bf16[16,40,4,128]{3,2,1,0:T(4,128)(2,1)S(1)}, u32[]{:S(2)}, u32[]{:S(2)}) collective-permute-start(bf16[16,40,4,128]{3,2,1,0:T(4,128)(2,1)} %get-tuple-element.6), channel_id=1, source_target_pairs={{2,0},{4,2},{6,4},{8,6},{10,8},{12,10},{14,12},{16,14},{18,16},{20... | collective-permute-start | bytes 1966088 | tf_op jit(solution)/shard_map/ppermute | solution.py:17
  42.1 4.5 %copy-start.3 = (bf16[16,40,16,128]{3,2,1,0:T(8,128)(2,1)S(1)}, bf16[16,40,16,128]{3,2,1,0:T(8,128)(2,1)}, u32[]{:S(2)}) copy-start(bf16[16,40,16,128]{3,2,1,0:T(8,128)(2,1)} %copy-done.2) | copy-start | bytes 7864324
  97.2 102.7 %copy-start.6 = (bf16[16,32,16,128]{3,2,1,0:T(8,128)(2,1)S(1)}, bf16[16,32,16,128]{3,2,1,0:T(8,128)(2,1)}, u32[]{:S(2)}) copy-start(bf16[16,32,16,128]{3,2,1,0:T(8,128)(2,1)} %param.5) | copy-start | bytes 6291460
  97.2 292.0 %reduce-scatter.5.cloned.1.call-start = ((), (), s32[]{:S(2)}) async-start(), calls=%async_computation.3 | async-start | bytes 12582912 | tf_op jit(solution)/shard_map/reduce_scatter | solution.py:51
  202.7 10.9 %collective-permute-start.5 = (bf16[16,2,16,128]{3,2,1,0:T(8,128)(2,1)S(1)}, bf16[16,2,16,128]{3,2,1,0:T(8,128)(2,1)S(1)}, u32[]{:S(2)}, u32[]{:S(2)}) collective-permute-start(bf16[16,2,16,128]{3,2,1,0:T(8,128)(2,1)S(1)} %get-tuple-element.11), channel_id=1, source_target_pairs={{32,0},{64,32},{96,64},{33,1},{65,33},{97,65},{34,2},{66,34},{98,6... | collective-permute-start | bytes 393224 | tf_op jit(solution)/shard_map/ppermute | solution.py:17
  205.5 8.2 %collective-permute-start.4 = (bf16[16,2,16,128]{3,2,1,0:T(8,128)(2,1)S(1)}, bf16[16,2,16,128]{3,2,1,0:T(8,128)(2,1)S(1)}, u32[]{:S(2)}, u32[]{:S(2)}) collective-permute-start(bf16[16,2,16,128]{3,2,1,0:T(8,128)(2,1)S(1)} %get-tuple-element.12), channel_id=1, source_target_pairs={{0,32},{32,64},{64,96},{1,33},{33,65},{65,97},{2,34},{34,66},{66,9... | collective-permute-start | bytes 393224 | tf_op jit(solution)/shard_map/ppermute | solution.py:15
  214.1 17.1 %collective-permute-start.6 = (bf16[16,36,2,128]{3,2,1,0:T(2,128)(2,1)S(1)}, bf16[16,36,2,128]{3,2,1,0:T(2,128)(2,1)S(1)}, u32[]{:S(2)}, u32[]{:S(2)}) collective-permute-start(bf16[16,36,2,128]{3,2,1,0:T(2,128)(2,1)S(1)} %get-tuple-element.10), channel_id=1, source_target_pairs={{2,0},{4,2},{6,4},{8,6},{10,8},{12,10},{14,12},{16,14},{18,16},{20... | collective-permute-start | bytes 884744 | tf_op jit(solution)/shard_map/ppermute | solution.py:17
  218.7 12.7 %collective-permute-start.7 = (bf16[16,36,2,128]{3,2,1,0:T(2,128)(2,1)S(1)}, bf16[16,36,2,128]{3,2,1,0:T(2,128)(2,1)S(1)}, u32[]{:S(2)}, u32[]{:S(2)}) collective-permute-start(bf16[16,36,2,128]{3,2,1,0:T(2,128)(2,1)S(1)} %get-tuple-element.9), channel_id=1, source_target_pairs={{0,2},{2,4},{4,6},{6,8},{8,10},{10,12},{12,14},{14,16},{16,18},{18... | collective-permute-start | bytes 884744 | tf_op jit(solution)/shard_map/ppermute | solution.py:15
  233.7 5.4 %copy-start.5 = (bf16[16,36,18,128]{3,2,1,0:T(8,128)(2,1)}, bf16[16,36,18,128]{3,2,1,0:T(8,128)(2,1)S(1)}, u32[]{:S(2)}) copy-start(bf16[16,36,18,128]{3,2,1,0:T(8,128)(2,1)S(1)} %get-tuple-element.7) | copy-start | bytes 7962628
  286.2 106.9 %copy-start.1 = (bf16[3,3,256,256]{3,2,1,0:T(8,128)(2,1)S(1)}, bf16[3,3,256,256]{3,2,1,0:T(8,128)(2,1)}, u32[]{:S(2)}) copy-start(bf16[3,3,256,256]{3,2,1,0:T(8,128)(2,1)} %param.7) | copy-start | bytes 3538948
Sparse Core Ops, SparseCore 0:
  97.4 102.5 reduce-scatter.2
  286.3 102.9 reduce-scatter.4
where the time goes:
time: 402 us; the launch traced here: 400 us
  waiting for transfers between devices  210 us (52%)
  matrix products  133 us (33%)
  starting transfers between devices  25.6 us (6%)
  between operations  13.6 us (3%)
  other arithmetic  9.38 us (2%)
  local copies, waits for them, and re-layouts  8.31 us (2%)
    dot_general x18, matrix products, tap_sum(): jnp.einsum('bhwo,io->bhwi', piece, weight[tap_row, tap_col], preferred_el...  133 us
    reduce_scatter x1, waiting for transfers between devices, per_device(): lax.psum_scatter(tap_sum(inner, cols_one, 2, rows, cols), 'filt', scatter...  103 us
    reduce_scatter x1, waiting for transfers between devices, per_device(): lax.psum_scatter(tap_sum(outer, cols_two, 4, rows, cols), 'filt', scatter...  103 us
    ppermute x4, starting transfers between devices, padded_2(): lax.ppermute(head, axis, [((i + 1) % count, i) for i in range(ends)])  13.7 us
    ppermute x4, starting transfers between devices, padded_2(): lax.ppermute(tail, axis, [(i, (i + 1) % count) for i in range(ends)])  11.9 us
  transfers between devices with their start and end apart: 10, of which 5 were waited for; matrix products, arithmetic and copies ran while one was open for 11% of the time, Pallas kernels for 0%

commit v1 on v0

v1 whole, which is shorter than its diff:
```python
import jax
import jax.numpy as jnp
from jax import lax
from jax.experimental import pallas as pl
from jax.experimental.pallas import tpu as pltpu
from jax.sharding import PartitionSpec as P

CHUNKS = (4, 4)
FAR = 4
NEAR = 2
SPREAD = FAR + NEAR


def from_before(x, axis):
    count = lax.axis_size(axis)
    return lax.ppermute(x, axis, [(i, i + 1) for i in range(count - 1)])


def from_after(x, axis):
    count = lax.axis_size(axis)
    return lax.ppermute(x, axis, [(i + 1, i) for i in range(count - 1)])


def to_partner(x):
    return lax.ppermute(x, "filt", [(0, 1), (1, 0)])


def relative_weight(weight, part):
    taps = weight.shape[:2]
    channels = weight.shape[2]
    half = channels // 2
    swapped = jnp.roll(weight, (half, half), (2, 3))
    own_first = jnp.where(part == 0, weight, swapped)
    turned = own_first[:, ::-1].transpose(0, 1, 3, 2)
    return turned.reshape(taps[0], taps[1] * channels, channels)


def fill_shifted(shifted, middle, left, right, spacing):
    rows, cols, channels = middle.shape
    shifted[:, spacing:, :channels] = middle[:, : cols - spacing]
    shifted[:, :spacing, :channels] = left
    shifted[:, :, channels : 2 * channels] = middle
    shifted[:, : cols - spacing, 2 * channels :] = middle[:, spacing:]
    shifted[:, cols - spacing :, 2 * channels :] = right


def taps_sum(shifted, weight_ref, spacing, rows):
    cols, depth = shifted.shape[1:]
    total = None
    for tap_row in range(3):
        top = spacing * (2 - tap_row)
        piece = shifted[top : top + rows].reshape(rows * cols, depth)
        term = jnp.dot(piece, weight_ref[tap_row], preferred_element_type=jnp.float32)
        total = term if total is None else total + term
    return total


def first_kernel(part_ref, own, other, top, bottom, left, right, gate_own, gate_other, weight, grad_h, edge_left, edge_right, whole, shifted):
    rows = own.shape[1]
    half = own.shape[3]
    whole[:SPREAD] = top[0]
    whole[SPREAD : SPREAD + rows, :, :half] = own[0]
    whole[SPREAD : SPREAD + rows, :, half:] = other[0]
    whole[SPREAD + rows :] = bottom[0]
    fill_shifted(shifted, whole[...], left[0], right[0], FAR)
    out_rows = rows + 2 * NEAR
    total = taps_sum(shifted, weight, FAR, out_rows).reshape(out_rows, own.shape[2], 2 * half)
    kept_own = jnp.where(gate_own[0].astype(jnp.float32) > 0, total[:, :, :half], 0.0).astype(jnp.bfloat16)
    kept_other = jnp.where(gate_other[0].astype(jnp.float32) > 0, total[:, :, half:], 0.0).astype(jnp.bfloat16)
    grad_h[0, :, :, :half] = kept_own
    grad_h[0, :, :, half:] = kept_other
    cols = own.shape[2]
    edge_left[0] = grad_h[0, :, :NEAR]
    edge_right[0] = grad_h[0, :, cols - NEAR :]


def second_kernel(grad_h, left, right, weight, kept, sent, shifted):
    fill_shifted(shifted, grad_h[0], left[0], right[0], NEAR)
    rows, cols, half = kept.shape[1:]
    total = taps_sum(shifted, weight, NEAR, rows).reshape(rows, cols, 2 * half).astype(jnp.bfloat16)
    kept[0] = total[:, :, :half]
    sent[0] = total[:, :, half:]


def per_device(grad_out, pre_act, weight_one, weight_two):
    batch, rows, cols, half = grad_out.shape
    mine = batch // 2
    part = lax.axis_index("filt")
    own_at = part * mine
    other_at = (1 - part) * mine
    channels = 2 * half

    other = to_partner(lax.dynamic_slice_in_dim(grad_out, other_at, mine, 0))
    own = lax.dynamic_slice_in_dim(grad_out, own_at, mine, 0)
    gate_top = from_before(pre_act[:, rows - NEAR :], "row")
    gate_bottom = from_after(pre_act[:, :NEAR], "row")
    gate = jnp.concatenate([gate_top, pre_act, gate_bottom], axis=1)
    gate_sent = lax.dynamic_slice_in_dim(gate, other_at, mine, 0)
    first_weight = relative_weight(weight_two, part)
    second_weight = relative_weight(weight_one, part)

    both = jnp.concatenate([own, other], axis=3)
    top = from_before(both[:, rows - SPREAD :], "row")
    bottom = from_after(both[:, :SPREAD], "row")
    tall = jnp.concatenate([top, both, bottom], axis=1)
    left = from_before(tall[:, :, cols - FAR :], "col")
    right = from_after(tall[:, :, :FAR], "col")

    tall_rows = rows + 2 * SPREAD
    gate_rows = rows + 2 * NEAR
    where = jnp.reshape(own_at, (1,)).astype(jnp.int32)
    result = jnp.zeros_like(grad_out)
    start = 0
    for size in CHUNKS:
        gate_other = to_partner(gate_sent[start : start + size])

        def by_own(i, ref, start=start):
            return (ref[0] + start + i, 0, 0, 0)

        def by_mine(i, ref, start=start):
            return (start + i, 0, 0, 0)

        def by_chunk(i, *refs):
            return (i, 0, 0, 0)

        def whole_weight(i, *refs):
            return (0, 0, 0)

        grad_h, edge_left, edge_right = pl.pallas_call(
            first_kernel,
            out_shape=(
                jax.ShapeDtypeStruct((size, gate_rows, cols, channels), jnp.bfloat16),
                jax.ShapeDtypeStruct((size, gate_rows, NEAR, channels), jnp.bfloat16),
                jax.ShapeDtypeStruct((size, gate_rows, NEAR, channels), jnp.bfloat16),
            ),
            grid_spec=pltpu.PrefetchScalarGridSpec(
                num_scalar_prefetch=1,
                grid=(size,),
                in_specs=[
                    pl.BlockSpec((1, rows, cols, half), by_own),
                    pl.BlockSpec((1, rows, cols, half), by_mine),
                    pl.BlockSpec((1, SPREAD, cols, channels), by_mine),
                    pl.BlockSpec((1, SPREAD, cols, channels), by_mine),
                    pl.BlockSpec((1, tall_rows, FAR, channels), by_mine),
                    pl.BlockSpec((1, tall_rows, FAR, channels), by_mine),
                    pl.BlockSpec((1, gate_rows, cols, half), by_own),
                    pl.BlockSpec((1, gate_rows, cols, half), by_chunk),
                    pl.BlockSpec((3, 3 * channels, channels), whole_weight),
                ],
                out_specs=(
                    pl.BlockSpec((1, gate_rows, cols, channels), by_chunk),
                    pl.BlockSpec((1, gate_rows, NEAR, channels), by_chunk),
                    pl.BlockSpec((1, gate_rows, NEAR, channels), by_chunk),
                ),
                scratch_shapes=[
                    pltpu.VMEM((tall_rows, cols, channels), jnp.bfloat16),
                    pltpu.VMEM((tall_rows, cols, 3 * channels), jnp.bfloat16),
                ],
            ),
            cost_estimate=pl.CostEstimate(flops=size * 2 * gate_rows * cols * 9 * channels * channels, bytes_accessed=size * 2**20, transcendentals=0),
            name="first",
        )(where, grad_out, other, top, bottom, left, right, gate, gate_other, first_weight)
        h_left = from_before(edge_right, "col")
        h_right = from_after(edge_left, "col")
        kept, sent = pl.pallas_call(
            second_kernel,
            out_shape=(
                jax.ShapeDtypeStruct((size, rows, cols, half), jnp.bfloat16),
                jax.ShapeDtypeStruct((size, rows, cols, half), jnp.bfloat16),
            ),
            grid=(size,),
            in_specs=[
                pl.BlockSpec((1, gate_rows, cols, channels), by_chunk),
                pl.BlockSpec((1, gate_rows, NEAR, channels), by_chunk),
                pl.BlockSpec((1, gate_rows, NEAR, channels), by_chunk),
                pl.BlockSpec((3, 3 * channels, channels), whole_weight),
            ],
            out_specs=(
                pl.BlockSpec((1, rows, cols, half), by_chunk),
                pl.BlockSpec((1, rows, cols, half), by_chunk),
            ),
            scratch_shapes=[pltpu.VMEM((gate_rows, cols, 3 * channels), jnp.bfloat16)],
            cost_estimate=pl.CostEstimate(flops=size * 2 * rows * cols * 9 * channels * channels, bytes_accessed=size * 2**20, transcendentals=0),
            name="second",
        )(grad_h, h_left, h_right, second_weight)
        back = to_partner(sent)
        result = lax.dynamic_update_slice_in_dim(result, kept, own_at + start, 0)
        result = lax.dynamic_update_slice_in_dim(result, back, other_at + start, 0)
        start += size
    return result


def solution(mesh):
    placed = (P(None, "row", "col", "filt"), P(None, "row", "col", "filt"), P(), P())
    return jax.shard_map(
        per_device,
        mesh=mesh,
        in_specs=placed,
        out_specs=P(None, "row", "col", "filt"),
        check_vma=False,
    )
```

time: 402 us -> 140 us (0.35)
  waiting for transfers between devices: 210 us -> 52.4 us
  matrix products: 133 us -> 0 us
  Pallas kernels: 0 us -> 24.9 us
  starting transfers between devices: 25.6 us -> 43.9 us
  between operations: 13.6 us -> 0.33 us
  other arithmetic: 9.38 us -> 2.58 us
  local copies, waits for them, and re-layouts: 8.31 us -> 14.6 us
    reduce_scatter x2 -> x0, waiting for transfers between devices: 206 us -> none  [the longest x1 103 us: per_device(): lax.psum_scatter(tap_sum(inner, cols_one, 2, rows, cols), 'filt', scatter...]
    dot_general x18 -> x0, matrix products: 133 us -> none  [tap_sum(): jnp.einsum('bhwo,io->bhwi', piece, weight[tap_row, tap_col], preferred_el...]
    ppermute x8 -> x15, waiting for transfers between devices: 3.85 us -> 52.4 us  [the longest x5 45.8 us: to_partner(): return lax.ppermute(x, 'filt', [(0, 1), (1, 0)])]
    pallas_call x0 -> x4, Pallas kernels: none -> 24.9 us  [the longest x2 13.7 us: per_device(): pl.pallas_call(first_kernel, out_shape=(jax.ShapeDtypeStruct((size, gate_...]
    ppermute x8 -> x15, starting transfers between devices: 25.6 us -> 43.9 us  [the longest x5 19.1 us: from_after(): return lax.ppermute(x, axis, [(i + 1, i) for i in range(count - 1)])]
    convert_element_type x2 -> x0, other arithmetic: 6.62 us -> none  [the longest x1 3.84 us: per_device(): return grad_in.astype(jnp.bfloat16)]
  transfers between devices with their start and end apart: 10 -> 15, of which waited for: 5 -> 6; matrix products, arithmetic and copies ran while one was open for 11% -> 6% of each run, Pallas kernels for 0% -> 18%
where the time goes in v1:
time: 140 us; the launch traced here: 139 us
  waiting for transfers between devices  52.4 us (37%)
  starting transfers between devices  43.9 us (31%)
  Pallas kernels  24.9 us (18%)
  local copies, waits for them, and re-layouts  14.6 us (10%)
  other arithmetic  2.58 us (2%)
    ppermute x5, waiting for transfers between devices, to_partner(): return lax.ppermute(x, 'filt', [(0, 1), (1, 0)])  45.8 us
    ppermute x5, starting transfers between devices, from_after(): return lax.ppermute(x, axis, [(i + 1, i) for i in range(count - 1)])  19.1 us
    ppermute x5, starting transfers between devices, from_before(): return lax.ppermute(x, axis, [(i, i + 1) for i in range(count - 1)])  14.7 us
    pallas_call x2, Pallas kernels, per_device(): pl.pallas_call(first_kernel, out_shape=(jax.ShapeDtypeStruct((size, gate_...  13.7 us
    pallas_call x2, Pallas kernels, per_device(): pl.pallas_call(second_kernel, out_shape=(jax.ShapeDtypeStruct((size, rows...  11.3 us
    ppermute x5, starting transfers between devices, to_partner(): return lax.ppermute(x, 'filt', [(0, 1), (1, 0)])  10.2 us
    ppermute x5, waiting for transfers between devices, from_after(): return lax.ppermute(x, axis, [(i + 1, i) for i in range(count - 1)])  4.4 us
    unnamed x30, local copies, waits for them, and re-layouts  3.72 us
  transfers between devices with their start and end apart: 15, of which 6 were waited for; matrix products, arithmetic and copies ran while one was open for 6% of the time, Pallas kernels for 18%

profile of v1, /device:TPU:9, one launch (start us, length us, event | category | flops | bytes accessed | tf_op | source)
XLA Modules:
  0.0 138.8 jit_solution(13492186282896243338)
XLA Ops:
  0.0 3.0 %constant_dynamic-slice_fusion.2 = (bf16[8,32,16,128]{3,2,1,0:T(8,128)(2,1)S(1)}, bf16[8,32,16,128]{3,2,1,0:T(8,128)(2,1)}) fusion(bf16[16,32,16,128]{3,2,1,0:T(8,128)(2,1)} %own.3, s32[]{:T(128)S(6)} %select_n.28, s32[]{:T(128)S(6)} %select_n.27), kind=kLoop, calls=%fused_computation.29 | loop fusion | bytes 4194312 | tf_op jit(solution)/shard_map/dynamic_slice | solution.py:94
  3.0 3.6 %collective-permute-start = (bf16[8,32,16,128]{3,2,1,0:T(8,128)(2,1)}, bf16[8,32,16,128]{3,2,1,0:T(8,128)(2,1)S(1)}, u32[]{:S(2)}, u32[]{:S(2)}) collective-permute-start(bf16[8,32,16,128]{3,2,1,0:T(8,128)(2,1)} %get-tuple-element.34), channel_id=1, source_target_pairs={{0,1},{1,0},{2,3},{3,2},{4,5},{5,4},{6,7},{7,6},{8,9},{9,8},{10,11... | collective-permute-start | bytes 3145736 | tf_op jit(solution)/shard_map/ppermute | solution.py:25
  6.6 1.7 %fusion.6 = (bf16[16,2,16,128]{3,2,1,0:T(8,128)(2,1)}, bf16[16,2,16,128]{3,2,1,0:T(8,128)(2,1)}) fusion(bf16[16,32,16,128]{3,2,1,0:T(8,128)(2,1)} %param.5), kind=kLoop, calls=%fused_computation.31 | loop fusion | bytes 524288 | tf_op jit(solution)/shard_map/slice | solution.py:96
  8.3 3.5 %collective-permute-start.5 = (bf16[16,2,16,128]{3,2,1,0:T(8,128)(2,1)}, bf16[16,2,16,128]{3,2,1,0:T(8,128)(2,1)S(1)}, u32[]{:S(2)}, u32[]{:S(2)}) collective-permute-start(bf16[16,2,16,128]{3,2,1,0:T(8,128)(2,1)} %get-tuple-element.30), channel_id=1, source_target_pairs={{0,32},{32,64},{64,96},{1,33},{33,65},{65,97},{2,34},{34,66},{66,9... | collective-permute-start | bytes 393224 | tf_op jit(solution)/shard_map/ppermute | solution.py:16
  11.8 1.9 %collective-permute-start.6 = (bf16[16,2,16,128]{3,2,1,0:T(8,128)(2,1)}, bf16[16,2,16,128]{3,2,1,0:T(8,128)(2,1)S(1)}, u32[]{:S(2)}, u32[]{:S(2)}) collective-permute-start(bf16[16,2,16,128]{3,2,1,0:T(8,128)(2,1)} %get-tuple-element.29), channel_id=1, source_target_pairs={{32,0},{64,32},{96,64},{33,1},{65,33},{97,65},{34,2},{66,34},{98,6... | collective-permute-start | bytes 393224 | tf_op jit(solution)/shard_map/ppermute | solution.py:21
  13.8 0.1 fusion.7
  13.9 0.1 fusion.4
  14.0 1.1 copy-done.1
  15.1 0.1 fusion.8
  15.2 0.1 fusion.5
  15.3 14.4 %collective-permute-done.other = bf16[8,32,16,128]{3,2,1,0:T(8,128)(2,1)S(1)} collective-permute-done((bf16[8,32,16,128]{3,2,1,0:T(8,128)(2,1)}, bf16[8,32,16,128]{3,2,1,0:T(8,128)(2,1)S(1)}, u32[]{:S(2)}, u32[]{:S(2)}) %collective-permute-start) | collective-permute-done | bytes 1048608 | tf_op jit(solution)/shard_map/ppermute | solution.py:25
  29.7 0.1 pad_maximum_fusion.6
  29.8 4.3 %collective-permute-start.1 = (bf16[8,6,16,256]{3,2,1,0:T(8,128)(2,1)S(1)}, bf16[8,6,16,256]{3,2,1,0:T(8,128)(2,1)S(1)}, u32[]{:S(2)}, u32[]{:S(2)}) collective-permute-start(bf16[8,6,16,256]{3,2,1,0:T(8,128)(2,1)S(1)} %get-tuple-element.32), channel_id=1, source_target_pairs={{0,32},{32,64},{64,96},{1,33},{33,65},{65,97},{2,34},{34,66},{66,9... | collective-permute-start | bytes 1179656 | tf_op jit(solution)/shard_map/ppermute | solution.py:16
  34.1 1.9 %collective-permute-start.2 = (bf16[8,6,16,256]{3,2,1,0:T(8,128)(2,1)S(1)}, bf16[8,6,16,256]{3,2,1,0:T(8,128)(2,1)S(1)}, u32[]{:S(2)}, u32[]{:S(2)}) collective-permute-start(bf16[8,6,16,256]{3,2,1,0:T(8,128)(2,1)S(1)} %get-tuple-element.31), channel_id=1, source_target_pairs={{32,0},{64,32},{96,64},{33,1},{65,33},{97,65},{34,2},{66,34},{98,6... | collective-permute-start | bytes 1179656 | tf_op jit(solution)/shard_map/ppermute | solution.py:21
  36.1 0.5 constant_dynamic-update-slice_fusion.1
  36.6 2.2 %collective-permute-done.1.top = bf16[8,6,16,256]{3,2,1,0:T(8,128)(2,1)S(1)} collective-permute-done((bf16[8,6,16,256]{3,2,1,0:T(8,128)(2,1)S(1)}, bf16[8,6,16,256]{3,2,1,0:T(8,128)(2,1)S(1)}, u32[]{:S(2)}, u32[]{:S(2)}) %collective-permute-start.1) | collective-permute-done | bytes 393248 | tf_op jit(solution)/shard_map/ppermute | solution.py:16
  38.8 4.4 %collective-permute-done.2.bottom = bf16[8,6,16,256]{3,2,1,0:T(8,128)(2,1)S(1)} collective-permute-done((bf16[8,6,16,256]{3,2,1,0:T(8,128)(2,1)S(1)}, bf16[8,6,16,256]{3,2,1,0:T(8,128)(2,1)S(1)}, u32[]{:S(2)}, u32[]{:S(2)}) %collective-permute-start.2) | collective-permute-done | bytes 393248 | tf_op jit(solution)/shard_map/ppermute | solution.py:21
  43.2 1.7 %pad_maximum_fusion.2 = (bf16[8,44,4,256]{3,2,1,0:T(4,128)(2,1)}, bf16[8,44,4,256]{3,2,1,0:T(4,128)(2,1)}) fusion(bf16[8,6,16,256]{3,2,1,0:T(8,128)(2,1)S(1)} %collective-permute-done.2.bottom, bf16[8,6,16,256]{3,2,1,0:T(8,128)(2,1)S(1)} %collective-permute-done.1.top, bf16[8,32,16,128]{3,2,1,0:T(8,128)(2,1)S(1)} %collective-permute-done.other, ...), kind=kLoop, calls=%fused_computation.12 | loop fusion | flops 5767168 | bytes 4325376 | tf_op jit(solution)/shard_map/concatenate | solution.py:105
  44.9 3.1 %collective-permute-start.3 = (bf16[8,44,4,256]{3,2,1,0:T(4,128)(2,1)}, bf16[8,44,4,256]{3,2,1,0:T(4,128)(2,1)}, u32[]{:S(2)}, u32[]{:S(2)}) collective-permute-start(bf16[8,44,4,256]{3,2,1,0:T(4,128)(2,1)} %get-tuple-element.26), channel_id=1, source_target_pairs={{0,2},{2,4},{4,6},{6,8},{8,10},{10,12},{12,14},{14,16},{16,18},{18... | collective-permute-start | bytes 2162696 | tf_op jit(solution)/shard_map/ppermute | solution.py:16
  48.0 4.3 %collective-permute-start.4 = (bf16[8,44,4,256]{3,2,1,0:T(4,128)(2,1)}, bf16[8,44,4,256]{3,2,1,0:T(4,128)(2,1)}, u32[]{:S(2)}, u32[]{:S(2)}) collective-permute-start(bf16[8,44,4,256]{3,2,1,0:T(4,128)(2,1)} %get-tuple-element.25), channel_id=1, source_target_pairs={{2,0},{4,2},{6,4},{8,6},{10,8},{12,10},{14,12},{16,14},{18,16},{20... | collective-permute-start | bytes 2162696 | tf_op jit(solution)/shard_map/ppermute | solution.py:21
  52.3 1.3 constant_dynamic-slice_fusion.1
  53.6 3.3 %collective-permute-start.11 = (bf16[4,36,16,128]{3,2,1,0:T(8,128)(2,1)}, bf16[4,36,16,128]{3,2,1,0:T(8,128)(2,1)}, u32[]{:S(2)}, u32[]{:S(2)}) collective-permute-start(bf16[4,36,16,128]{3,2,1,0:T(8,128)(2,1)} %get-tuple-element.27), channel_id=1, source_target_pairs={{0,1},{1,0},{2,3},{3,2},{4,5},{5,4},{6,7},{7,6},{8,9},{9,8},{10,11... | collective-permute-start | bytes 1769480 | tf_op jit(solution)/shard_map/ppermute | solution.py:25
  56.9 0.6 fusion.1
  57.5 0.1 reverse_bitcast_fusion.1
  57.6 1.5 %copy.5 = bf16[3,3,256,256]{3,2,1,0:T(8,128)(2,1)} copy(bf16[3,3,256,256]{2,3,1,0:T(8,128)(2,1)S(1)} %reverse_bitcast_fusion.1) | data formatting | bytes 2359296 | tf_op jit(solution)/shard_map/transpose | solution.py:34
  59.1 0.1 reverse_bitcast_fusion
  59.2 1.5 %copy.6 = bf16[3,3,256,256]{3,2,1,0:T(8,128)(2,1)} copy(bf16[3,3,256,256]{2,3,1,0:T(8,128)(2,1)S(1)} %reverse_bitcast_fusion) | data formatting | bytes 2359296 | tf_op jit(solution)/shard_map/transpose | solution.py:34
  60.8 17.9 %collective-permute-done.7.gate_other = bf16[4,36,16,128]{3,2,1,0:T(8,128)(2,1)} collective-permute-done((bf16[4,36,16,128]{3,2,1,0:T(8,128)(2,1)}, bf16[4,36,16,128]{3,2,1,0:T(8,128)(2,1)}, u32[]{:S(2)}, u32[]{:S(2)}) %collective-permute-start.7) | collective-permute-done | bytes 589856 | tf_op jit(solution)/shard_map/ppermute | solution.py:25
  78.7 6.8 %first.2 = (bf16[4,36,16,256]{3,2,1,0:T(8,128)(2,1)}, bf16[4,36,2,256]{3,2,1,0:T(2,128)(2,1)}, bf16[4,36,2,256]{3,2,1,0:T(2,128)(2,1)}) custom-call(s32[1]{0:T(128)} %bitcast.part_ref, bf16[16,32,16,128]{3,2,1,0:T(8,128)(2,1)} %own.3, bf16[8,32,16,128]{3,2,1,0:T(8,128)(2,1)} %copy-done.2, bf16[8,6,16,256]{3,2,1,0:T(8,128)(2,1)} %copy-done.8, ...), custom_call_target="tpu_custom_call" | custom-call | flops 2717908992 | bytes 4194304 | tf_op jit(solution)/shard_map/first/pallas_call | solution.py:129
  85.5 1.9 %collective-permute-start.8 = (bf16[4,36,2,256]{3,2,1,0:T(2,128)(2,1)}, bf16[4,36,2,256]{3,2,1,0:T(2,128)(2,1)S(1)}, u32[]{:S(2)}, u32[]{:S(2)}) collective-permute-start(bf16[4,36,2,256]{3,2,1,0:T(2,128)(2,1)} %get-tuple-element.16), channel_id=1, source_target_pairs={{0,2},{2,4},{4,6},{6,8},{8,10},{10,12},{12,14},{14,16},{16,18},{18... | collective-permute-start | bytes 442376 | tf_op jit(solution)/shard_map/ppermute | solution.py:16
  87.4 5.5 %collective-permute-start.9 = (bf16[4,36,2,256]{3,2,1,0:T(2,128)(2,1)}, bf16[4,36,2,256]{3,2,1,0:T(2,128)(2,1)S(1)}, u32[]{:S(2)}, u32[]{:S(2)}) collective-permute-start(bf16[4,36,2,256]{3,2,1,0:T(2,128)(2,1)} %get-tuple-element.17), channel_id=1, source_target_pairs={{2,0},{4,2},{6,4},{8,6},{10,8},{12,10},{14,12},{16,14},{18,16},{20... | collective-permute-start | bytes 442376 | tf_op jit(solution)/shard_map/ppermute | solution.py:21
  92.9 6.9 %first.3 = (bf16[4,36,16,256]{3,2,1,0:T(8,128)(2,1)}, bf16[4,36,2,256]{3,2,1,0:T(2,128)(2,1)}, bf16[4,36,2,256]{3,2,1,0:T(2,128)(2,1)}) custom-call(s32[1]{0:T(128)} %bitcast.part_ref, bf16[16,32,16,128]{3,2,1,0:T(8,128)(2,1)} %own.3, bf16[8,32,16,128]{3,2,1,0:T(8,128)(2,1)} %copy-done.2, bf16[8,6,16,256]{3,2,1,0:T(8,128)(2,1)} %copy-done.8, ...), custom_call_target="tpu_custom_call" | custom-call | flops 2717908992 | bytes 4194304 | tf_op jit(solution)/shard_map/first/pallas_call | solution.py:129
  99.8 1.9 %collective-permute-start.12 = (bf16[4,36,2,256]{3,2,1,0:T(2,128)(2,1)}, bf16[4,36,2,256]{3,2,1,0:T(2,128)(2,1)S(1)}, u32[]{:S(2)}, u32[]{:S(2)}) collective-permute-start(bf16[4,36,2,256]{3,2,1,0:T(2,128)(2,1)} %get-tuple-element.21), channel_id=1, source_target_pairs={{0,2},{2,4},{4,6},{6,8},{8,10},{10,12},{12,14},{14,16},{16,18},{18... | collective-permute-start | bytes 442376 | tf_op jit(solution)/shard_map/ppermute | solution.py:16
  101.7 5.5 %collective-permute-start.13 = (bf16[4,36,2,256]{3,2,1,0:T(2,128)(2,1)}, bf16[4,36,2,256]{3,2,1,0:T(2,128)(2,1)S(1)}, u32[]{:S(2)}, u32[]{:S(2)}) collective-permute-start(bf16[4,36,2,256]{3,2,1,0:T(2,128)(2,1)} %get-tuple-element.22), channel_id=1, source_target_pairs={{2,0},{4,2},{6,4},{8,6},{10,8},{12,10},{14,12},{16,14},{18,16},{20... | collective-permute-start | bytes 442376 | tf_op jit(solution)/shard_map/ppermute | solution.py:21
  107.2 0.6 copy-done.10
  107.9 5.6 %second.2 = (bf16[4,32,16,128]{3,2,1,0:T(8,128)(2,1)}, bf16[4,32,16,128]{3,2,1,0:T(8,128)(2,1)}) custom-call(bf16[4,36,16,256]{3,2,1,0:T(8,128)(2,1)} %get-tuple-element.15.grad_h, bf16[4,36,2,256]{3,2,1,0:T(2,128)(2,1)} %copy-done.10, bf16[4,36,2,256]{3,2,1,0:T(2,128)(2,1)} %copy-done.11, bf16[3,768,256]{2,1,0:T(8,128)(2,1)} %bitcast.7), custom_call_target="tpu_custom_call" | custom-call | flops 2415919104 | bytes 4194304 | tf_op jit(solution)/shard_map/second/pallas_call | solution.py:165
  113.5 3.2 %collective-permute-start.10 = (bf16[4,32,16,128]{3,2,1,0:T(8,128)(2,1)}, bf16[4,32,16,128]{3,2,1,0:T(8,128)(2,1)S(1)}, u32[]{:S(2)}, u32[]{:S(2)}) collective-permute-start(bf16[4,32,16,128]{3,2,1,0:T(8,128)(2,1)} %get-tuple-element.19), channel_id=1, source_target_pairs={{0,1},{1,0},{2,3},{3,2},{4,5},{5,4},{6,7},{7,6},{8,9},{9,8},{10,11... | collective-permute-start | bytes 1572872 | tf_op jit(solution)/shard_map/ppermute | solution.py:25
  116.8 0.6 copy-done.12
  117.4 0.1 copy-done.13
  117.5 5.7 %second.3 = (bf16[4,32,16,128]{3,2,1,0:T(8,128)(2,1)}, bf16[4,32,16,128]{3,2,1,0:T(8,128)(2,1)}) custom-call(bf16[4,36,16,256]{3,2,1,0:T(8,128)(2,1)} %get-tuple-element.20.grad_h, bf16[4,36,2,256]{3,2,1,0:T(2,128)(2,1)} %copy-done.12, bf16[4,36,2,256]{3,2,1,0:T(2,128)(2,1)} %copy-done.13, bf16[3,768,256]{2,1,0:T(8,128)(2,1)} %bitcast.8), custom_call_target="tpu_custom_call" | custom-call | flops 2415919104 | bytes 4194304 | tf_op jit(solution)/shard_map/second/pallas_call | solution.py:165
  123.2 0.4 broadcast_in_dim.3
  123.6 0.6 copy-done.6
  124.2 0.1 constant_dynamic-update-slice_fusion.6
  124.3 4.6 %collective-permute-done.10 = bf16[4,32,16,128]{3,2,1,0:T(8,128)(2,1)S(1)} collective-permute-done((bf16[4,32,16,128]{3,2,1,0:T(8,128)(2,1)}, bf16[4,32,16,128]{3,2,1,0:T(8,128)(2,1)S(1)}, u32[]{:S(2)}, u32[]{:S(2)}) %collective-permute-start.10) | collective-permute-done | bytes 524320 | tf_op jit(solution)/shard_map/ppermute | solution.py:25
  128.8 0.1 constant_dynamic-update-slice_fusion.5
  128.9 0.1 constant_dynamic-update-slice_fusion.4
  129.0 8.9 %collective-permute-done.14 = bf16[4,32,16,128]{3,2,1,0:T(8,128)(2,1)S(1)} collective-permute-done((bf16[4,32,16,128]{3,2,1,0:T(8,128)(2,1)}, bf16[4,32,16,128]{3,2,1,0:T(8,128)(2,1)S(1)}, u32[]{:S(2)}, u32[]{:S(2)}) %collective-permute-start.14) | collective-permute-done | bytes 524320 | tf_op jit(solution)/shard_map/ppermute | solution.py:25
  137.9 0.8 constant_dynamic-update-slice_fusion.3
  (36 shorter events, 0.2 us)
Async XLA Ops:
  0.0 13.7 %copy-start = (bf16[3,3,256,256]{3,2,1,0:T(8,128)(2,1)S(1)}, bf16[3,3,256,256]{3,2,1,0:T(8,128)(2,1)}, u32[]{:S(2)}) copy-start(bf16[3,3,256,256]{3,2,1,0:T(8,128)(2,1)} %param.6) | copy-start | bytes 3538948
  3.0 26.7 %collective-permute-start = (bf16[8,32,16,128]{3,2,1,0:T(8,128)(2,1)}, bf16[8,32,16,128]{3,2,1,0:T(8,128)(2,1)S(1)}, u32[]{:S(2)}, u32[]{:S(2)}) collective-permute-start(bf16[8,32,16,128]{3,2,1,0:T(8,128)(2,1)} %get-tuple-element.34), channel_id=1, source_target_pairs={{0,1},{1,0},{2,3},{3,2},{4,5},{5,4},{6,7},{7,6},{8,9},{9,8},{10,11... | collective-permute-start | bytes 3145736 | tf_op jit(solution)/shard_map/ppermute | solution.py:25
  8.3 27.7 %collective-permute-start.5 = (bf16[16,2,16,128]{3,2,1,0:T(8,128)(2,1)}, bf16[16,2,16,128]{3,2,1,0:T(8,128)(2,1)S(1)}, u32[]{:S(2)}, u32[]{:S(2)}) collective-permute-start(bf16[16,2,16,128]{3,2,1,0:T(8,128)(2,1)} %get-tuple-element.30), channel_id=1, source_target_pairs={{0,32},{32,64},{64,96},{1,33},{33,65},{65,97},{2,34},{34,66},{66,9... | collective-permute-start | bytes 393224 | tf_op jit(solution)/shard_map/ppermute | solution.py:16
  11.8 24.8 %collective-permute-start.6 = (bf16[16,2,16,128]{3,2,1,0:T(8,128)(2,1)}, bf16[16,2,16,128]{3,2,1,0:T(8,128)(2,1)S(1)}, u32[]{:S(2)}, u32[]{:S(2)}) collective-permute-start(bf16[16,2,16,128]{3,2,1,0:T(8,128)(2,1)} %get-tuple-element.29), channel_id=1, source_target_pairs={{32,0},{64,32},{96,64},{33,1},{65,33},{97,65},{34,2},{66,34},{98,6... | collective-permute-start | bytes 393224 | tf_op jit(solution)/shard_map/ppermute | solution.py:21
  13.8 1.3 copy-start.1
  29.7 13.5 %copy-start.2 = (bf16[8,32,16,128]{3,2,1,0:T(8,128)(2,1)}, bf16[8,32,16,128]{3,2,1,0:T(8,128)(2,1)S(1)}, u32[]{:S(2)}) copy-start(bf16[8,32,16,128]{3,2,1,0:T(8,128)(2,1)S(1)} %collective-permute-done.other) | copy-start | bytes 3145732
  29.7 6.4 %copy-start.3 = (bf16[16,32,16,128]{3,2,1,0:T(8,128)(2,1)S(1)}, bf16[16,32,16,128]{3,2,1,0:T(8,128)(2,1)}, u32[]{:S(2)}) copy-start(bf16[16,32,16,128]{3,2,1,0:T(8,128)(2,1)} %param.5) | copy-start | bytes 6291460
  29.8 9.0 %collective-permute-start.1 = (bf16[8,6,16,256]{3,2,1,0:T(8,128)(2,1)S(1)}, bf16[8,6,16,256]{3,2,1,0:T(8,128)(2,1)S(1)}, u32[]{:S(2)}, u32[]{:S(2)}) collective-permute-start(bf16[8,6,16,256]{3,2,1,0:T(8,128)(2,1)S(1)} %get-tuple-element.32), channel_id=1, source_target_pairs={{0,32},{32,64},{64,96},{1,33},{33,65},{65,97},{2,34},{34,66},{66,9... | collective-permute-start | bytes 1179656 | tf_op jit(solution)/shard_map/ppermute | solution.py:16
  34.1 9.1 %collective-permute-start.2 = (bf16[8,6,16,256]{3,2,1,0:T(8,128)(2,1)S(1)}, bf16[8,6,16,256]{3,2,1,0:T(8,128)(2,1)S(1)}, u32[]{:S(2)}, u32[]{:S(2)}) collective-permute-start(bf16[8,6,16,256]{3,2,1,0:T(8,128)(2,1)S(1)} %get-tuple-element.31), channel_id=1, source_target_pairs={{32,0},{64,32},{96,64},{33,1},{65,33},{97,65},{34,2},{66,34},{98,6... | collective-permute-start | bytes 1179656 | tf_op jit(solution)/shard_map/ppermute | solution.py:21
  36.6 15.6 %copy-start.5 = (bf16[16,36,16,128]{3,2,1,0:T(8,128)(2,1)}, bf16[16,36,16,128]{3,2,1,0:T(8,128)(2,1)S(1)}, u32[]{:S(2)}) copy-start(bf16[16,36,16,128]{3,2,1,0:T(8,128)(2,1)S(1)} %constant_dynamic-update-slice_fusion.gate_own) | copy-start | bytes 7077892
  38.8 6.1 %copy-start.8 = (bf16[8,6,16,256]{3,2,1,0:T(8,128)(2,1)}, bf16[8,6,16,256]{3,2,1,0:T(8,128)(2,1)S(1)}, u32[]{:S(2)}) copy-start(bf16[8,6,16,256]{3,2,1,0:T(8,128)(2,1)S(1)} %collective-permute-done.1.top) | copy-start | bytes 1179652
  43.2 1.7 %copy-start.9 = (bf16[8,6,16,256]{3,2,1,0:T(8,128)(2,1)}, bf16[8,6,16,256]{3,2,1,0:T(8,128)(2,1)S(1)}, u32[]{:S(2)}) copy-start(bf16[8,6,16,256]{3,2,1,0:T(8,128)(2,1)S(1)} %collective-permute-done.2.bottom) | copy-start | bytes 1179652
  44.9 33.8 %collective-permute-start.3 = (bf16[8,44,4,256]{3,2,1,0:T(4,128)(2,1)}, bf16[8,44,4,256]{3,2,1,0:T(4,128)(2,1)}, u32[]{:S(2)}, u32[]{:S(2)}) collective-permute-start(bf16[8,44,4,256]{3,2,1,0:T(4,128)(2,1)} %get-tuple-element.26), channel_id=1, source_target_pairs={{0,2},{2,4},{4,6},{6,8},{8,10},{10,12},{12,14},{14,16},{16,18},{18... | collective-permute-start | bytes 2162696 | tf_op jit(solution)/shard_map/ppermute | solution.py:16
  48.0 30.7 %collective-permute-start.4 = (bf16[8,44,4,256]{3,2,1,0:T(4,128)(2,1)}, bf16[8,44,4,256]{3,2,1,0:T(4,128)(2,1)}, u32[]{:S(2)}, u32[]{:S(2)}) collective-permute-start(bf16[8,44,4,256]{3,2,1,0:T(4,128)(2,1)} %get-tuple-element.25), channel_id=1, source_target_pairs={{2,0},{4,2},{6,4},{8,6},{10,8},{12,10},{14,12},{16,14},{18,16},{20... | collective-permute-start | bytes 2162696 | tf_op jit(solution)/shard_map/ppermute | solution.py:21
  53.6 39.3 %collective-permute-start.11 = (bf16[4,36,16,128]{3,2,1,0:T(8,128)(2,1)}, bf16[4,36,16,128]{3,2,1,0:T(8,128)(2,1)}, u32[]{:S(2)}, u32[]{:S(2)}) collective-permute-start(bf16[4,36,16,128]{3,2,1,0:T(8,128)(2,1)} %get-tuple-element.27), channel_id=1, source_target_pairs={{0,1},{1,0},{2,3},{3,2},{4,5},{5,4},{6,7},{7,6},{8,9},{9,8},{10,11... | collective-permute-start | bytes 1769480 | tf_op jit(solution)/shard_map/ppermute | solution.py:25
  56.9 21.8 %collective-permute-start.7 = (bf16[4,36,16,128]{3,2,1,0:T(8,128)(2,1)}, bf16[4,36,16,128]{3,2,1,0:T(8,128)(2,1)}, u32[]{:S(2)}, u32[]{:S(2)}) collective-permute-start(bf16[4,36,16,128]{3,2,1,0:T(8,128)(2,1)} %get-tuple-element.28), channel_id=1, source_target_pairs={{0,1},{1,0},{2,3},{3,2},{4,5},{5,4},{6,7},{7,6},{8,9},{9,8},{10,11... | collective-permute-start | bytes 1769480 | tf_op jit(solution)/shard_map/ppermute | solution.py:25
  85.5 21.7 %collective-permute-start.8 = (bf16[4,36,2,256]{3,2,1,0:T(2,128)(2,1)}, bf16[4,36,2,256]{3,2,1,0:T(2,128)(2,1)S(1)}, u32[]{:S(2)}, u32[]{:S(2)}) collective-permute-start(bf16[4,36,2,256]{3,2,1,0:T(2,128)(2,1)} %get-tuple-element.16), channel_id=1, source_target_pairs={{0,2},{2,4},{4,6},{6,8},{8,10},{10,12},{12,14},{14,16},{16,18},{18... | collective-permute-start | bytes 442376 | tf_op jit(solution)/shard_map/ppermute | solution.py:16
  87.4 19.8 %collective-permute-start.9 = (bf16[4,36,2,256]{3,2,1,0:T(2,128)(2,1)}, bf16[4,36,2,256]{3,2,1,0:T(2,128)(2,1)S(1)}, u32[]{:S(2)}, u32[]{:S(2)}) collective-permute-start(bf16[4,36,2,256]{3,2,1,0:T(2,128)(2,1)} %get-tuple-element.17), channel_id=1, source_target_pairs={{2,0},{4,2},{6,4},{8,6},{10,8},{12,10},{14,12},{16,14},{18,16},{20... | collective-permute-start | bytes 442376 | tf_op jit(solution)/shard_map/ppermute | solution.py:21
  99.8 17.0 %collective-permute-start.12 = (bf16[4,36,2,256]{3,2,1,0:T(2,128)(2,1)}, bf16[4,36,2,256]{3,2,1,0:T(2,128)(2,1)S(1)}, u32[]{:S(2)}, u32[]{:S(2)}) collective-permute-start(bf16[4,36,2,256]{3,2,1,0:T(2,128)(2,1)} %get-tuple-element.21), channel_id=1, source_target_pairs={{0,2},{2,4},{4,6},{6,8},{8,10},{10,12},{12,14},{14,16},{16,18},{18... | collective-permute-start | bytes 442376 | tf_op jit(solution)/shard_map/ppermute | solution.py:16
  101.7 15.1 %collective-permute-start.13 = (bf16[4,36,2,256]{3,2,1,0:T(2,128)(2,1)}, bf16[4,36,2,256]{3,2,1,0:T(2,128)(2,1)S(1)}, u32[]{:S(2)}, u32[]{:S(2)}) collective-permute-start(bf16[4,36,2,256]{3,2,1,0:T(2,128)(2,1)} %get-tuple-element.22), channel_id=1, source_target_pairs={{2,0},{4,2},{6,4},{8,6},{10,8},{12,10},{14,12},{16,14},{18,16},{20... | collective-permute-start | bytes 442376 | tf_op jit(solution)/shard_map/ppermute | solution.py:21
  107.2 0.6 copy-start.10
  107.2 0.7 copy-start.11
  113.5 15.3 %collective-permute-start.10 = (bf16[4,32,16,128]{3,2,1,0:T(8,128)(2,1)}, bf16[4,32,16,128]{3,2,1,0:T(8,128)(2,1)S(1)}, u32[]{:S(2)}, u32[]{:S(2)}) collective-permute-start(bf16[4,32,16,128]{3,2,1,0:T(8,128)(2,1)} %get-tuple-element.19), channel_id=1, source_target_pairs={{0,1},{1,0},{2,3},{3,2},{4,5},{5,4},{6,7},{7,6},{8,9},{9,8},{10,11... | collective-permute-start | bytes 1572872 | tf_op jit(solution)/shard_map/ppermute | solution.py:25
  116.8 0.6 copy-start.12
  116.8 0.7 copy-start.13
  123.1 1.0 copy-start.6
  123.1 14.8 %collective-permute-start.14 = (bf16[4,32,16,128]{3,2,1,0:T(8,128)(2,1)}, bf16[4,32,16,128]{3,2,1,0:T(8,128)(2,1)S(1)}, u32[]{:S(2)}, u32[]{:S(2)}) collective-permute-start(bf16[4,32,16,128]{3,2,1,0:T(8,128)(2,1)} %get-tuple-element.24), channel_id=1, source_target_pairs={{0,1},{1,0},{2,3},{3,2},{4,5},{5,4},{6,7},{7,6},{8,9},{9,8},{10,11... | collective-permute-start | bytes 1572872 | tf_op jit(solution)/shard_map/ppermute | solution.py:25
  124.2 4.7 %copy-start.7 = (bf16[4,32,16,128]{3,2,1,0:T(8,128)(2,1)S(1)}, bf16[4,32,16,128]{3,2,1,0:T(8,128)(2,1)}, u32[]{:S(2)}) copy-start(bf16[4,32,16,128]{3,2,1,0:T(8,128)(2,1)} %get-tuple-element.23) | copy-start | bytes 1572868
  129.0 9.0 %copy-start.4 = (bf16[16,32,16,128]{3,2,1,0:T(8,128)(2,1)}, bf16[16,32,16,128]{3,2,1,0:T(8,128)(2,1)S(1)}, u32[]{:S(2)}) copy-start(bf16[16,32,16,128]{3,2,1,0:T(8,128)(2,1)S(1)} %constant_dynamic-update-slice_fusion.4) | copy-start | bytes 6291460

commit v2 on v1

--- a/solution.py
+++ b/solution.py
@@ -36,7 +36,7 @@
 
 
 def fill_shifted(shifted, middle, left, right, spacing):
-    rows, cols, channels = middle.shape
+    _, cols, channels = middle.shape
     shifted[:, spacing:, :channels] = middle[:, : cols - spacing]
     shifted[:, :spacing, :channels] = left
     shifted[:, :, channels : 2 * channels] = middle
@@ -55,14 +55,20 @@
     return total
 
 
-def first_kernel(part_ref, own, other, top, bottom, left, right, gate_own, gate_other, weight, grad_h, edge_left, edge_right, whole, shifted):
+def first_kernel(part_ref, own, other, top_own, top_other, bottom_own, bottom_other, left_own, left_other, right_own, right_other, gate_own, gate_other, weight, grad_h, edge_left, edge_right, whole, shifted):
     rows = own.shape[1]
     half = own.shape[3]
-    whole[:SPREAD] = top[0]
-    whole[SPREAD : SPREAD + rows, :, :half] = own[0]
-    whole[SPREAD : SPREAD + rows, :, half:] = other[0]
-    whole[SPREAD + rows :] = bottom[0]
-    fill_shifted(shifted, whole[...], left[0], right[0], FAR)
+    halves = (
+        (slice(0, half), own, top_own, bottom_own, left_own, right_own),
+        (slice(half, 2 * half), other, top_other, bottom_other, left_other, right_other),
+    )
+    for lanes, middle, top, bottom, _, _ in halves:
+        whole[:SPREAD, :, lanes] = top[0]
+        whole[SPREAD : SPREAD + rows, :, lanes] = middle[0]
+        whole[SPREAD + rows :, :, lanes] = bottom[0]
+    left = jnp.concatenate([left_own[0], left_other[0]], axis=2)
+    right = jnp.concatenate([right_own[0], right_other[0]], axis=2)
+    fill_shifted(shifted, whole[...], left, right, FAR)
     out_rows = rows + 2 * NEAR
     total = taps_sum(shifted, weight, FAR, out_rows).reshape(out_rows, own.shape[2], 2 * half)
     kept_own = jnp.where(gate_own[0].astype(jnp.float32) > 0, total[:, :, :half], 0.0).astype(jnp.bfloat16)
@@ -82,7 +88,7 @@
     sent[0] = total[:, :, half:]
 
 
-def per_device(grad_out, pre_act, weight_one, weight_two):
+def on_device(grad_out, pre_act, weight_one, weight_two):
     batch, rows, cols, half = grad_out.shape
     mine = batch // 2
     part = lax.axis_index("filt")
@@ -90,29 +96,38 @@
     other_at = (1 - part) * mine
     channels = 2 * half
 
+    def halo_rows(x):
+        return from_before(x[:, rows - SPREAD :], "row"), from_after(x[:, :SPREAD], "row")
+
+    def halo_cols(x, top, bottom):
+        last = [piece[:, :, cols - FAR :] for piece in (top, x, bottom)]
+        first = [piece[:, :, :FAR] for piece in (top, x, bottom)]
+        return from_before(jnp.concatenate(last, axis=1), "col"), from_after(jnp.concatenate(first, axis=1), "col")
+
     other = to_partner(lax.dynamic_slice_in_dim(grad_out, other_at, mine, 0))
-    own = lax.dynamic_slice_in_dim(grad_out, own_at, mine, 0)
     gate_top = from_before(pre_act[:, rows - NEAR :], "row")
     gate_bottom = from_after(pre_act[:, :NEAR], "row")
     gate = jnp.concatenate([gate_top, pre_act, gate_bottom], axis=1)
-    gate_sent = lax.dynamic_slice_in_dim(gate, other_at, mine, 0)
+    own = lax.dynamic_slice_in_dim(grad_out, own_at, mine, 0)
+    top_own, bottom_own = halo_rows(own)
+    left_own, right_own = halo_cols(own, top_own, bottom_own)
     first_weight = relative_weight(weight_two, part)
     second_weight = relative_weight(weight_one, part)
-
-    both = jnp.concatenate([own, other], axis=3)
-    top = from_before(both[:, rows - SPREAD :], "row")
-    bottom = from_after(both[:, :SPREAD], "row")
-    tall = jnp.concatenate([top, both, bottom], axis=1)
-    left = from_before(tall[:, :, cols - FAR :], "col")
-    right = from_after(tall[:, :, :FAR], "col")
+    top_other, bottom_other = halo_rows(other)
+    gate_others = []
+    start = 0
+    for size in CHUNKS:
+        gate_others.append(to_partner(lax.dynamic_slice_in_dim(gate, other_at + start, size, 0)))
+        start += size
+    left_other, right_other = halo_cols(other, top_other, bottom_other)
 
     tall_rows = rows + 2 * SPREAD
     gate_rows = rows + 2 * NEAR
     where = jnp.reshape(own_at, (1,)).astype(jnp.int32)
     result = jnp.zeros_like(grad_out)
     start = 0
-    for size in CHUNKS:
-        gate_other = to_partner(gate_sent[start : start + size])
+    for step, size in enumerate(CHUNKS):
+        gate_other = gate_others[step]
 
         def by_own(i, ref, start=start):
             return (ref[0] + start + i, 0, 0, 0)
@@ -139,10 +154,8 @@
                 in_specs=[
                     pl.BlockSpec((1, rows, cols, half), by_own),
                     pl.BlockSpec((1, rows, cols, half), by_mine),
-                    pl.BlockSpec((1, SPREAD, cols, channels), by_mine),
-                    pl.BlockSpec((1, SPREAD, cols, channels), by_mine),
-                    pl.BlockSpec((1, tall_rows, FAR, channels), by_mine),
-                    pl.BlockSpec((1, tall_rows, FAR, channels), by_mine),
+                    *[pl.BlockSpec((1, SPREAD, cols, half), by_mine)] * 4,
+                    *[pl.BlockSpec((1, tall_rows, FAR, half), by_mine)] * 4,
                     pl.BlockSpec((1, gate_rows, cols, half), by_own),
                     pl.BlockSpec((1, gate_rows, cols, half), by_chunk),
                     pl.BlockSpec((3, 3 * channels, channels), whole_weight),
@@ -159,7 +172,7 @@
             ),
             cost_estimate=pl.CostEstimate(flops=size * 2 * gate_rows * cols * 9 * channels * channels, bytes_accessed=size * 2**20, transcendentals=0),
             name="first",
-        )(where, grad_out, other, top, bottom, left, right, gate, gate_other, first_weight)
+        )(where, grad_out, other, top_own, top_other, bottom_own, bottom_other, left_own, left_other, right_own, right_other, gate, gate_other, first_weight)
         h_left = from_before(edge_right, "col")
         h_right = from_after(edge_left, "col")
         kept, sent = pl.pallas_call(
@@ -193,7 +206,7 @@
 def solution(mesh):
     placed = (P(None, "row", "col", "filt"), P(None, "row", "col", "filt"), P(), P())
     return jax.shard_map(
-        per_device,
+        on_device,
         mesh=mesh,
         in_specs=placed,
         out_specs=P(None, "row", "col", "filt"),

time: 140 us -> 150 us (1.071)
  waiting for transfers between devices: 52.4 us -> 33.4 us
  local copies, waits for them, and re-layouts: 14.6 us -> 28.5 us
  starting transfers between devices: 43.9 us -> 55.3 us
  other arithmetic: 2.58 us -> 5.93 us
    ppermute x5, waiting for transfers between devices: 45.8 us -> 15.3 us  [to_partner(): return lax.ppermute(x, 'filt', [(0, 1), (1, 0)])]
    ppermute x5 -> x7, waiting for transfers between devices: 2.19 us -> 12.3 us  [from_before(): return lax.ppermute(x, axis, [(i, i + 1) for i in range(count - 1)])]
    ppermute x5 -> x7, starting transfers between devices: 14.7 us -> 22.7 us  [from_before(): return lax.ppermute(x, axis, [(i, i + 1) for i in range(count - 1)])]
    slice x2 -> x9, local copies, waits for them, and re-layouts: 2.96 us -> 10.3 us  [the longest x6 5.75 us: halo_cols(): first = [piece[:, :, :FAR] for piece in (top, x, bottom)]]
    ppermute x5 -> x7, starting transfers between devices: 19.1 us -> 23.1 us  [from_after(): return lax.ppermute(x, axis, [(i + 1, i) for i in range(count - 1)])]
    unnamed x30 -> x36, local copies, waits for them, and re-layouts: 3.72 us -> 5.95 us
    concatenate x2 -> x4, other arithmetic: 1.74 us -> 3.3 us  [the longest x2 2.02 us: halo_cols(): jnp.concatenate(first, axis=1)]
    ppermute x5 -> x7, waiting for transfers between devices: 4.4 us -> 5.77 us  [from_after(): return lax.ppermute(x, axis, [(i + 1, i) for i in range(count - 1)])]
  transfers between devices with their start and end apart: 15 -> 19, of which waited for: 6 -> 6; matrix products, arithmetic and copies ran while one was open for 6% -> 18% of each run, Pallas kernels for 18% -> 17%
where the time goes in v2:
time: 150 us; the launch traced here: 149 us
  starting transfers between devices  55.3 us (37%)
  waiting for transfers between devices  33.4 us (22%)
  local copies, waits for them, and re-layouts  28.5 us (19%)
  Pallas kernels  25 us (17%)
  other arithmetic  5.93 us (4%)
    ppermute x7, starting transfers between devices, from_after(): return lax.ppermute(x, axis, [(i + 1, i) for i in range(count - 1)])  23.1 us
    ppermute x7, starting transfers between devices, from_before(): return lax.ppermute(x, axis, [(i, i + 1) for i in range(count - 1)])  22.7 us
    ppermute x5, waiting for transfers between devices, to_partner(): return lax.ppermute(x, 'filt', [(0, 1), (1, 0)])  15.3 us
    pallas_call x2, Pallas kernels, on_device(): pl.pallas_call(first_kernel, out_shape=(jax.ShapeDtypeStruct((size, gate_...  13.7 us
    ppermute x7, waiting for transfers between devices, from_before(): return lax.ppermute(x, axis, [(i, i + 1) for i in range(count - 1)])  12.3 us
    pallas_call x2, Pallas kernels, on_device(): pl.pallas_call(second_kernel, out_shape=(jax.ShapeDtypeStruct((size, rows...  11.3 us
    ppermute x5, starting transfers between devices, to_partner(): return lax.ppermute(x, 'filt', [(0, 1), (1, 0)])  9.54 us
    unnamed x36, local copies, waits for them, and re-layouts  5.95 us
  transfers between devices with their start and end apart: 19, of which 6 were waited for; matrix products, arithmetic and copies ran while one was open for 18% of the time, Pallas kernels for 17%

profile of v2, /device:TPU:9, one launch (start us, length us, event | category | flops | bytes accessed | tf_op | source)
XLA Modules:
  0.0 148.6 jit_solution(8779980220375256030)
XLA Ops:
  0.0 2.5 %constant_dynamic-slice_fusion.6 = bf16[8,32,16,128]{3,2,1,0:T(8,128)(2,1)} fusion(bf16[16,32,16,128]{3,2,1,0:T(8,128)(2,1)} %own.3, s32[]{:T(128)S(6)} %select_n.28), kind=kLoop, calls=%fused_computation.31 | loop fusion | bytes 2097156 | tf_op jit(solution)/shard_map/dynamic_slice | solution.py:107
  2.5 3.6 %collective-permute-start = (bf16[8,32,16,128]{3,2,1,0:T(8,128)(2,1)}, bf16[8,32,16,128]{3,2,1,0:T(8,128)(2,1)}, u32[]{:S(2)}, u32[]{:S(2)}) collective-permute-start(bf16[8,32,16,128]{3,2,1,0:T(8,128)(2,1)} %constant_dynamic-slice_fusion.6), channel_id=1, source_target_pairs={{0,1},{1,0},{2,3},{3,2},{4,5},{5,4},{6,7},{7,6},{8,9},{9,8},{10,11... | collective-permute-start | bytes 3145736 | tf_op jit(solution)/shard_map/ppermute | solution.py:25
  6.1 1.8 %constant_dynamic-slice_fusion.1 = (bf16[8,6,16,128]{3,2,1,0:T(8,128)(2,1)}, bf16[8,6,16,128]{3,2,1,0:T(8,128)(2,1)}) fusion(bf16[16,32,16,128]{3,2,1,0:T(8,128)(2,1)} %own.3, s32[]{:T(128)S(6)} %select_n.29, s32[]{:T(128)S(6)} %add.33), kind=kLoop, calls=%fused_computation.22 | loop fusion | bytes 786440 | tf_op jit(solution)/shard_map/slice | solution.py:100
  7.9 3.5 %collective-permute-start.1 = (bf16[8,6,16,128]{3,2,1,0:T(8,128)(2,1)}, bf16[8,6,16,128]{3,2,1,0:T(8,128)(2,1)}, u32[]{:S(2)}, u32[]{:S(2)}) collective-permute-start(bf16[8,6,16,128]{3,2,1,0:T(8,128)(2,1)} %get-tuple-element.32), channel_id=1, source_target_pairs={{0,32},{32,64},{64,96},{1,33},{33,65},{65,97},{2,34},{34,66},{66,9... | collective-permute-start | bytes 589832 | tf_op jit(solution)/shard_map/ppermute | solution.py:16
  11.4 1.9 %collective-permute-start.3 = (bf16[8,6,16,128]{3,2,1,0:T(8,128)(2,1)}, bf16[8,6,16,128]{3,2,1,0:T(8,128)(2,1)}, u32[]{:S(2)}, u32[]{:S(2)}) collective-permute-start(bf16[8,6,16,128]{3,2,1,0:T(8,128)(2,1)} %get-tuple-element.31), channel_id=1, source_target_pairs={{32,0},{64,32},{96,64},{33,1},{65,33},{97,65},{34,2},{66,34},{98,6... | collective-permute-start | bytes 589832 | tf_op jit(solution)/shard_map/ppermute | solution.py:21
  13.3 1.7 %fusion.6 = (bf16[16,2,16,128]{3,2,1,0:T(8,128)(2,1)}, bf16[16,2,16,128]{3,2,1,0:T(8,128)(2,1)}) fusion(bf16[16,32,16,128]{3,2,1,0:T(8,128)(2,1)} %param.5), kind=kLoop, calls=%fused_computation.32 | loop fusion | bytes 524288 | tf_op jit(solution)/shard_map/slice | solution.py:109
  15.0 3.6 %collective-permute-start.9 = (bf16[16,2,16,128]{3,2,1,0:T(8,128)(2,1)}, bf16[16,2,16,128]{3,2,1,0:T(8,128)(2,1)}, u32[]{:S(2)}, u32[]{:S(2)}) collective-permute-start(bf16[16,2,16,128]{3,2,1,0:T(8,128)(2,1)} %get-tuple-element.28), channel_id=1, source_target_pairs={{0,32},{32,64},{64,96},{1,33},{33,65},{65,97},{2,34},{34,66},{66,9... | collective-permute-start | bytes 393224 | tf_op jit(solution)/shard_map/ppermute | solution.py:16
  18.7 1.9 %collective-permute-start.10 = (bf16[16,2,16,128]{3,2,1,0:T(8,128)(2,1)}, bf16[16,2,16,128]{3,2,1,0:T(8,128)(2,1)}, u32[]{:S(2)}, u32[]{:S(2)}) collective-permute-start(bf16[16,2,16,128]{3,2,1,0:T(8,128)(2,1)} %get-tuple-element.27), channel_id=1, source_target_pairs={{32,0},{64,32},{96,64},{33,1},{65,33},{97,65},{34,2},{66,34},{98,6... | collective-permute-start | bytes 393224 | tf_op jit(solution)/shard_map/ppermute | solution.py:21
  20.7 1.3 fusion.8
  22.1 0.9 fusion.4
  23.0 2.2 %constant_dynamic-slice_fusion.5 = (bf16[8,32,4,128]{3,2,1,0:T(4,128)(2,1)}, bf16[8,32,4,128]{3,2,1,0:T(4,128)(2,1)}) fusion(bf16[16,32,16,128]{3,2,1,0:T(8,128)(2,1)} %own.3, s32[]{:T(128)S(6)} %select_n.29, s32[]{:T(128)S(6)} %add.34), kind=kLoop, calls=%fused_computation.30 | loop fusion | bytes 1048584 | tf_op jit(solution)/shard_map/slice | solution.py:104
  25.3 8.5 %collective-permute-done.9 = bf16[16,2,16,128]{3,2,1,0:T(8,128)(2,1)} collective-permute-done((bf16[16,2,16,128]{3,2,1,0:T(8,128)(2,1)}, bf16[16,2,16,128]{3,2,1,0:T(8,128)(2,1)}, u32[]{:S(2)}, u32[]{:S(2)}) %collective-permute-start.9) | collective-permute-done | bytes 131104 | tf_op jit(solution)/shard_map/ppermute | solution.py:16
  34.7 2.2 %constant_dynamic-update-slice_fusion.1 = bf16[16,36,16,128]{3,2,1,0:T(8,128)(2,1)S(1)} fusion(bf16[16,36,16,128]{3,2,1,0:T(8,128)(2,1)S(1)} %constant_dynamic-update-slice_fusion.2, bf16[16,32,16,128]{3,2,1,0:T(8,128)(2,1)} %param.5), kind=kLoop, calls=%fused_computation.19 | loop fusion | bytes 4194304
  36.9 1.0 constant_dynamic-update-slice_fusion.gate_own
  37.9 1.5 %constant_dynamic-slice_fusion.3 = (bf16[4,36,16,128]{3,2,1,0:T(8,128)(2,1)}, bf16[4,36,16,128]{3,2,1,0:T(8,128)(2,1)}) fusion(bf16[16,36,16,128]{3,2,1,0:T(8,128)(2,1)S(1)} %constant_dynamic-update-slice_fusion.gate_own, s32[]{:T(128)S(6)} %select_n.33, s32[]{:T(128)S(6)} %select_n.28), kind=kLoop, calls=%fused_computation.26 | loop fusion | bytes 2359304 | tf_op jit(solution)/shard_map/dynamic_slice | solution.py:120
  39.5 3.0 %collective-permute-start.11 = (bf16[4,36,16,128]{3,2,1,0:T(8,128)(2,1)}, bf16[4,36,16,128]{3,2,1,0:T(8,128)(2,1)}, u32[]{:S(2)}, u32[]{:S(2)}) collective-permute-start(bf16[4,36,16,128]{3,2,1,0:T(8,128)(2,1)} %get-tuple-element.26), channel_id=1, source_target_pairs={{0,1},{1,0},{2,3},{3,2},{4,5},{5,4},{6,7},{7,6},{8,9},{9,8},{10,11... | collective-permute-start | bytes 1769480 | tf_op jit(solution)/shard_map/ppermute | solution.py:25
  42.4 1.0 fusion.13
  43.4 1.0 fusion.14
  44.7 3.1 %collective-permute-start.5 = (bf16[8,44,4,128]{3,2,1,0:T(4,128)(2,1)S(1)}, bf16[8,44,4,128]{3,2,1,0:T(4,128)(2,1)S(1)}, u32[]{:S(2)}, u32[]{:S(2)}) collective-permute-start(bf16[8,44,4,128]{3,2,1,0:T(4,128)(2,1)S(1)} %pad_maximum_fusion.2), channel_id=1, source_target_pairs={{0,2},{2,4},{4,6},{6,8},{8,10},{10,12},{12,14},{14,16},{16,18},{18... | collective-permute-start | bytes 1081352 | tf_op jit(solution)/shard_map/ppermute | solution.py:16
  47.8 1.0 pad_maximum_fusion.4
  48.9 4.3 %collective-permute-start.7 = (bf16[8,44,4,128]{3,2,1,0:T(4,128)(2,1)}, bf16[8,44,4,128]{3,2,1,0:T(4,128)(2,1)}, u32[]{:S(2)}, u32[]{:S(2)}) collective-permute-start(bf16[8,44,4,128]{3,2,1,0:T(4,128)(2,1)} %pad_maximum_fusion.4), channel_id=1, source_target_pairs={{2,0},{4,2},{6,4},{8,6},{10,8},{12,10},{14,12},{16,14},{18,16},{20... | collective-permute-start | bytes 1081352 | tf_op jit(solution)/shard_map/ppermute | solution.py:21
  53.1 1.1 fusion.10
  54.2 5.5 %collective-permute-start.2 = (bf16[8,6,16,128]{3,2,1,0:T(8,128)(2,1)S(1)}, bf16[8,6,16,128]{3,2,1,0:T(8,128)(2,1)S(1)}, u32[]{:S(2)}, u32[]{:S(2)}) collective-permute-start(bf16[8,6,16,128]{3,2,1,0:T(8,128)(2,1)S(1)} %get-tuple-element.40), channel_id=1, source_target_pairs={{0,32},{32,64},{64,96},{1,33},{33,65},{65,97},{2,34},{34,66},{66,9... | collective-permute-start | bytes 589832 | tf_op jit(solution)/shard_map/ppermute | solution.py:16
  59.7 1.5 fusion.9
  61.2 1.1 collective-permute-done.2.top_other
  62.3 1.9 %collective-permute-start.4 = (bf16[8,6,16,128]{3,2,1,0:T(8,128)(2,1)S(1)}, bf16[8,6,16,128]{3,2,1,0:T(8,128)(2,1)S(1)}, u32[]{:S(2)}, u32[]{:S(2)}) collective-permute-start(bf16[8,6,16,128]{3,2,1,0:T(8,128)(2,1)S(1)} %get-tuple-element.39), channel_id=1, source_target_pairs={{32,0},{64,32},{96,64},{33,1},{65,33},{97,65},{34,2},{66,34},{98,6... | collective-permute-start | bytes 589832 | tf_op jit(solution)/shard_map/ppermute | solution.py:21
  64.3 5.8 %collective-permute-done.4.bottom_other = bf16[8,6,16,128]{3,2,1,0:T(8,128)(2,1)S(1)} collective-permute-done((bf16[8,6,16,128]{3,2,1,0:T(8,128)(2,1)S(1)}, bf16[8,6,16,128]{3,2,1,0:T(8,128)(2,1)S(1)}, u32[]{:S(2)}, u32[]{:S(2)}) %collective-permute-start.4) | collective-permute-done | bytes 196640 | tf_op jit(solution)/shard_map/ppermute | solution.py:21
  70.8 1.0 pad_maximum_fusion.5
  71.8 2.2 %collective-permute-start.8 = (bf16[8,44,4,128]{3,2,1,0:T(4,128)(2,1)}, bf16[8,44,4,128]{3,2,1,0:T(4,128)(2,1)}, u32[]{:S(2)}, u32[]{:S(2)}) collective-permute-start(bf16[8,44,4,128]{3,2,1,0:T(4,128)(2,1)} %pad_maximum_fusion.5), channel_id=1, source_target_pairs={{2,0},{4,2},{6,4},{8,6},{10,8},{12,10},{14,12},{16,14},{18,16},{20... | collective-permute-start | bytes 1081352 | tf_op jit(solution)/shard_map/ppermute | solution.py:21
  73.9 1.0 pad_maximum_fusion.3
  75.7 3.1 %collective-permute-start.6 = (bf16[8,44,4,128]{3,2,1,0:T(4,128)(2,1)}, bf16[8,44,4,128]{3,2,1,0:T(4,128)(2,1)}, u32[]{:S(2)}, u32[]{:S(2)}) collective-permute-start(bf16[8,44,4,128]{3,2,1,0:T(4,128)(2,1)} %pad_maximum_fusion.3), channel_id=1, source_target_pairs={{0,2},{2,4},{4,6},{6,8},{8,10},{10,12},{12,14},{14,16},{16,18},{18... | collective-permute-start | bytes 1081352 | tf_op jit(solution)/shard_map/ppermute | solution.py:16
  78.8 1.6 %fusion.1 = (bf16[3,3,256,256]{3,2,1,0:T(8,128)(2,1)}, bf16[3,3,256,256]{3,2,1,0:T(8,128)(2,1)S(1)}) fusion(bf16[3,3,256,256]{3,2,1,0:T(8,128)(2,1)S(1)} %copy-done, bf16[3,3,128,256]{3,2,1,0:T(8,128)(2,1)S(1)} %get-tuple-element.34, bf16[3,3,128,256]{3,2,1,0:T(8,128)(2,1)S(1)} %get-tuple-element.33, bf16[3,3,256,128]{3,2,1,0:T(8,128)(2,1)S(1)} %copy-done.3, ...), kind=kLoop, calls=%fused_computation.2 | loop fusion | flops 8257536 | bytes 8257537 | tf_op jit(solution)/shard_map/jit(_where)/select_n | solution.py:33
  80.5 1.6 %copy.5 = bf16[3,3,256,256]{3,2,1,0:T(8,128)(2,1)} copy(bf16[3,3,256,256]{2,3,1,0:T(8,128)(2,1)S(1)} %reverse_bitcast_fusion.1) | data formatting | bytes 2359296 | tf_op jit(solution)/shard_map/transpose | solution.py:34
  82.2 1.5 %copy.6 = bf16[3,3,256,256]{3,2,1,0:T(8,128)(2,1)} copy(bf16[3,3,256,256]{2,3,1,0:T(8,128)(2,1)S(1)} %reverse_bitcast_fusion) | data formatting | bytes 2359296 | tf_op jit(solution)/shard_map/transpose | solution.py:34
  83.7 2.8 %collective-permute-done.6.left_other = bf16[8,44,4,128]{3,2,1,0:T(4,128)(2,1)} collective-permute-done((bf16[8,44,4,128]{3,2,1,0:T(4,128)(2,1)}, bf16[8,44,4,128]{3,2,1,0:T(4,128)(2,1)}, u32[]{:S(2)}, u32[]{:S(2)}) %collective-permute-start.6) | collective-permute-done | bytes 360480 | tf_op jit(solution)/shard_map/ppermute | solution.py:16
  86.5 6.9 %first.2 = (bf16[4,36,16,256]{3,2,1,0:T(8,128)(2,1)}, bf16[4,36,2,256]{3,2,1,0:T(2,128)(2,1)}, bf16[4,36,2,256]{3,2,1,0:T(2,128)(2,1)}) custom-call(s32[1]{0:T(128)} %bitcast.part_ref, bf16[16,32,16,128]{3,2,1,0:T(8,128)(2,1)} %own.3, bf16[8,32,16,128]{3,2,1,0:T(8,128)(2,1)} %collective-permute-done.other, ...), custom_call_target="tpu_custom_call" | custom-call | flops 2717908992 | bytes 4194304 | tf_op jit(solution)/shard_map/first/pallas_call | solution.py:144
  93.4 1.9 %collective-permute-start.12 = (bf16[4,36,2,256]{3,2,1,0:T(2,128)(2,1)}, bf16[4,36,2,256]{3,2,1,0:T(2,128)(2,1)S(1)}, u32[]{:S(2)}, u32[]{:S(2)}) collective-permute-start(bf16[4,36,2,256]{3,2,1,0:T(2,128)(2,1)} %get-tuple-element.16), channel_id=1, source_target_pairs={{0,2},{2,4},{4,6},{6,8},{8,10},{10,12},{12,14},{14,16},{16,18},{18... | collective-permute-start | bytes 442376 | tf_op jit(solution)/shard_map/ppermute | solution.py:16
  95.3 5.5 %collective-permute-start.13 = (bf16[4,36,2,256]{3,2,1,0:T(2,128)(2,1)}, bf16[4,36,2,256]{3,2,1,0:T(2,128)(2,1)S(1)}, u32[]{:S(2)}, u32[]{:S(2)}) collective-permute-start(bf16[4,36,2,256]{3,2,1,0:T(2,128)(2,1)} %get-tuple-element.17), channel_id=1, source_target_pairs={{2,0},{4,2},{6,4},{8,6},{10,8},{12,10},{14,12},{16,14},{18,16},{20... | collective-permute-start | bytes 442376 | tf_op jit(solution)/shard_map/ppermute | solution.py:21
  100.8 6.9 %first.3 = (bf16[4,36,16,256]{3,2,1,0:T(8,128)(2,1)}, bf16[4,36,2,256]{3,2,1,0:T(2,128)(2,1)}, bf16[4,36,2,256]{3,2,1,0:T(2,128)(2,1)}) custom-call(s32[1]{0:T(128)} %bitcast.part_ref, bf16[16,32,16,128]{3,2,1,0:T(8,128)(2,1)} %own.3, bf16[8,32,16,128]{3,2,1,0:T(8,128)(2,1)} %collective-permute-done.other, ...), custom_call_target="tpu_custom_call" | custom-call | flops 2717908992 | bytes 4194304 | tf_op jit(solution)/shard_map/first/pallas_call | solution.py:144
  107.7 1.9 %collective-permute-start.16 = (bf16[4,36,2,256]{3,2,1,0:T(2,128)(2,1)}, bf16[4,36,2,256]{3,2,1,0:T(2,128)(2,1)S(1)}, u32[]{:S(2)}, u32[]{:S(2)}) collective-permute-start(bf16[4,36,2,256]{3,2,1,0:T(2,128)(2,1)} %get-tuple-element.21), channel_id=1, source_target_pairs={{0,2},{2,4},{4,6},{6,8},{8,10},{10,12},{12,14},{14,16},{16,18},{18... | collective-permute-start | bytes 442376 | tf_op jit(solution)/shard_map/ppermute | solution.py:16
  109.6 5.5 %collective-permute-start.17 = (bf16[4,36,2,256]{3,2,1,0:T(2,128)(2,1)}, bf16[4,36,2,256]{3,2,1,0:T(2,128)(2,1)S(1)}, u32[]{:S(2)}, u32[]{:S(2)}) collective-permute-start(bf16[4,36,2,256]{3,2,1,0:T(2,128)(2,1)} %get-tuple-element.22), channel_id=1, source_target_pairs={{2,0},{4,2},{6,4},{8,6},{10,8},{12,10},{14,12},{16,14},{18,16},{20... | collective-permute-start | bytes 442376 | tf_op jit(solution)/shard_map/ppermute | solution.py:21
  115.8 5.7 %second.2 = (bf16[4,32,16,128]{3,2,1,0:T(8,128)(2,1)}, bf16[4,32,16,128]{3,2,1,0:T(8,128)(2,1)}) custom-call(bf16[4,36,16,256]{3,2,1,0:T(8,128)(2,1)} %get-tuple-element.15.grad_h, bf16[4,36,2,256]{3,2,1,0:T(2,128)(2,1)} %copy-done.13, bf16[4,36,2,256]{3,2,1,0:T(2,128)(2,1)} %copy-done.14, bf16[3,768,256]{2,1,0:T(8,128)(2,1)} %bitcast.7), custom_call_target="tpu_custom_call" | custom-call | flops 2415919104 | bytes 4194304 | tf_op jit(solution)/shard_map/second/pallas_call | solution.py:178
  121.5 1.1 collective-permute-start.14
  123.3 5.6 %second.3 = (bf16[4,32,16,128]{3,2,1,0:T(8,128)(2,1)}, bf16[4,32,16,128]{3,2,1,0:T(8,128)(2,1)}) custom-call(bf16[4,36,16,256]{3,2,1,0:T(8,128)(2,1)} %get-tuple-element.20.grad_h, bf16[4,36,2,256]{3,2,1,0:T(2,128)(2,1)} %copy-done.15, bf16[4,36,2,256]{3,2,1,0:T(2,128)(2,1)} %copy-done.16, bf16[3,768,256]{2,1,0:T(8,128)(2,1)} %bitcast.8), custom_call_target="tpu_custom_call" | custom-call | flops 2415919104 | bytes 4194304 | tf_op jit(solution)/shard_map/second/pallas_call | solution.py:178
  128.9 1.9 %collective-permute-start.18 = (bf16[4,32,16,128]{3,2,1,0:T(8,128)(2,1)}, bf16[4,32,16,128]{3,2,1,0:T(8,128)(2,1)}, u32[]{:S(2)}, u32[]{:S(2)}) collective-permute-start(bf16[4,32,16,128]{3,2,1,0:T(8,128)(2,1)} %get-tuple-element.24), channel_id=1, source_target_pairs={{0,1},{1,0},{2,3},{3,2},{4,5},{5,4},{6,7},{7,6},{8,9},{9,8},{10,11... | collective-permute-start | bytes 1572872 | tf_op jit(solution)/shard_map/ppermute | solution.py:25
  131.3 5.9 %collective-permute-done.14 = bf16[4,32,16,128]{3,2,1,0:T(8,128)(2,1)S(1)} collective-permute-done((bf16[4,32,16,128]{3,2,1,0:T(8,128)(2,1)}, bf16[4,32,16,128]{3,2,1,0:T(8,128)(2,1)S(1)}, u32[]{:S(2)}, u32[]{:S(2)}) %collective-permute-start.14) | collective-permute-done | bytes 524320 | tf_op jit(solution)/shard_map/ppermute | solution.py:25
  137.4 9.4 %collective-permute-done.18 = bf16[4,32,16,128]{3,2,1,0:T(8,128)(2,1)} collective-permute-done((bf16[4,32,16,128]{3,2,1,0:T(8,128)(2,1)}, bf16[4,32,16,128]{3,2,1,0:T(8,128)(2,1)}, u32[]{:S(2)}, u32[]{:S(2)}) %collective-permute-start.18) | collective-permute-done | bytes 524320 | tf_op jit(solution)/shard_map/ppermute | solution.py:25
  146.8 1.9 %constant_dynamic-update-slice_fusion.3 = bf16[16,32,16,128]{3,2,1,0:T(8,128)(2,1)} fusion(bf16[16,32,16,128]{3,2,1,0:T(8,128)(2,1)} %copy-done.4, bf16[4,32,16,128]{3,2,1,0:T(8,128)(2,1)} %collective-permute-done.18, s32[]{:T(128)S(6)} %select_n.33), kind=kLoop, calls=%fused_computation.24 | loop fusion | bytes 1048580 | tf_op jit(solution)/shard_map/dynamic_update_slice | solution.py:201
  (60 shorter events, 5.1 us)
Async XLA Ops:
  0.0 20.6 %copy-start = (bf16[3,3,256,256]{3,2,1,0:T(8,128)(2,1)S(1)}, bf16[3,3,256,256]{3,2,1,0:T(8,128)(2,1)}, u32[]{:S(2)}) copy-start(bf16[3,3,256,256]{3,2,1,0:T(8,128)(2,1)} %param.6) | copy-start | bytes 3538948
  2.5 50.7 %collective-permute-start = (bf16[8,32,16,128]{3,2,1,0:T(8,128)(2,1)}, bf16[8,32,16,128]{3,2,1,0:T(8,128)(2,1)}, u32[]{:S(2)}, u32[]{:S(2)}) collective-permute-start(bf16[8,32,16,128]{3,2,1,0:T(8,128)(2,1)} %constant_dynamic-slice_fusion.6), channel_id=1, source_target_pairs={{0,1},{1,0},{2,3},{3,2},{4,5},{5,4},{6,7},{7,6},{8,9},{9,8},{10,11... | collective-permute-start | bytes 3145736 | tf_op jit(solution)/shard_map/ppermute | solution.py:25
  7.9 34.5 %collective-permute-start.1 = (bf16[8,6,16,128]{3,2,1,0:T(8,128)(2,1)}, bf16[8,6,16,128]{3,2,1,0:T(8,128)(2,1)}, u32[]{:S(2)}, u32[]{:S(2)}) collective-permute-start(bf16[8,6,16,128]{3,2,1,0:T(8,128)(2,1)} %get-tuple-element.32), channel_id=1, source_target_pairs={{0,32},{32,64},{64,96},{1,33},{33,65},{65,97},{2,34},{34,66},{66,9... | collective-permute-start | bytes 589832 | tf_op jit(solution)/shard_map/ppermute | solution.py:16
  11.4 32.0 %collective-permute-start.3 = (bf16[8,6,16,128]{3,2,1,0:T(8,128)(2,1)}, bf16[8,6,16,128]{3,2,1,0:T(8,128)(2,1)}, u32[]{:S(2)}, u32[]{:S(2)}) collective-permute-start(bf16[8,6,16,128]{3,2,1,0:T(8,128)(2,1)} %get-tuple-element.31), channel_id=1, source_target_pairs={{32,0},{64,32},{96,64},{33,1},{65,33},{97,65},{34,2},{66,34},{98,6... | collective-permute-start | bytes 589832 | tf_op jit(solution)/shard_map/ppermute | solution.py:21
  15.0 18.8 %collective-permute-start.9 = (bf16[16,2,16,128]{3,2,1,0:T(8,128)(2,1)}, bf16[16,2,16,128]{3,2,1,0:T(8,128)(2,1)}, u32[]{:S(2)}, u32[]{:S(2)}) collective-permute-start(bf16[16,2,16,128]{3,2,1,0:T(8,128)(2,1)} %get-tuple-element.28), channel_id=1, source_target_pairs={{0,32},{32,64},{64,96},{1,33},{33,65},{65,97},{2,34},{34,66},{66,9... | collective-permute-start | bytes 393224 | tf_op jit(solution)/shard_map/ppermute | solution.py:16
  18.7 18.3 %collective-permute-start.10 = (bf16[16,2,16,128]{3,2,1,0:T(8,128)(2,1)}, bf16[16,2,16,128]{3,2,1,0:T(8,128)(2,1)}, u32[]{:S(2)}, u32[]{:S(2)}) collective-permute-start(bf16[16,2,16,128]{3,2,1,0:T(8,128)(2,1)} %get-tuple-element.27), channel_id=1, source_target_pairs={{32,0},{64,32},{96,64},{33,1},{65,33},{97,65},{34,2},{66,34},{98,6... | collective-permute-start | bytes 393224 | tf_op jit(solution)/shard_map/ppermute | solution.py:21
  36.9 7.5 %copy-start.6 = (bf16[8,32,4,128]{3,2,1,0:T(4,128)(2,1)S(1)}, bf16[8,32,4,128]{3,2,1,0:T(4,128)(2,1)}, u32[]{:S(2)}) copy-start(bf16[8,32,4,128]{3,2,1,0:T(4,128)(2,1)} %get-tuple-element.30) | copy-start | bytes 786436
  36.9 10.9 %copy-start.5 = (bf16[8,32,4,128]{3,2,1,0:T(4,128)(2,1)S(1)}, bf16[8,32,4,128]{3,2,1,0:T(4,128)(2,1)}, u32[]{:S(2)}) copy-start(bf16[8,32,4,128]{3,2,1,0:T(4,128)(2,1)} %get-tuple-element.29) | copy-start | bytes 786436
  37.9 11.0 %copy-start.7 = (bf16[16,36,16,128]{3,2,1,0:T(8,128)(2,1)}, bf16[16,36,16,128]{3,2,1,0:T(8,128)(2,1)S(1)}, u32[]{:S(2)}) copy-start(bf16[16,36,16,128]{3,2,1,0:T(8,128)(2,1)S(1)} %constant_dynamic-update-slice_fusion.gate_own) | copy-start | bytes 7077892
  39.5 61.3 %collective-permute-start.15 = (bf16[4,36,16,128]{3,2,1,0:T(8,128)(2,1)}, bf16[4,36,16,128]{3,2,1,0:T(8,128)(2,1)}, u32[]{:S(2)}, u32[]{:S(2)}) collective-permute-start(bf16[4,36,16,128]{3,2,1,0:T(8,128)(2,1)} %get-tuple-element.25), channel_id=1, source_target_pairs={{0,1},{1,0},{2,3},{3,2},{4,5},{5,4},{6,7},{7,6},{8,9},{9,8},{10,11... | collective-permute-start | bytes 1769480 | tf_op jit(solution)/shard_map/ppermute | solution.py:25
  39.5 44.3 %collective-permute-start.11 = (bf16[4,36,16,128]{3,2,1,0:T(8,128)(2,1)}, bf16[4,36,16,128]{3,2,1,0:T(8,128)(2,1)}, u32[]{:S(2)}, u32[]{:S(2)}) collective-permute-start(bf16[4,36,16,128]{3,2,1,0:T(8,128)(2,1)} %get-tuple-element.26), channel_id=1, source_target_pairs={{0,1},{1,0},{2,3},{3,2},{4,5},{5,4},{6,7},{7,6},{8,9},{9,8},{10,11... | collective-permute-start | bytes 1769480 | tf_op jit(solution)/shard_map/ppermute | solution.py:25
  44.7 30.3 %collective-permute-start.5 = (bf16[8,44,4,128]{3,2,1,0:T(4,128)(2,1)S(1)}, bf16[8,44,4,128]{3,2,1,0:T(4,128)(2,1)S(1)}, u32[]{:S(2)}, u32[]{:S(2)}) collective-permute-start(bf16[8,44,4,128]{3,2,1,0:T(4,128)(2,1)S(1)} %pad_maximum_fusion.2), channel_id=1, source_target_pairs={{0,2},{2,4},{4,6},{6,8},{8,10},{10,12},{12,14},{14,16},{16,18},{18... | collective-permute-start | bytes 1081352 | tf_op jit(solution)/shard_map/ppermute | solution.py:16
  47.8 31.0 %copy-start.1 = (bf16[3,3,256,256]{3,2,1,0:T(8,128)(2,1)S(1)}, bf16[3,3,256,256]{3,2,1,0:T(8,128)(2,1)}, u32[]{:S(2)}) copy-start(bf16[3,3,256,256]{3,2,1,0:T(8,128)(2,1)} %param.7) | copy-start | bytes 3538948
  47.8 31.0 %copy-start.3 = (bf16[3,3,256,128]{3,2,1,0:T(8,128)(2,1)S(1)}, bf16[3,3,256,128]{3,2,1,0:T(8,128)(2,1)}, u32[]{:S(2)}) copy-start(bf16[3,3,256,128]{3,2,1,0:T(8,128)(2,1)} %fusion.4) | copy-start | bytes 1769476
  48.9 34.9 %collective-permute-start.7 = (bf16[8,44,4,128]{3,2,1,0:T(4,128)(2,1)}, bf16[8,44,4,128]{3,2,1,0:T(4,128)(2,1)}, u32[]{:S(2)}, u32[]{:S(2)}) collective-permute-start(bf16[8,44,4,128]{3,2,1,0:T(4,128)(2,1)} %pad_maximum_fusion.4), channel_id=1, source_target_pairs={{2,0},{4,2},{6,4},{8,6},{10,8},{12,10},{14,12},{16,14},{18,16},{20... | collective-permute-start | bytes 1081352 | tf_op jit(solution)/shard_map/ppermute | solution.py:21
  54.2 8.1 %collective-permute-start.2 = (bf16[8,6,16,128]{3,2,1,0:T(8,128)(2,1)S(1)}, bf16[8,6,16,128]{3,2,1,0:T(8,128)(2,1)S(1)}, u32[]{:S(2)}, u32[]{:S(2)}) collective-permute-start(bf16[8,6,16,128]{3,2,1,0:T(8,128)(2,1)S(1)} %get-tuple-element.40), channel_id=1, source_target_pairs={{0,32},{32,64},{64,96},{1,33},{33,65},{65,97},{2,34},{34,66},{66,9... | collective-permute-start | bytes 589832 | tf_op jit(solution)/shard_map/ppermute | solution.py:16
  62.3 12.6 %copy-start.10 = (bf16[8,6,16,128]{3,2,1,0:T(8,128)(2,1)}, bf16[8,6,16,128]{3,2,1,0:T(8,128)(2,1)S(1)}, u32[]{:S(2)}) copy-start(bf16[8,6,16,128]{3,2,1,0:T(8,128)(2,1)S(1)} %collective-permute-done.2.top_other) | copy-start | bytes 589828
  62.3 7.7 %collective-permute-start.4 = (bf16[8,6,16,128]{3,2,1,0:T(8,128)(2,1)S(1)}, bf16[8,6,16,128]{3,2,1,0:T(8,128)(2,1)S(1)}, u32[]{:S(2)}, u32[]{:S(2)}) collective-permute-start(bf16[8,6,16,128]{3,2,1,0:T(8,128)(2,1)S(1)} %get-tuple-element.39), channel_id=1, source_target_pairs={{32,0},{64,32},{96,64},{33,1},{65,33},{97,65},{34,2},{66,34},{98,6... | collective-permute-start | bytes 589832 | tf_op jit(solution)/shard_map/ppermute | solution.py:21
  70.0 0.7 copy-start.11
  71.8 12.0 %collective-permute-start.8 = (bf16[8,44,4,128]{3,2,1,0:T(4,128)(2,1)}, bf16[8,44,4,128]{3,2,1,0:T(4,128)(2,1)}, u32[]{:S(2)}, u32[]{:S(2)}) collective-permute-start(bf16[8,44,4,128]{3,2,1,0:T(4,128)(2,1)} %pad_maximum_fusion.5), channel_id=1, source_target_pairs={{2,0},{4,2},{6,4},{8,6},{10,8},{12,10},{14,12},{16,14},{18,16},{20... | collective-permute-start | bytes 1081352 | tf_op jit(solution)/shard_map/ppermute | solution.py:21
  74.9 0.7 copy-start.12
  75.7 10.8 %collective-permute-start.6 = (bf16[8,44,4,128]{3,2,1,0:T(4,128)(2,1)}, bf16[8,44,4,128]{3,2,1,0:T(4,128)(2,1)}, u32[]{:S(2)}, u32[]{:S(2)}) collective-permute-start(bf16[8,44,4,128]{3,2,1,0:T(4,128)(2,1)} %pad_maximum_fusion.3), channel_id=1, source_target_pairs={{0,2},{2,4},{4,6},{6,8},{8,10},{10,12},{12,14},{14,16},{16,18},{18... | collective-permute-start | bytes 1081352 | tf_op jit(solution)/shard_map/ppermute | solution.py:16
  80.4 1.7 %copy-start.2 = (bf16[3,3,256,256]{3,2,1,0:T(8,128)(2,1)S(1)}, bf16[3,3,256,256]{3,2,1,0:T(8,128)(2,1)}, u32[]{:S(2)}) copy-start(bf16[3,3,256,256]{3,2,1,0:T(8,128)(2,1)} %get-tuple-element.49) | copy-start | bytes 3538948
  93.4 21.7 %collective-permute-start.12 = (bf16[4,36,2,256]{3,2,1,0:T(2,128)(2,1)}, bf16[4,36,2,256]{3,2,1,0:T(2,128)(2,1)S(1)}, u32[]{:S(2)}, u32[]{:S(2)}) collective-permute-start(bf16[4,36,2,256]{3,2,1,0:T(2,128)(2,1)} %get-tuple-element.16), channel_id=1, source_target_pairs={{0,2},{2,4},{4,6},{6,8},{8,10},{10,12},{12,14},{14,16},{16,18},{18... | collective-permute-start | bytes 442376 | tf_op jit(solution)/shard_map/ppermute | solution.py:16
  95.3 19.8 %collective-permute-start.13 = (bf16[4,36,2,256]{3,2,1,0:T(2,128)(2,1)}, bf16[4,36,2,256]{3,2,1,0:T(2,128)(2,1)S(1)}, u32[]{:S(2)}, u32[]{:S(2)}) collective-permute-start(bf16[4,36,2,256]{3,2,1,0:T(2,128)(2,1)} %get-tuple-element.17), channel_id=1, source_target_pairs={{2,0},{4,2},{6,4},{8,6},{10,8},{12,10},{14,12},{16,14},{18,16},{20... | collective-permute-start | bytes 442376 | tf_op jit(solution)/shard_map/ppermute | solution.py:21
  107.7 14.9 %collective-permute-start.16 = (bf16[4,36,2,256]{3,2,1,0:T(2,128)(2,1)}, bf16[4,36,2,256]{3,2,1,0:T(2,128)(2,1)S(1)}, u32[]{:S(2)}, u32[]{:S(2)}) collective-permute-start(bf16[4,36,2,256]{3,2,1,0:T(2,128)(2,1)} %get-tuple-element.21), channel_id=1, source_target_pairs={{0,2},{2,4},{4,6},{6,8},{8,10},{10,12},{12,14},{14,16},{16,18},{18... | collective-permute-start | bytes 442376 | tf_op jit(solution)/shard_map/ppermute | solution.py:16
  109.6 13.0 %collective-permute-start.17 = (bf16[4,36,2,256]{3,2,1,0:T(2,128)(2,1)}, bf16[4,36,2,256]{3,2,1,0:T(2,128)(2,1)S(1)}, u32[]{:S(2)}, u32[]{:S(2)}) collective-permute-start(bf16[4,36,2,256]{3,2,1,0:T(2,128)(2,1)} %get-tuple-element.22), channel_id=1, source_target_pairs={{2,0},{4,2},{6,4},{8,6},{10,8},{12,10},{14,12},{16,14},{18,16},{20... | collective-permute-start | bytes 442376 | tf_op jit(solution)/shard_map/ppermute | solution.py:21
  115.1 0.7 copy-start.13
  115.1 0.7 copy-start.14
  121.5 15.8 %collective-permute-start.14 = (bf16[4,32,16,128]{3,2,1,0:T(8,128)(2,1)}, bf16[4,32,16,128]{3,2,1,0:T(8,128)(2,1)S(1)}, u32[]{:S(2)}, u32[]{:S(2)}) collective-permute-start(bf16[4,32,16,128]{3,2,1,0:T(8,128)(2,1)} %get-tuple-element.19), channel_id=1, source_target_pairs={{0,1},{1,0},{2,3},{3,2},{4,5},{5,4},{6,7},{7,6},{8,9},{9,8},{10,11... | collective-permute-start | bytes 1572872 | tf_op jit(solution)/shard_map/ppermute | solution.py:25
  122.6 0.7 copy-start.15
  122.6 0.7 copy-start.16
  128.9 2.3 %copy-start.8 = (bf16[4,32,16,128]{3,2,1,0:T(8,128)(2,1)S(1)}, bf16[4,32,16,128]{3,2,1,0:T(8,128)(2,1)}, u32[]{:S(2)}) copy-start(bf16[4,32,16,128]{3,2,1,0:T(8,128)(2,1)} %get-tuple-element.18) | copy-start | bytes 1572868
  128.9 17.8 %collective-permute-start.18 = (bf16[4,32,16,128]{3,2,1,0:T(8,128)(2,1)}, bf16[4,32,16,128]{3,2,1,0:T(8,128)(2,1)}, u32[]{:S(2)}, u32[]{:S(2)}) collective-permute-start(bf16[4,32,16,128]{3,2,1,0:T(8,128)(2,1)} %get-tuple-element.24), channel_id=1, source_target_pairs={{0,1},{1,0},{2,3},{3,2},{4,5},{5,4},{6,7},{7,6},{8,9},{9,8},{10,11... | collective-permute-start | bytes 1572872 | tf_op jit(solution)/shard_map/ppermute | solution.py:25
  130.8 6.5 %copy-start.9 = (bf16[4,32,16,128]{3,2,1,0:T(8,128)(2,1)S(1)}, bf16[4,32,16,128]{3,2,1,0:T(8,128)(2,1)}, u32[]{:S(2)}) copy-start(bf16[4,32,16,128]{3,2,1,0:T(8,128)(2,1)} %get-tuple-element.23) | copy-start | bytes 1572868
  137.4 9.4 %copy-start.4 = (bf16[16,32,16,128]{3,2,1,0:T(8,128)(2,1)}, bf16[16,32,16,128]{3,2,1,0:T(8,128)(2,1)S(1)}, u32[]{:S(2)}) copy-start(bf16[16,32,16,128]{3,2,1,0:T(8,128)(2,1)S(1)} %constant_dynamic-update-slice_fusion.4) | copy-start | bytes 6291460

commit v3 on v1

v3 whole, which is shorter than its diff:
```python
import jax
import jax.numpy as jnp
from jax import lax
from jax.experimental import pallas as pl
from jax.experimental.pallas import tpu as pltpu
from jax.sharding import PartitionSpec as P

PARTS = (2, 3, 3)
FAR = 4
NEAR = 2
SPREAD = FAR + NEAR


def from_before(x, axis):
    count = lax.axis_size(axis)
    return lax.ppermute(x, axis, [(i, i + 1) for i in range(count - 1)])


def from_after(x, axis):
    count = lax.axis_size(axis)
    return lax.ppermute(x, axis, [(i + 1, i) for i in range(count - 1)])


def to_partner(x):
    return lax.ppermute(x, "filt", [(0, 1), (1, 0)])


def relative_weight(weight, part):
    taps = weight.shape[:2]
    channels = weight.shape[2]
    half = channels // 2
    swapped = jnp.roll(weight, (half, half), (2, 3))
    own_first = jnp.where(part == 0, weight, swapped)
    turned = own_first[:, ::-1].transpose(0, 1, 3, 2)
    return turned.reshape(taps[0], taps[1] * channels, channels)


def fill_shifted(shifted, middle, left, right, spacing):
    _, cols, channels = middle.shape
    shifted[:, spacing:, :channels] = middle[:, : cols - spacing]
    shifted[:, :spacing, :channels] = left
    shifted[:, :, channels : 2 * channels] = middle
    shifted[:, : cols - spacing, 2 * channels :] = middle[:, spacing:]
    shifted[:, cols - spacing :, 2 * channels :] = right


def taps_sum(shifted, weight_ref, spacing, rows):
    cols, depth = shifted.shape[1:]
    total = None
    for tap_row in range(3):
        top = spacing * (2 - tap_row)
        piece = shifted[top : top + rows].reshape(rows * cols, depth)
        term = jnp.dot(piece, weight_ref[tap_row], preferred_element_type=jnp.float32)
        total = term if total is None else total + term
    return total


def first_kernel(part_ref, own, other_a, other_b, top, bottom, left, right, gate_own, gate_other, weight, grad_h, edge_left, edge_right, whole, shifted):
    rows = own.shape[1]
    half = own.shape[3]
    early = pl.program_id(0) < pl.num_programs(0) // 2
    whole[:SPREAD] = top[0]
    whole[SPREAD : SPREAD + rows, :, :half] = own[0]

    @pl.when(early)
    def _():
        whole[SPREAD : SPREAD + rows, :, half:] = other_a[0]

    @pl.when(jnp.logical_not(early))
    def _():
        whole[SPREAD : SPREAD + rows, :, half:] = other_b[0]

    whole[SPREAD + rows :] = bottom[0]
    fill_shifted(shifted, whole[...], left[0], right[0], FAR)
    out_rows = rows + 2 * NEAR
    total = taps_sum(shifted, weight, FAR, out_rows).reshape(out_rows, own.shape[2], 2 * half)
    kept_own = jnp.where(gate_own[0].astype(jnp.float32) > 0, total[:, :, :half], 0.0).astype(jnp.bfloat16)
    kept_other = jnp.where(gate_other[0].astype(jnp.float32) > 0, total[:, :, half:], 0.0).astype(jnp.bfloat16)
    grad_h[0, :, :, :half] = kept_own
    grad_h[0, :, :, half:] = kept_other
    cols = own.shape[2]
    edge_left[0] = grad_h[0, :, :NEAR]
    edge_right[0] = grad_h[0, :, cols - NEAR :]


def second_kernel(grad_h, left, right, weight, kept, sent, shifted):
    fill_shifted(shifted, grad_h[0], left[0], right[0], NEAR)
    rows, cols, half = kept.shape[1:]
    total = taps_sum(shifted, weight, NEAR, rows).reshape(rows, cols, 2 * half).astype(jnp.bfloat16)
    kept[0] = total[:, :, :half]
    sent[0] = total[:, :, half:]


def on_device(grad_out, pre_act, weight_one, weight_two):
    batch, rows, cols, half = grad_out.shape
    mine = batch // 2
    part = lax.axis_index("filt")
    own_at = part * mine
    other_at = (1 - part) * mine
    channels = 2 * half

    few = mine // 2
    other_a = to_partner(lax.dynamic_slice_in_dim(grad_out, other_at, few, 0))
    gate_top = from_before(pre_act[:, rows - NEAR :], "row")
    gate_bottom = from_after(pre_act[:, :NEAR], "row")
    other_b = to_partner(lax.dynamic_slice_in_dim(grad_out, other_at + few, few, 0))
    gate = jnp.concatenate([gate_top, pre_act, gate_bottom], axis=1)
    own = lax.dynamic_slice_in_dim(grad_out, own_at, mine, 0)
    first_weight = relative_weight(weight_two, part)
    second_weight = relative_weight(weight_one, part)
    both = jnp.concatenate([own, jnp.concatenate([other_a, other_b], axis=0)], axis=3)
    top = from_before(both[:, rows - SPREAD :], "row")
    bottom = from_after(both[:, :SPREAD], "row")
    gate_other = to_partner(lax.dynamic_slice_in_dim(gate, other_at, mine, 0))
    last = [piece[:, :, cols - FAR :] for piece in (top, both, bottom)]
    left = from_before(jnp.concatenate(last, axis=1), "col")
    head = [piece[:, :, :FAR] for piece in (top, both, bottom)]
    right = from_after(jnp.concatenate(head, axis=1), "col")

    tall_rows = rows + 2 * SPREAD
    gate_rows = rows + 2 * NEAR
    where = jnp.reshape(own_at, (1,)).astype(jnp.int32)

    def by_own(i, ref):
        return (ref[0] + i, 0, 0, 0)

    def by_mine(i, *refs):
        return (i, 0, 0, 0)

    def whole_weight(i, *refs):
        return (0, 0, 0)

    grad_h, edge_left, edge_right = pl.pallas_call(
        first_kernel,
        out_shape=(
            jax.ShapeDtypeStruct((mine, gate_rows, cols, channels), jnp.bfloat16),
            jax.ShapeDtypeStruct((mine, gate_rows, NEAR, channels), jnp.bfloat16),
            jax.ShapeDtypeStruct((mine, gate_rows, NEAR, channels), jnp.bfloat16),
        ),
        grid_spec=pltpu.PrefetchScalarGridSpec(
            num_scalar_prefetch=1,
            grid=(mine,),
            in_specs=[
                pl.BlockSpec((1, rows, cols, half), by_own),
                pl.BlockSpec((1, rows, cols, half), lambda i, ref: (jnp.minimum(i, few - 1), 0, 0, 0)),
                pl.BlockSpec((1, rows, cols, half), lambda i, ref: (jnp.maximum(i - few, 0), 0, 0, 0)),
                pl.BlockSpec((1, SPREAD, cols, channels), by_mine),
                pl.BlockSpec((1, SPREAD, cols, channels), by_mine),
                pl.BlockSpec((1, tall_rows, FAR, channels), by_mine),
                pl.BlockSpec((1, tall_rows, FAR, channels), by_mine),
                pl.BlockSpec((1, gate_rows, cols, half), by_own),
                pl.BlockSpec((1, gate_rows, cols, half), by_mine),
                pl.BlockSpec((3, 3 * channels, channels), whole_weight),
            ],
            out_specs=(
                pl.BlockSpec((1, gate_rows, cols, channels), by_mine),
                pl.BlockSpec((1, gate_rows, NEAR, channels), by_mine),
                pl.BlockSpec((1, gate_rows, NEAR, channels), by_mine),
            ),
            scratch_shapes=[
                pltpu.VMEM((tall_rows, cols, channels), jnp.bfloat16),
                pltpu.VMEM((tall_rows, cols, 3 * channels), jnp.bfloat16),
            ],
        ),
        cost_estimate=pl.CostEstimate(flops=mine * 2 * gate_rows * cols * 9 * channels * channels, bytes_accessed=mine * 2**20, transcendentals=0),
        name="first",
    )(where, grad_out, other_a, other_b, top, bottom, left, right, gate, gate_other, first_weight)
    h_left = from_before(edge_right, "col")
    h_right = from_after(edge_left, "col")

    result = jnp.zeros_like(grad_out)
    start = 0
    for size in PARTS:

        def by_part(i, start=start):
            return (start + i, 0, 0, 0)

        def by_chunk(i):
            return (i, 0, 0, 0)

        kept, sent = pl.pallas_call(
            second_kernel,
            out_shape=(
                jax.ShapeDtypeStruct((size, rows, cols, half), jnp.bfloat16),
                jax.ShapeDtypeStruct((size, rows, cols, half), jnp.bfloat16),
            ),
            grid=(size,),
            in_specs=[
                pl.BlockSpec((1, gate_rows, cols, channels), by_part),
                pl.BlockSpec((1, gate_rows, NEAR, channels), by_part),
                pl.BlockSpec((1, gate_rows, NEAR, channels), by_part),
                pl.BlockSpec((3, 3 * channels, channels), whole_weight),
            ],
            out_specs=(
                pl.BlockSpec((1, rows, cols, half), by_chunk),
                pl.BlockSpec((1, rows, cols, half), by_chunk),
            ),
            scratch_shapes=[pltpu.VMEM((gate_rows, cols, 3 * channels), jnp.bfloat16)],
            cost_estimate=pl.CostEstimate(flops=size * 2 * rows * cols * 9 * channels * channels, bytes_accessed=size * 2**20, transcendentals=0),
            name="second",
        )(grad_h, h_left, h_right, second_weight)
        back = to_partner(sent)
        result = lax.dynamic_update_slice_in_dim(result, kept, own_at + start, 0)
        result = lax.dynamic_update_slice_in_dim(result, back, other_at + start, 0)
        start += size
    return result


def solution(mesh):
    placed = (P(None, "row", "col", "filt"), P(None, "row", "col", "filt"), P(), P())
    return jax.shard_map(
        on_device,
        mesh=mesh,
        in_specs=placed,
        out_specs=P(None, "row", "col", "filt"),
        check_vma=False,
    )
```

time: 140 us -> 133 us (0.950)
  waiting for transfers between devices: 52.4 us -> 44.2 us
  starting transfers between devices: 43.9 us -> 36.6 us
  other arithmetic: 2.58 us -> 8 us
  local copies, waits for them, and re-layouts: 14.6 us -> 17.4 us
    ppermute x5 -> x6, waiting for transfers between devices: 45.8 us -> 13.5 us  [to_partner(): return lax.ppermute(x, 'filt', [(0, 1), (1, 0)])]
    ppermute x5 -> x4, waiting for transfers between devices: 2.19 us -> 20.6 us  [from_before(): return lax.ppermute(x, axis, [(i, i + 1) for i in range(count - 1)])]
    ppermute x5 -> x4, waiting for transfers between devices: 4.4 us -> 10.1 us  [from_after(): return lax.ppermute(x, axis, [(i + 1, i) for i in range(count - 1)])]
    ppermute x5 -> x4, starting transfers between devices: 19.1 us -> 14 us  [from_after(): return lax.ppermute(x, axis, [(i + 1, i) for i in range(count - 1)])]
    concatenate x2 -> x1, other arithmetic: 1.74 us -> 4.06 us  [on_device(): right = from_after(jnp.concatenate(head, axis=1), 'col')]
    ppermute x5 -> x4, starting transfers between devices: 14.7 us -> 13.4 us  [from_before(): return lax.ppermute(x, axis, [(i, i + 1) for i in range(count - 1)])]
    slice x2 -> x3, local copies, waits for them, and re-layouts: 2.96 us -> 1.84 us  [the longest x1 1.68 us: on_device(): gate_bottom = from_after(pre_act[:, :NEAR], 'row')]
    ppermute x5 -> x6, starting transfers between devices: 10.2 us -> 9.15 us  [to_partner(): return lax.ppermute(x, 'filt', [(0, 1), (1, 0)])]
  transfers between devices with their start and end apart: 15 -> 14, of which waited for: 6 -> 8; matrix products, arithmetic and copies ran while one was open for 6% -> 15% of each run, Pallas kernels for 18% -> 7%
where the time goes in v3:
time: 133 us; the launch traced here: 132 us
  waiting for transfers between devices  44.2 us (33%)
  starting transfers between devices  36.6 us (28%)
  Pallas kernels  25 us (19%)
  local copies, waits for them, and re-layouts  17.4 us (13%)
  other arithmetic  8 us (6%)
    ppermute x4, waiting for transfers between devices, from_before(): return lax.ppermute(x, axis, [(i, i + 1) for i in range(count - 1)])  20.6 us
    ppermute x4, starting transfers between devices, from_after(): return lax.ppermute(x, axis, [(i + 1, i) for i in range(count - 1)])  14 us
    ppermute x6, waiting for transfers between devices, to_partner(): return lax.ppermute(x, 'filt', [(0, 1), (1, 0)])  13.5 us
    ppermute x4, starting transfers between devices, from_before(): return lax.ppermute(x, axis, [(i, i + 1) for i in range(count - 1)])  13.4 us
    pallas_call x3, Pallas kernels, on_device(): pl.pallas_call(second_kernel, out_shape=(jax.ShapeDtypeStruct((size, rows...  13.3 us
    pallas_call x1, Pallas kernels, on_device(): pl.pallas_call(first_kernel, out_shape=(jax.ShapeDtypeStruct((mine, gate_...  11.7 us
    ppermute x4, waiting for transfers between devices, from_after(): return lax.ppermute(x, axis, [(i + 1, i) for i in range(count - 1)])  10.1 us
    ppermute x6, starting transfers between devices, to_partner(): return lax.ppermute(x, 'filt', [(0, 1), (1, 0)])  9.15 us
  transfers between devices with their start and end apart: 14, of which 8 were waited for; matrix products, arithmetic and copies ran while one was open for 15% of the time, Pallas kernels for 7%

profile of v3, /device:TPU:9, one launch (start us, length us, event | category | flops | bytes accessed | tf_op | source)
XLA Modules:
  0.0 131.6 jit_solution(7606323197061981724)
XLA Ops:
  0.0 2.4 %constant_dynamic-slice_fusion.2 = (bf16[4,32,16,128]{3,2,1,0:T(8,128)(2,1)}, bf16[4,32,16,128]{3,2,1,0:T(8,128)(2,1)}) fusion(bf16[16,32,16,128]{3,2,1,0:T(8,128)(2,1)} %own.1, s32[]{:T(128)S(6)} %select_n.37, s32[]{:T(128)S(6)} %select_n.36), kind=kLoop, calls=%fused_computation.35 | loop fusion | bytes 2097160 | tf_op jit(solution)/shard_map/dynamic_slice | solution.py:106
  2.4 3.6 %collective-permute-start = (bf16[4,32,16,128]{3,2,1,0:T(8,128)(2,1)}, bf16[4,32,16,128]{3,2,1,0:T(8,128)(2,1)}, u32[]{:S(2)}, u32[]{:S(2)}) collective-permute-start(bf16[4,32,16,128]{3,2,1,0:T(8,128)(2,1)} %get-tuple-element.30), channel_id=1, source_target_pairs={{0,1},{1,0},{2,3},{3,2},{4,5},{5,4},{6,7},{7,6},{8,9},{9,8},{10,11... | collective-permute-start | bytes 1572872 | tf_op jit(solution)/shard_map/ppermute | solution.py:25
  6.0 1.7 %fusion.10 = (bf16[16,2,16,128]{3,2,1,0:T(8,128)(2,1)}, bf16[16,2,16,128]{3,2,1,0:T(8,128)(2,1)}) fusion(bf16[16,32,16,128]{3,2,1,0:T(8,128)(2,1)} %param.5), kind=kLoop, calls=%fused_computation.37 | loop fusion | bytes 524288 | tf_op jit(solution)/shard_map/slice | solution.py:105
  7.7 4.0 %collective-permute-start.6 = (bf16[16,2,16,128]{3,2,1,0:T(8,128)(2,1)}, bf16[16,2,16,128]{3,2,1,0:T(8,128)(2,1)}, u32[]{:S(2)}, u32[]{:S(2)}) collective-permute-start(bf16[16,2,16,128]{3,2,1,0:T(8,128)(2,1)} %get-tuple-element.24), channel_id=1, source_target_pairs={{0,32},{32,64},{64,96},{1,33},{33,65},{65,97},{2,34},{34,66},{66,9... | collective-permute-start | bytes 393224 | tf_op jit(solution)/shard_map/ppermute | solution.py:16
  11.7 1.9 %collective-permute-start.7 = (bf16[16,2,16,128]{3,2,1,0:T(8,128)(2,1)}, bf16[16,2,16,128]{3,2,1,0:T(8,128)(2,1)}, u32[]{:S(2)}, u32[]{:S(2)}) collective-permute-start(bf16[16,2,16,128]{3,2,1,0:T(8,128)(2,1)} %get-tuple-element.23), channel_id=1, source_target_pairs={{32,0},{64,32},{96,64},{33,1},{65,33},{97,65},{34,2},{66,34},{98,6... | collective-permute-start | bytes 393224 | tf_op jit(solution)/shard_map/ppermute | solution.py:21
  13.7 0.1 fusion.11
  13.8 1.5 %fusion.12 = (bf16[3,3,128,256]{3,2,1,0:T(8,128)(2,1)S(1)}, bf16[3,3,128,256]{3,2,1,0:T(8,128)(2,1)S(1)}) fusion(bf16[3,3,256,256]{3,2,1,0:T(8,128)(2,1)} %param.7), kind=kLoop, calls=%fused_computation.39 | loop fusion | bytes 2359296 | tf_op jit(solution)/shard_map/jit(_roll_static)/slice | solution.py:32
  15.3 0.5 copy-done.6
  15.8 0.2 constant_dynamic-slice_fusion.1
  15.9 14.8 %collective-permute-done.6 = bf16[16,2,16,128]{3,2,1,0:T(8,128)(2,1)} collective-permute-done((bf16[16,2,16,128]{3,2,1,0:T(8,128)(2,1)}, bf16[16,2,16,128]{3,2,1,0:T(8,128)(2,1)}, u32[]{:S(2)}, u32[]{:S(2)}) %collective-permute-start.6) | collective-permute-done | bytes 131104 | tf_op jit(solution)/shard_map/ppermute | solution.py:16
  30.7 0.9 constant_dynamic-update-slice_fusion.2
  31.7 1.3 %pad_maximum_fusion.6 = (bf16[8,6,16,256]{3,2,1,0:T(8,128)(2,1)S(1)}, bf16[8,6,16,256]{3,2,1,0:T(8,128)(2,1)S(1)}) fusion(bf16[8,32,16,128]{3,2,1,0:T(8,128)(2,1)S(1)} %constant_dynamic-slice_fusion.1, bf16[4,32,16,128]{3,2,1,0:T(8,128)(2,1)} %collective-permute-done.1.other_b, bf16[4,32,16,128]{3,2,1,0:T(8,128)(2,1)} %collective-permute-done.other_a), kind=kLoop, calls=%fused_computation.22 | loop fusion | flops 2359296 | bytes 2883584 | tf_op jit(solution)/shard_map/slice | solution.py:113
  33.0 4.4 %collective-permute-start.2 = (bf16[8,6,16,256]{3,2,1,0:T(8,128)(2,1)S(1)}, bf16[8,6,16,256]{3,2,1,0:T(8,128)(2,1)S(1)}, u32[]{:S(2)}, u32[]{:S(2)}) collective-permute-start(bf16[8,6,16,256]{3,2,1,0:T(8,128)(2,1)S(1)} %get-tuple-element.28), channel_id=1, source_target_pairs={{0,32},{32,64},{64,96},{1,33},{33,65},{65,97},{2,34},{34,66},{66,9... | collective-permute-start | bytes 1179656 | tf_op jit(solution)/shard_map/ppermute | solution.py:16
  37.4 0.5 constant_dynamic-update-slice_fusion.1
  37.9 1.9 %collective-permute-start.3 = (bf16[8,6,16,256]{3,2,1,0:T(8,128)(2,1)S(1)}, bf16[8,6,16,256]{3,2,1,0:T(8,128)(2,1)S(1)}, u32[]{:S(2)}, u32[]{:S(2)}) collective-permute-start(bf16[8,6,16,256]{3,2,1,0:T(8,128)(2,1)S(1)} %get-tuple-element.27), channel_id=1, source_target_pairs={{32,0},{64,32},{96,64},{33,1},{65,33},{97,65},{34,2},{66,34},{98,6... | collective-permute-start | bytes 1179656 | tf_op jit(solution)/shard_map/ppermute | solution.py:21
  39.9 0.9 constant_dynamic-update-slice_fusion.gate_own
  40.8 1.4 %constant_dynamic-slice_fusion = bf16[8,36,16,128]{3,2,1,0:T(8,128)(2,1)} fusion(bf16[16,36,16,128]{3,2,1,0:T(8,128)(2,1)S(1)} %constant_dynamic-update-slice_fusion.gate_own, s32[]{:T(128)S(6)} %select_n.36), kind=kLoop, calls=%fused_computation.33 | loop fusion | bytes 2359300 | tf_op jit(solution)/shard_map/dynamic_slice | solution.py:114
  42.2 0.5 collective-permute-start.8
  42.7 8.2 %collective-permute-done.3.bottom = bf16[8,6,16,256]{3,2,1,0:T(8,128)(2,1)S(1)} collective-permute-done((bf16[8,6,16,256]{3,2,1,0:T(8,128)(2,1)S(1)}, bf16[8,6,16,256]{3,2,1,0:T(8,128)(2,1)S(1)}, u32[]{:S(2)}, u32[]{:S(2)}) %collective-permute-start.3) | collective-permute-done | bytes 393248 | tf_op jit(solution)/shard_map/ppermute | solution.py:21
  51.0 4.1 %fusion.5 = (bf16[8,44,4,256]{3,2,1,0:T(4,128)(2,1)}, bf16[8,44,4,256]{3,2,1,0:T(4,128)(2,1)}) fusion(bf16[8,32,16,128]{3,2,1,0:T(8,128)(2,1)S(1)} %constant_dynamic-slice_fusion.1, bf16[4,32,16,128]{3,2,1,0:T(8,128)(2,1)} %collective-permute-done.1.other_b, bf16[4,32,16,128]{3,2,1,0:T(8,128)(2,1)} %collective-permute-done.other_a, ...), kind=kLoop, calls=%fused_computation.14 | loop fusion | flops 7208960 | bytes 3932160 | tf_op jit(solution)/shard_map/concatenate | solution.py:118
  55.1 3.1 %collective-permute-start.4 = (bf16[8,44,4,256]{3,2,1,0:T(4,128)(2,1)}, bf16[8,44,4,256]{3,2,1,0:T(4,128)(2,1)}, u32[]{:S(2)}, u32[]{:S(2)}) collective-permute-start(bf16[8,44,4,256]{3,2,1,0:T(4,128)(2,1)} %get-tuple-element.26), channel_id=1, source_target_pairs={{0,2},{2,4},{4,6},{6,8},{8,10},{10,12},{12,14},{14,16},{16,18},{18... | collective-permute-start | bytes 2162696 | tf_op jit(solution)/shard_map/ppermute | solution.py:16
  58.2 4.3 %collective-permute-start.5 = (bf16[8,44,4,256]{3,2,1,0:T(4,128)(2,1)}, bf16[8,44,4,256]{3,2,1,0:T(4,128)(2,1)}, u32[]{:S(2)}, u32[]{:S(2)}) collective-permute-start(bf16[8,44,4,256]{3,2,1,0:T(4,128)(2,1)} %get-tuple-element.25), channel_id=1, source_target_pairs={{2,0},{4,2},{6,4},{8,6},{10,8},{12,10},{14,12},{16,14},{18,16},{20... | collective-permute-start | bytes 2162696 | tf_op jit(solution)/shard_map/ppermute | solution.py:21
  62.5 0.9 fusion.8
  63.4 0.1 fusion.9
  63.5 1.2 copy-done.1
  64.7 0.1 copy-done.4
  64.9 1.6 %fusion.1 = (bf16[3,3,256,256]{3,2,1,0:T(8,128)(2,1)}, bf16[3,3,256,256]{3,2,1,0:T(8,128)(2,1)S(1)}) fusion(bf16[3,3,256,256]{3,2,1,0:T(8,128)(2,1)S(1)} %copy-done, bf16[3,3,128,256]{3,2,1,0:T(8,128)(2,1)S(1)} %get-tuple-element.32, bf16[3,3,128,256]{3,2,1,0:T(8,128)(2,1)S(1)} %get-tuple-element.31, bf16[3,3,256,128]{3,2,1,0:T(8,128)(2,1)S(1)} %copy-done.4, ...), kind=kLoop, calls=%fused_computation.2 | loop fusion | flops 8257536 | bytes 8257537 | tf_op jit(solution)/shard_map/jit(_where)/select_n | solution.py:33
  66.6 1.6 %copy.5 = bf16[3,3,256,256]{3,2,1,0:T(8,128)(2,1)} copy(bf16[3,3,256,256]{2,3,1,0:T(8,128)(2,1)S(1)} %reverse_bitcast_fusion.1) | data formatting | bytes 2359296 | tf_op jit(solution)/shard_map/transpose | solution.py:34
  68.1 1.4 %collective-permute-done.8.gate_other = bf16[8,36,16,128]{3,2,1,0:T(8,128)(2,1)} collective-permute-done((bf16[8,36,16,128]{3,2,1,0:T(8,128)(2,1)}, bf16[8,36,16,128]{3,2,1,0:T(8,128)(2,1)}, u32[]{:S(2)}, u32[]{:S(2)}) %collective-permute-start.8) | collective-permute-done | bytes 1179680 | tf_op jit(solution)/shard_map/ppermute | solution.py:25
  69.6 1.5 %collective-permute-done.5.right = bf16[8,44,4,256]{3,2,1,0:T(4,128)(2,1)} collective-permute-done((bf16[8,44,4,256]{3,2,1,0:T(4,128)(2,1)}, bf16[8,44,4,256]{3,2,1,0:T(4,128)(2,1)}, u32[]{:S(2)}, u32[]{:S(2)}) %collective-permute-start.5) | collective-permute-done | bytes 720928 | tf_op jit(solution)/shard_map/ppermute | solution.py:21
  71.1 11.7 %first.1 = (bf16[8,36,16,256]{3,2,1,0:T(8,128)(2,1)}, bf16[8,36,2,256]{3,2,1,0:T(2,128)(2,1)}, bf16[8,36,2,256]{3,2,1,0:T(2,128)(2,1)}) custom-call(s32[1]{0:T(128)} %bitcast.part_ref, bf16[16,32,16,128]{3,2,1,0:T(8,128)(2,1)} %own.1, bf16[4,32,16,128]{3,2,1,0:T(8,128)(2,1)} %collective-permute-done.other_a, ...), custom_call_target="tpu_custom_call" | custom-call | flops 5435817984 | bytes 8388608 | tf_op jit(solution)/shard_map/first/pallas_call | solution.py:133
  82.7 5.9 %collective-permute-start.10 = (bf16[8,36,2,256]{3,2,1,0:T(2,128)(2,1)}, bf16[8,36,2,256]{3,2,1,0:T(2,128)(2,1)S(1)}, u32[]{:S(2)}, u32[]{:S(2)}) collective-permute-start(bf16[8,36,2,256]{3,2,1,0:T(2,128)(2,1)} %get-tuple-element.16), channel_id=1, source_target_pairs={{2,0},{4,2},{6,4},{8,6},{10,8},{12,10},{14,12},{16,14},{18,16},{20... | collective-permute-start | bytes 884744 | tf_op jit(solution)/shard_map/ppermute | solution.py:21
  88.6 1.9 %collective-permute-start.9 = (bf16[8,36,2,256]{3,2,1,0:T(2,128)(2,1)}, bf16[8,36,2,256]{3,2,1,0:T(2,128)(2,1)S(1)}, u32[]{:S(2)}, u32[]{:S(2)}) collective-permute-start(bf16[8,36,2,256]{3,2,1,0:T(2,128)(2,1)} %get-tuple-element.15), channel_id=1, source_target_pairs={{0,2},{2,4},{4,6},{6,8},{8,10},{10,12},{12,14},{14,16},{16,18},{18... | collective-permute-start | bytes 884744 | tf_op jit(solution)/shard_map/ppermute | solution.py:16
  90.7 1.5 %copy.6 = bf16[3,3,256,256]{3,2,1,0:T(8,128)(2,1)} copy(bf16[3,3,256,256]{2,3,1,0:T(8,128)(2,1)S(1)} %reverse_bitcast_fusion) | data formatting | bytes 2359296 | tf_op jit(solution)/shard_map/transpose | solution.py:34
  92.2 0.4 collective-permute-done.10.right
  92.6 5.8 %collective-permute-done.9.left = bf16[8,36,2,256]{3,2,1,0:T(2,128)(2,1)S(1)} collective-permute-done((bf16[8,36,2,256]{3,2,1,0:T(2,128)(2,1)}, bf16[8,36,2,256]{3,2,1,0:T(2,128)(2,1)S(1)}, u32[]{:S(2)}, u32[]{:S(2)}) %collective-permute-start.9) | collective-permute-done | bytes 294944 | tf_op jit(solution)/shard_map/ppermute | solution.py:16
  98.4 0.7 copy-done.14
  99.2 3.7 %second.3 = (bf16[2,32,16,128]{3,2,1,0:T(8,128)(2,1)}, bf16[2,32,16,128]{3,2,1,0:T(8,128)(2,1)}) custom-call(bf16[8,36,16,256]{3,2,1,0:T(8,128)(2,1)} %get-tuple-element.14.grad_h, bf16[8,36,2,256]{3,2,1,0:T(2,128)(2,1)} %copy-done.14, bf16[8,36,2,256]{3,2,1,0:T(2,128)(2,1)} %copy-done.13, bf16[3,768,256]{2,1,0:T(8,128)(2,1)} %bitcast.7), custom_call_target="tpu_custom_call" | custom-call | flops 1207959552 | bytes 2097152 | tf_op jit(solution)/shard_map/second/pallas_call | solution.py:181
  102.9 2.1 %collective-permute-start.11 = (bf16[2,32,16,128]{3,2,1,0:T(8,128)(2,1)}, bf16[2,32,16,128]{3,2,1,0:T(8,128)(2,1)S(1)}, u32[]{:S(2)}, u32[]{:S(2)}) collective-permute-start(bf16[2,32,16,128]{3,2,1,0:T(8,128)(2,1)} %get-tuple-element.18), channel_id=1, source_target_pairs={{0,1},{1,0},{2,3},{3,2},{4,5},{5,4},{6,7},{7,6},{8,9},{9,8},{10,11... | collective-permute-start | bytes 786440 | tf_op jit(solution)/shard_map/ppermute | solution.py:25
  105.0 4.8 %second.4 = (bf16[3,32,16,128]{3,2,1,0:T(8,128)(2,1)}, bf16[3,32,16,128]{3,2,1,0:T(8,128)(2,1)}) custom-call(bf16[8,36,16,256]{3,2,1,0:T(8,128)(2,1)} %get-tuple-element.14.grad_h, bf16[8,36,2,256]{3,2,1,0:T(2,128)(2,1)} %copy-done.14, bf16[8,36,2,256]{3,2,1,0:T(2,128)(2,1)} %copy-done.13, bf16[3,768,256]{2,1,0:T(8,128)(2,1)} %bitcast.8), custom_call_target="tpu_custom_call" | custom-call | flops 1811939328 | bytes 3145728 | tf_op jit(solution)/shard_map/second/pallas_call | solution.py:181
  109.8 0.9 collective-permute-start.12
  110.7 4.8 %second.5 = (bf16[3,32,16,128]{3,2,1,0:T(8,128)(2,1)}, bf16[3,32,16,128]{3,2,1,0:T(8,128)(2,1)}) custom-call(bf16[8,36,16,256]{3,2,1,0:T(8,128)(2,1)} %get-tuple-element.14.grad_h, bf16[8,36,2,256]{3,2,1,0:T(2,128)(2,1)} %copy-done.14, bf16[8,36,2,256]{3,2,1,0:T(2,128)(2,1)} %copy-done.13, bf16[3,768,256]{2,1,0:T(8,128)(2,1)} %bitcast.9), custom_call_target="tpu_custom_call" | custom-call | flops 1811939328 | bytes 3145728 | tf_op jit(solution)/shard_map/second/pallas_call | solution.py:181
  115.5 2.1 %collective-permute-start.13 = (bf16[3,32,16,128]{3,2,1,0:T(8,128)(2,1)}, bf16[3,32,16,128]{3,2,1,0:T(8,128)(2,1)S(1)}, u32[]{:S(2)}, u32[]{:S(2)}) collective-permute-start(bf16[3,32,16,128]{3,2,1,0:T(8,128)(2,1)} %get-tuple-element.22), channel_id=1, source_target_pairs={{0,1},{1,0},{2,3},{3,2},{4,5},{5,4},{6,7},{7,6},{8,9},{9,8},{10,11... | collective-permute-start | bytes 1179656 | tf_op jit(solution)/shard_map/ppermute | solution.py:25
  117.6 0.4 broadcast_in_dim.3
  118.1 0.5 copy-done.9
  118.6 4.0 %collective-permute-done.12 = bf16[3,32,16,128]{3,2,1,0:T(8,128)(2,1)S(1)} collective-permute-done((bf16[3,32,16,128]{3,2,1,0:T(8,128)(2,1)}, bf16[3,32,16,128]{3,2,1,0:T(8,128)(2,1)S(1)}, u32[]{:S(2)}, u32[]{:S(2)}) %collective-permute-start.12) | collective-permute-done | bytes 393248 | tf_op jit(solution)/shard_map/ppermute | solution.py:25
  122.8 8.0 %collective-permute-done.13 = bf16[3,32,16,128]{3,2,1,0:T(8,128)(2,1)S(1)} collective-permute-done((bf16[3,32,16,128]{3,2,1,0:T(8,128)(2,1)}, bf16[3,32,16,128]{3,2,1,0:T(8,128)(2,1)S(1)}, u32[]{:S(2)}, u32[]{:S(2)}) %collective-permute-start.13) | collective-permute-done | bytes 393248 | tf_op jit(solution)/shard_map/ppermute | solution.py:25
  130.8 0.8 constant_dynamic-update-slice_fusion.3
  (41 shorter events, 0.7 us)
Async XLA Ops:
  0.0 13.7 %copy-start = (bf16[3,3,256,256]{3,2,1,0:T(8,128)(2,1)S(1)}, bf16[3,3,256,256]{3,2,1,0:T(8,128)(2,1)}, u32[]{:S(2)}) copy-start(bf16[3,3,256,256]{3,2,1,0:T(8,128)(2,1)} %param.6) | copy-start | bytes 3538948
  2.4 29.2 %collective-permute-start = (bf16[4,32,16,128]{3,2,1,0:T(8,128)(2,1)}, bf16[4,32,16,128]{3,2,1,0:T(8,128)(2,1)}, u32[]{:S(2)}, u32[]{:S(2)}) collective-permute-start(bf16[4,32,16,128]{3,2,1,0:T(8,128)(2,1)} %get-tuple-element.30), channel_id=1, source_target_pairs={{0,1},{1,0},{2,3},{3,2},{4,5},{5,4},{6,7},{7,6},{8,9},{9,8},{10,11... | collective-permute-start | bytes 1572872 | tf_op jit(solution)/shard_map/ppermute | solution.py:25
  6.0 25.6 %collective-permute-start.1 = (bf16[4,32,16,128]{3,2,1,0:T(8,128)(2,1)}, bf16[4,32,16,128]{3,2,1,0:T(8,128)(2,1)}, u32[]{:S(2)}, u32[]{:S(2)}) collective-permute-start(bf16[4,32,16,128]{3,2,1,0:T(8,128)(2,1)} %get-tuple-element.29), channel_id=1, source_target_pairs={{0,1},{1,0},{2,3},{3,2},{4,5},{5,4},{6,7},{7,6},{8,9},{9,8},{10,11... | collective-permute-start | bytes 1572872 | tf_op jit(solution)/shard_map/ppermute | solution.py:25
  7.7 23.0 %collective-permute-start.6 = (bf16[16,2,16,128]{3,2,1,0:T(8,128)(2,1)}, bf16[16,2,16,128]{3,2,1,0:T(8,128)(2,1)}, u32[]{:S(2)}, u32[]{:S(2)}) collective-permute-start(bf16[16,2,16,128]{3,2,1,0:T(8,128)(2,1)} %get-tuple-element.24), channel_id=1, source_target_pairs={{0,32},{32,64},{64,96},{1,33},{33,65},{65,97},{2,34},{34,66},{66,9... | collective-permute-start | bytes 393224 | tf_op jit(solution)/shard_map/ppermute | solution.py:16
  11.7 28.1 %collective-permute-start.7 = (bf16[16,2,16,128]{3,2,1,0:T(8,128)(2,1)}, bf16[16,2,16,128]{3,2,1,0:T(8,128)(2,1)}, u32[]{:S(2)}, u32[]{:S(2)}) collective-permute-start(bf16[16,2,16,128]{3,2,1,0:T(8,128)(2,1)} %get-tuple-element.23), channel_id=1, source_target_pairs={{32,0},{64,32},{96,64},{33,1},{65,33},{97,65},{34,2},{66,34},{98,6... | collective-permute-start | bytes 393224 | tf_op jit(solution)/shard_map/ppermute | solution.py:21
  13.8 1.9 %copy-start.6 = (bf16[16,32,16,128]{3,2,1,0:T(8,128)(2,1)S(1)}, bf16[16,32,16,128]{3,2,1,0:T(8,128)(2,1)}, u32[]{:S(2)}) copy-start(bf16[16,32,16,128]{3,2,1,0:T(8,128)(2,1)} %own.1) | copy-start | bytes 6291460
  31.6 5.8 %copy-start.3 = (bf16[16,32,16,128]{3,2,1,0:T(8,128)(2,1)S(1)}, bf16[16,32,16,128]{3,2,1,0:T(8,128)(2,1)}, u32[]{:S(2)}) copy-start(bf16[16,32,16,128]{3,2,1,0:T(8,128)(2,1)} %param.5) | copy-start | bytes 6291460
  33.0 9.6 %collective-permute-start.2 = (bf16[8,6,16,256]{3,2,1,0:T(8,128)(2,1)S(1)}, bf16[8,6,16,256]{3,2,1,0:T(8,128)(2,1)S(1)}, u32[]{:S(2)}, u32[]{:S(2)}) collective-permute-start(bf16[8,6,16,256]{3,2,1,0:T(8,128)(2,1)S(1)} %get-tuple-element.28), channel_id=1, source_target_pairs={{0,32},{32,64},{64,96},{1,33},{33,65},{65,97},{2,34},{34,66},{66,9... | collective-permute-start | bytes 1179656 | tf_op jit(solution)/shard_map/ppermute | solution.py:16
  37.9 13.0 %collective-permute-start.3 = (bf16[8,6,16,256]{3,2,1,0:T(8,128)(2,1)S(1)}, bf16[8,6,16,256]{3,2,1,0:T(8,128)(2,1)S(1)}, u32[]{:S(2)}, u32[]{:S(2)}) collective-permute-start(bf16[8,6,16,256]{3,2,1,0:T(8,128)(2,1)S(1)} %get-tuple-element.27), channel_id=1, source_target_pairs={{32,0},{64,32},{96,64},{33,1},{65,33},{97,65},{34,2},{66,34},{98,6... | collective-permute-start | bytes 1179656 | tf_op jit(solution)/shard_map/ppermute | solution.py:21
  40.8 10.3 %copy-start.7 = (bf16[16,36,16,128]{3,2,1,0:T(8,128)(2,1)}, bf16[16,36,16,128]{3,2,1,0:T(8,128)(2,1)S(1)}, u32[]{:S(2)}) copy-start(bf16[16,36,16,128]{3,2,1,0:T(8,128)(2,1)S(1)} %constant_dynamic-update-slice_fusion.gate_own) | copy-start | bytes 7077892
  42.2 27.4 %collective-permute-start.8 = (bf16[8,36,16,128]{3,2,1,0:T(8,128)(2,1)}, bf16[8,36,16,128]{3,2,1,0:T(8,128)(2,1)}, u32[]{:S(2)}, u32[]{:S(2)}) collective-permute-start(bf16[8,36,16,128]{3,2,1,0:T(8,128)(2,1)} %constant_dynamic-slice_fusion), channel_id=1, source_target_pairs={{0,1},{1,0},{2,3},{3,2},{4,5},{5,4},{6,7},{7,6},{8,9},{9,8},{10,11... | collective-permute-start | bytes 3538952 | tf_op jit(solution)/shard_map/ppermute | solution.py:25
  42.6 12.5 %copy-start.11 = (bf16[8,6,16,256]{3,2,1,0:T(8,128)(2,1)}, bf16[8,6,16,256]{3,2,1,0:T(8,128)(2,1)S(1)}, u32[]{:S(2)}) copy-start(bf16[8,6,16,256]{3,2,1,0:T(8,128)(2,1)S(1)} %collective-permute-done.2.top) | copy-start | bytes 1179652
  51.0 4.2 %copy-start.12 = (bf16[8,6,16,256]{3,2,1,0:T(8,128)(2,1)}, bf16[8,6,16,256]{3,2,1,0:T(8,128)(2,1)S(1)}, u32[]{:S(2)}) copy-start(bf16[8,6,16,256]{3,2,1,0:T(8,128)(2,1)S(1)} %collective-permute-done.3.bottom) | copy-start | bytes 1179652
  55.1 14.5 %collective-permute-start.4 = (bf16[8,44,4,256]{3,2,1,0:T(4,128)(2,1)}, bf16[8,44,4,256]{3,2,1,0:T(4,128)(2,1)}, u32[]{:S(2)}, u32[]{:S(2)}) collective-permute-start(bf16[8,44,4,256]{3,2,1,0:T(4,128)(2,1)} %get-tuple-element.26), channel_id=1, source_target_pairs={{0,2},{2,4},{4,6},{6,8},{8,10},{10,12},{12,14},{14,16},{16,18},{18... | collective-permute-start | bytes 2162696 | tf_op jit(solution)/shard_map/ppermute | solution.py:16
  58.2 12.8 %collective-permute-start.5 = (bf16[8,44,4,256]{3,2,1,0:T(4,128)(2,1)}, bf16[8,44,4,256]{3,2,1,0:T(4,128)(2,1)}, u32[]{:S(2)}, u32[]{:S(2)}) collective-permute-start(bf16[8,44,4,256]{3,2,1,0:T(4,128)(2,1)} %get-tuple-element.25), channel_id=1, source_target_pairs={{2,0},{4,2},{6,4},{8,6},{10,8},{12,10},{14,12},{16,14},{18,16},{20... | collective-permute-start | bytes 2162696 | tf_op jit(solution)/shard_map/ppermute | solution.py:21
  63.4 1.3 copy-start.1
  63.4 1.4 %copy-start.4 = (bf16[3,3,256,128]{3,2,1,0:T(8,128)(2,1)S(1)}, bf16[3,3,256,128]{3,2,1,0:T(8,128)(2,1)}, u32[]{:S(2)}) copy-start(bf16[3,3,256,128]{3,2,1,0:T(8,128)(2,1)} %fusion.8) | copy-start | bytes 1769476
  71.1 19.5 %copy-start.2 = (bf16[3,3,256,256]{3,2,1,0:T(8,128)(2,1)S(1)}, bf16[3,3,256,256]{3,2,1,0:T(8,128)(2,1)}, u32[]{:S(2)}) copy-start(bf16[3,3,256,256]{3,2,1,0:T(8,128)(2,1)} %get-tuple-element.39) | copy-start | bytes 3538948
  82.7 9.9 %collective-permute-start.10 = (bf16[8,36,2,256]{3,2,1,0:T(2,128)(2,1)}, bf16[8,36,2,256]{3,2,1,0:T(2,128)(2,1)S(1)}, u32[]{:S(2)}, u32[]{:S(2)}) collective-permute-start(bf16[8,36,2,256]{3,2,1,0:T(2,128)(2,1)} %get-tuple-element.16), channel_id=1, source_target_pairs={{2,0},{4,2},{6,4},{8,6},{10,8},{12,10},{14,12},{16,14},{18,16},{20... | collective-permute-start | bytes 884744 | tf_op jit(solution)/shard_map/ppermute | solution.py:21
  88.6 9.8 %collective-permute-start.9 = (bf16[8,36,2,256]{3,2,1,0:T(2,128)(2,1)}, bf16[8,36,2,256]{3,2,1,0:T(2,128)(2,1)S(1)}, u32[]{:S(2)}, u32[]{:S(2)}) collective-permute-start(bf16[8,36,2,256]{3,2,1,0:T(2,128)(2,1)} %get-tuple-element.15), channel_id=1, source_target_pairs={{0,2},{2,4},{4,6},{6,8},{8,10},{10,12},{12,14},{14,16},{16,18},{18... | collective-permute-start | bytes 884744 | tf_op jit(solution)/shard_map/ppermute | solution.py:16
  92.6 5.8 %copy-start.13 = (bf16[8,36,2,256]{3,2,1,0:T(2,128)(2,1)}, bf16[8,36,2,256]{3,2,1,0:T(2,128)(2,1)S(1)}, u32[]{:S(2)}) copy-start(bf16[8,36,2,256]{3,2,1,0:T(2,128)(2,1)S(1)} %collective-permute-done.10.right) | copy-start | bytes 884740
  98.4 0.7 copy-start.14
  102.9 15.2 %collective-permute-start.11 = (bf16[2,32,16,128]{3,2,1,0:T(8,128)(2,1)}, bf16[2,32,16,128]{3,2,1,0:T(8,128)(2,1)S(1)}, u32[]{:S(2)}, u32[]{:S(2)}) collective-permute-start(bf16[2,32,16,128]{3,2,1,0:T(8,128)(2,1)} %get-tuple-element.18), channel_id=1, source_target_pairs={{0,1},{1,0},{2,3},{3,2},{4,5},{5,4},{6,7},{7,6},{8,9},{9,8},{10,11... | collective-permute-start | bytes 786440 | tf_op jit(solution)/shard_map/ppermute | solution.py:25
  109.8 12.8 %collective-permute-start.12 = (bf16[3,32,16,128]{3,2,1,0:T(8,128)(2,1)}, bf16[3,32,16,128]{3,2,1,0:T(8,128)(2,1)S(1)}, u32[]{:S(2)}, u32[]{:S(2)}) collective-permute-start(bf16[3,32,16,128]{3,2,1,0:T(8,128)(2,1)} %get-tuple-element.20), channel_id=1, source_target_pairs={{0,1},{1,0},{2,3},{3,2},{4,5},{5,4},{6,7},{7,6},{8,9},{9,8},{10,11... | collective-permute-start | bytes 1179656 | tf_op jit(solution)/shard_map/ppermute | solution.py:25
  115.5 2.5 %copy-start.10 = (bf16[2,32,16,128]{3,2,1,0:T(8,128)(2,1)S(1)}, bf16[2,32,16,128]{3,2,1,0:T(8,128)(2,1)}, u32[]{:S(2)}) copy-start(bf16[2,32,16,128]{3,2,1,0:T(8,128)(2,1)} %get-tuple-element.17) | copy-start | bytes 786436
  115.5 15.3 %collective-permute-start.13 = (bf16[3,32,16,128]{3,2,1,0:T(8,128)(2,1)}, bf16[3,32,16,128]{3,2,1,0:T(8,128)(2,1)S(1)}, u32[]{:S(2)}, u32[]{:S(2)}) collective-permute-start(bf16[3,32,16,128]{3,2,1,0:T(8,128)(2,1)} %get-tuple-element.22), channel_id=1, source_target_pairs={{0,1},{1,0},{2,3},{3,2},{4,5},{5,4},{6,7},{7,6},{8,9},{9,8},{10,11... | collective-permute-start | bytes 1179656 | tf_op jit(solution)/shard_map/ppermute | solution.py:25
  117.6 1.0 copy-start.9
  118.0 4.7 %copy-start.8 = (bf16[3,32,16,128]{3,2,1,0:T(8,128)(2,1)S(1)}, bf16[3,32,16,128]{3,2,1,0:T(8,128)(2,1)}, u32[]{:S(2)}) copy-start(bf16[3,32,16,128]{3,2,1,0:T(8,128)(2,1)} %get-tuple-element.21) | copy-start | bytes 1179652
  122.8 8.0 %copy-start.5 = (bf16[16,32,16,128]{3,2,1,0:T(8,128)(2,1)}, bf16[16,32,16,128]{3,2,1,0:T(8,128)(2,1)S(1)}, u32[]{:S(2)}) copy-start(bf16[16,32,16,128]{3,2,1,0:T(8,128)(2,1)S(1)} %constant_dynamic-update-slice_fusion.4) | copy-start | bytes 6291460

commit v4 on v3

--- a/solution.py
+++ b/solution.py
@@ -5,7 +5,7 @@
 from jax.experimental.pallas import tpu as pltpu
 from jax.sharding import PartitionSpec as P
 
-PARTS = (2, 3, 3)
+PARTS = (3, 5)
 FAR = 4
 NEAR = 2
 SPREAD = FAR + NEAR
@@ -101,9 +101,10 @@
 
     few = mine // 2
     other_a = to_partner(lax.dynamic_slice_in_dim(grad_out, other_at, few, 0))
-    gate_top = from_before(pre_act[:, rows - NEAR :], "row")
+    late, gate_last = lax.optimization_barrier((grad_out, pre_act[:, rows - NEAR :]))
+    gate_top = from_before(gate_last, "row")
     gate_bottom = from_after(pre_act[:, :NEAR], "row")
-    other_b = to_partner(lax.dynamic_slice_in_dim(grad_out, other_at + few, few, 0))
+    other_b = to_partner(lax.dynamic_slice_in_dim(late, other_at + few, few, 0))
     gate = jnp.concatenate([gate_top, pre_act, gate_bottom], axis=1)
     own = lax.dynamic_slice_in_dim(grad_out, own_at, mine, 0)
     first_weight = relative_weight(weight_two, part)
@@ -112,10 +113,9 @@
     top = from_before(both[:, rows - SPREAD :], "row")
     bottom = from_after(both[:, :SPREAD], "row")
     gate_other = to_partner(lax.dynamic_slice_in_dim(gate, other_at, mine, 0))
-    last = [piece[:, :, cols - FAR :] for piece in (top, both, bottom)]
-    left = from_before(jnp.concatenate(last, axis=1), "col")
-    head = [piece[:, :, :FAR] for piece in (top, both, bottom)]
-    right = from_after(jnp.concatenate(head, axis=1), "col")
+    tall = jnp.concatenate([top, both, bottom], axis=1)
+    left = from_before(tall[:, :, cols - FAR :], "col")
+    right = from_after(tall[:, :, :FAR], "col")
 
     tall_rows = rows + 2 * SPREAD
     gate_rows = rows + 2 * NEAR

time: 133 us -> 136 us (1.023)
  waiting for transfers between devices: 44.2 us -> 52.1 us
  starting transfers between devices: 36.6 us -> 34.2 us
  other arithmetic: 8 us -> 5.84 us
  Pallas kernels: 25 us -> 23.2 us
  local copies, waits for them, and re-layouts: 17.4 us -> 19 us
    ppermute x6 -> x5, waiting for transfers between devices: 13.5 us -> 18.1 us  [to_partner(): return lax.ppermute(x, 'filt', [(0, 1), (1, 0)])]
    ppermute x4, waiting for transfers between devices: 20.6 us -> 25.2 us  [from_before(): return lax.ppermute(x, axis, [(i, i + 1) for i in range(count - 1)])]
    ppermute x6 -> x5, starting transfers between devices: 9.15 us -> 6.57 us  [to_partner(): return lax.ppermute(x, 'filt', [(0, 1), (1, 0)])]
    pallas_call x3 -> x2, Pallas kernels: 13.3 us -> 11.5 us  [on_device(): pl.pallas_call(second_kernel, out_shape=(jax.ShapeDtypeStruct((size, rows...]
    slice x2, local copies, waits for them, and re-layouts: 1.57 us -> 0.16 us  [relative_weight(): swapped = jnp.roll(weight, (half, half), (2, 3))]
    dynamic_slice x1, local copies, waits for them, and re-layouts: 0.18 us -> 1.56 us  [on_device(): own = lax.dynamic_slice_in_dim(grad_out, own_at, mine, 0)]
    dynamic_slice x1 -> x2, local copies, waits for them, and re-layouts: 2.43 us -> 3.73 us  [the longest x1 1.87 us: on_device(): other_a = to_partner(lax.dynamic_slice_in_dim(grad_out, other_at, few, 0))]
    unnamed x32 -> x38, local copies, waits for them, and re-layouts: 4.41 us -> 5.62 us
  transfers between devices with their start and end apart: 14 -> 13, of which waited for: 8 -> 9; matrix products, arithmetic and copies ran while one was open for 15% -> 12% of each run, Pallas kernels for 7% -> 4%
where the time goes in v4:
time: 136 us; the launch traced here: 135 us
  waiting for transfers between devices  52.1 us (38%)
  starting transfers between devices  34.2 us (25%)
  Pallas kernels  23.2 us (17%)
  local copies, waits for them, and re-layouts  19 us (14%)
  other arithmetic  5.84 us (4%)
    ppermute x4, waiting for transfers between devices, from_before(): return lax.ppermute(x, axis, [(i, i + 1) for i in range(count - 1)])  25.2 us
    ppermute x5, waiting for transfers between devices, to_partner(): return lax.ppermute(x, 'filt', [(0, 1), (1, 0)])  18.1 us
    ppermute x4, starting transfers between devices, from_after(): return lax.ppermute(x, axis, [(i + 1, i) for i in range(count - 1)])  14 us
    ppermute x4, starting transfers between devices, from_before(): return lax.ppermute(x, axis, [(i, i + 1) for i in range(count - 1)])  13.6 us
    pallas_call x1, Pallas kernels, on_device(): pl.pallas_call(first_kernel, out_shape=(jax.ShapeDtypeStruct((mine, gate_...  11.7 us
    pallas_call x2, Pallas kernels, on_device(): pl.pallas_call(second_kernel, out_shape=(jax.ShapeDtypeStruct((size, rows...  11.5 us
    ppermute x4, waiting for transfers between devices, from_after(): return lax.ppermute(x, axis, [(i + 1, i) for i in range(count - 1)])  8.87 us
    ppermute x5, starting transfers between devices, to_partner(): return lax.ppermute(x, 'filt', [(0, 1), (1, 0)])  6.57 us
  transfers between devices with their start and end apart: 13, of which 9 were waited for; matrix products, arithmetic and copies ran while one was open for 12% of the time, Pallas kernels for 4%

profile of v4, /device:TPU:9, one launch (start us, length us, event | category | flops | bytes accessed | tf_op | source)
XLA Modules:
  0.0 134.6 jit_solution(15524078131658429208)
XLA Ops:
  0.0 1.8 %fusion.6 = (bf16[16,2,16,128]{3,2,1,0:T(8,128)(2,1)}, bf16[16,2,16,128]{3,2,1,0:T(8,128)(2,1)}) fusion(bf16[16,32,16,128]{3,2,1,0:T(8,128)(2,1)} %param.5), kind=kLoop, calls=%fused_computation.33 | loop fusion | bytes 524288 | tf_op jit(solution)/shard_map/slice | solution.py:106
  1.8 1.9 %constant_dynamic-slice_fusion.2 = bf16[4,32,16,128]{3,2,1,0:T(8,128)(2,1)} fusion(bf16[16,32,16,128]{3,2,1,0:T(8,128)(2,1)} %own.1, s32[]{:T(128)S(6)} %select_n.31), kind=kLoop, calls=%fused_computation.31 | loop fusion | bytes 1048580 | tf_op jit(solution)/shard_map/dynamic_slice | solution.py:107
  3.6 3.6 %collective-permute-start.1 = (bf16[4,32,16,128]{3,2,1,0:T(8,128)(2,1)}, bf16[4,32,16,128]{3,2,1,0:T(8,128)(2,1)S(1)}, u32[]{:S(2)}, u32[]{:S(2)}) collective-permute-start(bf16[4,32,16,128]{3,2,1,0:T(8,128)(2,1)} %constant_dynamic-slice_fusion.2), channel_id=1, source_target_pairs={{0,1},{1,0},{2,3},{3,2},{4,5},{5,4},{6,7},{7,6},{8,9},{9,8},{10,11... | collective-permute-start | bytes 1572872 | tf_op jit(solution)/shard_map/ppermute | solution.py:25
  7.2 1.9 %constant_dynamic-slice_fusion.3 = bf16[4,32,16,128]{3,2,1,0:T(8,128)(2,1)} fusion(bf16[16,32,16,128]{3,2,1,0:T(8,128)(2,1)} %own.1, s32[]{:T(128)S(6)} %select_n.30), kind=kLoop, calls=%fused_computation.32 | loop fusion | bytes 1048580 | tf_op jit(solution)/shard_map/dynamic_slice | solution.py:103
  9.1 4.0 %collective-permute-start.6 = (bf16[16,2,16,128]{3,2,1,0:T(8,128)(2,1)}, bf16[16,2,16,128]{3,2,1,0:T(8,128)(2,1)}, u32[]{:S(2)}, u32[]{:S(2)}) collective-permute-start(bf16[16,2,16,128]{3,2,1,0:T(8,128)(2,1)} %get-tuple-element.15), channel_id=1, source_target_pairs={{0,32},{32,64},{64,96},{1,33},{33,65},{65,97},{2,34},{34,66},{66,9... | collective-permute-start | bytes 393224 | tf_op jit(solution)/shard_map/ppermute | solution.py:16
  13.1 1.9 %collective-permute-start.7 = (bf16[16,2,16,128]{3,2,1,0:T(8,128)(2,1)}, bf16[16,2,16,128]{3,2,1,0:T(8,128)(2,1)S(1)}, u32[]{:S(2)}, u32[]{:S(2)}) collective-permute-start(bf16[16,2,16,128]{3,2,1,0:T(8,128)(2,1)} %get-tuple-element.25), channel_id=1, source_target_pairs={{32,0},{64,32},{96,64},{33,1},{65,33},{97,65},{34,2},{66,34},{98,6... | collective-permute-start | bytes 393224 | tf_op jit(solution)/shard_map/ppermute | solution.py:21
  15.2 1.6 %constant_dynamic-slice_fusion.1 = bf16[8,32,16,128]{3,2,1,0:T(8,128)(2,1)S(1)} fusion(bf16[16,32,16,128]{3,2,1,0:T(8,128)(2,1)} %own.1, s32[]{:T(128)S(6)} %select_n.32), kind=kLoop, calls=%fused_computation.30 | loop fusion | bytes 2097156 | tf_op jit(solution)/shard_map/dynamic_slice | solution.py:109
  16.8 15.2 %collective-permute-done.6 = bf16[16,2,16,128]{3,2,1,0:T(8,128)(2,1)} collective-permute-done((bf16[16,2,16,128]{3,2,1,0:T(8,128)(2,1)}, bf16[16,2,16,128]{3,2,1,0:T(8,128)(2,1)}, u32[]{:S(2)}, u32[]{:S(2)}) %collective-permute-start.6) | collective-permute-done | bytes 131104 | tf_op jit(solution)/shard_map/ppermute | solution.py:16
  31.9 0.9 constant_dynamic-update-slice_fusion.2
  32.9 0.5 constant_dynamic-update-slice_fusion.1
  33.5 0.1 pad_maximum_fusion.7
  33.6 0.6 copy-done.7
  34.3 0.2 copy-done.9
  34.4 4.5 %collective-permute-start.2 = (bf16[8,6,16,256]{3,2,1,0:T(8,128)(2,1)S(1)}, bf16[8,6,16,256]{3,2,1,0:T(8,128)(2,1)S(1)}, u32[]{:S(2)}, u32[]{:S(2)}) collective-permute-start(bf16[8,6,16,256]{3,2,1,0:T(8,128)(2,1)S(1)} %get-tuple-element.28), channel_id=1, source_target_pairs={{0,32},{32,64},{64,96},{1,33},{33,65},{65,97},{2,34},{34,66},{66,9... | collective-permute-start | bytes 1179656 | tf_op jit(solution)/shard_map/ppermute | solution.py:16
  39.0 1.9 %collective-permute-start.3 = (bf16[8,6,16,256]{3,2,1,0:T(8,128)(2,1)S(1)}, bf16[8,6,16,256]{3,2,1,0:T(8,128)(2,1)S(1)}, u32[]{:S(2)}, u32[]{:S(2)}) collective-permute-start(bf16[8,6,16,256]{3,2,1,0:T(8,128)(2,1)S(1)} %get-tuple-element.27), channel_id=1, source_target_pairs={{32,0},{64,32},{96,64},{33,1},{65,33},{97,65},{34,2},{66,34},{98,6... | collective-permute-start | bytes 1179656 | tf_op jit(solution)/shard_map/ppermute | solution.py:21
  40.9 1.2 constant_dynamic-slice_fusion
  42.2 3.5 %collective-permute-done.2.top = bf16[8,6,16,256]{3,2,1,0:T(8,128)(2,1)S(1)} collective-permute-done((bf16[8,6,16,256]{3,2,1,0:T(8,128)(2,1)S(1)}, bf16[8,6,16,256]{3,2,1,0:T(8,128)(2,1)S(1)}, u32[]{:S(2)}, u32[]{:S(2)}) %collective-permute-start.2) | collective-permute-done | bytes 393248 | tf_op jit(solution)/shard_map/ppermute | solution.py:16
  45.7 7.0 %collective-permute-done.3.bottom = bf16[8,6,16,256]{3,2,1,0:T(8,128)(2,1)S(1)} collective-permute-done((bf16[8,6,16,256]{3,2,1,0:T(8,128)(2,1)S(1)}, bf16[8,6,16,256]{3,2,1,0:T(8,128)(2,1)S(1)}, u32[]{:S(2)}, u32[]{:S(2)}) %collective-permute-start.3) | collective-permute-done | bytes 393248 | tf_op jit(solution)/shard_map/ppermute | solution.py:21
  52.7 3.1 %pad_maximum_fusion.2 = (bf16[8,44,4,256]{3,2,1,0:T(4,128)(2,1)}, bf16[8,44,4,256]{3,2,1,0:T(4,128)(2,1)}) fusion(bf16[8,6,16,256]{3,2,1,0:T(8,128)(2,1)S(1)} %collective-permute-done.3.bottom, bf16[8,6,16,256]{3,2,1,0:T(8,128)(2,1)S(1)} %collective-permute-done.2.top, bf16[8,32,16,128]{3,2,1,0:T(8,128)(2,1)S(1)} %constant_dynamic-slice_fusion.1, ...), kind=kLoop, calls=%fused_computation.12 | loop fusion | flops 7208960 | bytes 4325376 | tf_op jit(solution)/shard_map/concatenate | solution.py:116
  55.8 3.1 %collective-permute-start.4 = (bf16[8,44,4,256]{3,2,1,0:T(4,128)(2,1)}, bf16[8,44,4,256]{3,2,1,0:T(4,128)(2,1)}, u32[]{:S(2)}, u32[]{:S(2)}) collective-permute-start(bf16[8,44,4,256]{3,2,1,0:T(4,128)(2,1)} %get-tuple-element.24), channel_id=1, source_target_pairs={{0,2},{2,4},{4,6},{6,8},{8,10},{10,12},{12,14},{14,16},{16,18},{18... | collective-permute-start | bytes 2162696 | tf_op jit(solution)/shard_map/ppermute | solution.py:16
  58.9 4.3 %collective-permute-start.5 = (bf16[8,44,4,256]{3,2,1,0:T(4,128)(2,1)}, bf16[8,44,4,256]{3,2,1,0:T(4,128)(2,1)}, u32[]{:S(2)}, u32[]{:S(2)}) collective-permute-start(bf16[8,44,4,256]{3,2,1,0:T(4,128)(2,1)} %get-tuple-element.23), channel_id=1, source_target_pairs={{2,0},{4,2},{6,4},{8,6},{10,8},{12,10},{14,12},{16,14},{18,16},{20... | collective-permute-start | bytes 2162696 | tf_op jit(solution)/shard_map/ppermute | solution.py:21
  63.2 0.9 fusion.4
  64.1 0.1 fusion.5
  64.2 1.2 copy-done.2
  65.4 0.1 copy-done.5
  65.5 1.6 %fusion.1 = (bf16[3,3,256,256]{3,2,1,0:T(8,128)(2,1)}, bf16[3,3,256,256]{3,2,1,0:T(8,128)(2,1)S(1)}) fusion(bf16[3,3,256,256]{3,2,1,0:T(8,128)(2,1)S(1)} %copy-done, bf16[3,3,128,256]{3,2,1,0:T(8,128)(2,1)S(1)} %get-tuple-element.30, bf16[3,3,128,256]{3,2,1,0:T(8,128)(2,1)S(1)} %get-tuple-element.29, bf16[3,3,256,128]{3,2,1,0:T(8,128)(2,1)S(1)} %copy-done.5, ...), kind=kLoop, calls=%fused_computation.2 | loop fusion | flops 8257536 | bytes 8257537 | tf_op jit(solution)/shard_map/jit(_where)/select_n | solution.py:33
  67.1 0.1 reverse_bitcast_fusion.1
  67.2 1.6 %copy.5 = bf16[3,3,256,256]{3,2,1,0:T(8,128)(2,1)} copy(bf16[3,3,256,256]{2,3,1,0:T(8,128)(2,1)S(1)} %reverse_bitcast_fusion.1) | data formatting | bytes 2359296 | tf_op jit(solution)/shard_map/transpose | solution.py:34
  68.8 0.7 collective-permute-done.8.gate_other
  69.5 0.7 collective-permute-done.4.left
  70.2 1.5 %collective-permute-done.5.right = bf16[8,44,4,256]{3,2,1,0:T(4,128)(2,1)} collective-permute-done((bf16[8,44,4,256]{3,2,1,0:T(4,128)(2,1)}, bf16[8,44,4,256]{3,2,1,0:T(4,128)(2,1)}, u32[]{:S(2)}, u32[]{:S(2)}) %collective-permute-start.5) | collective-permute-done | bytes 720928 | tf_op jit(solution)/shard_map/ppermute | solution.py:21
  71.7 11.7 %first.1 = (bf16[8,36,16,256]{3,2,1,0:T(8,128)(2,1)}, bf16[8,36,2,256]{3,2,1,0:T(2,128)(2,1)}, bf16[8,36,2,256]{3,2,1,0:T(2,128)(2,1)}) custom-call(s32[1]{0:T(128)} %bitcast.part_ref, bf16[16,32,16,128]{3,2,1,0:T(8,128)(2,1)} %own.1, bf16[4,32,16,128]{3,2,1,0:T(8,128)(2,1)} %copy-done.9, bf16[4,32,16,128]{3,2,1,0:T(8,128)(2,1)} %copy-done.7, ...), custom_call_target="tpu_custom_call" | custom-call | flops 5435817984 | bytes 8388608 | tf_op jit(solution)/shard_map/first/pallas_call | solution.py:133
  83.4 5.9 %collective-permute-start.10 = (bf16[8,36,2,256]{3,2,1,0:T(2,128)(2,1)}, bf16[8,36,2,256]{3,2,1,0:T(2,128)(2,1)S(1)}, u32[]{:S(2)}, u32[]{:S(2)}) collective-permute-start(bf16[8,36,2,256]{3,2,1,0:T(2,128)(2,1)} %get-tuple-element.18), channel_id=1, source_target_pairs={{2,0},{4,2},{6,4},{8,6},{10,8},{12,10},{14,12},{16,14},{18,16},{20... | collective-permute-start | bytes 884744 | tf_op jit(solution)/shard_map/ppermute | solution.py:21
  89.3 1.9 %collective-permute-start.9 = (bf16[8,36,2,256]{3,2,1,0:T(2,128)(2,1)}, bf16[8,36,2,256]{3,2,1,0:T(2,128)(2,1)S(1)}, u32[]{:S(2)}, u32[]{:S(2)}) collective-permute-start(bf16[8,36,2,256]{3,2,1,0:T(2,128)(2,1)} %get-tuple-element.17), channel_id=1, source_target_pairs={{0,2},{2,4},{4,6},{6,8},{8,10},{10,12},{12,14},{14,16},{16,18},{18... | collective-permute-start | bytes 884744 | tf_op jit(solution)/shard_map/ppermute | solution.py:16
  91.3 0.1 reverse_bitcast_fusion
  91.3 1.5 %copy.6 = bf16[3,3,256,256]{3,2,1,0:T(8,128)(2,1)} copy(bf16[3,3,256,256]{2,3,1,0:T(8,128)(2,1)S(1)} %reverse_bitcast_fusion) | data formatting | bytes 2359296 | tf_op jit(solution)/shard_map/transpose | solution.py:34
  92.9 0.4 collective-permute-done.10.right
  93.3 5.8 %collective-permute-done.9.left = bf16[8,36,2,256]{3,2,1,0:T(2,128)(2,1)S(1)} collective-permute-done((bf16[8,36,2,256]{3,2,1,0:T(2,128)(2,1)}, bf16[8,36,2,256]{3,2,1,0:T(2,128)(2,1)S(1)}, u32[]{:S(2)}, u32[]{:S(2)}) %collective-permute-start.9) | collective-permute-done | bytes 294944 | tf_op jit(solution)/shard_map/ppermute | solution.py:16
  99.1 0.7 copy-done.17
  99.8 6.7 %second.3 = (bf16[5,32,16,128]{3,2,1,0:T(8,128)(2,1)}, bf16[5,32,16,128]{3,2,1,0:T(8,128)(2,1)}) custom-call(bf16[8,36,16,256]{3,2,1,0:T(8,128)(2,1)} %get-tuple-element.16.grad_h, bf16[8,36,2,256]{3,2,1,0:T(2,128)(2,1)} %copy-done.17, bf16[8,36,2,256]{3,2,1,0:T(2,128)(2,1)} %copy-done.16, bf16[3,768,256]{2,1,0:T(8,128)(2,1)} %bitcast.8), custom_call_target="tpu_custom_call" | custom-call | flops 3019898880 | bytes 5242880 | tf_op jit(solution)/shard_map/second/pallas_call | solution.py:181
  106.5 1.7 %collective-permute-start.12 = (bf16[5,32,16,128]{3,2,1,0:T(8,128)(2,1)}, bf16[5,32,16,128]{3,2,1,0:T(8,128)(2,1)S(1)}, u32[]{:S(2)}, u32[]{:S(2)}) collective-permute-start(bf16[5,32,16,128]{3,2,1,0:T(8,128)(2,1)} %get-tuple-element.22), channel_id=1, source_target_pairs={{0,1},{1,0},{2,3},{3,2},{4,5},{5,4},{6,7},{7,6},{8,9},{9,8},{10,11... | collective-permute-start | bytes 1966088 | tf_op jit(solution)/shard_map/ppermute | solution.py:25
  108.2 4.8 %second.2 = (bf16[3,32,16,128]{3,2,1,0:T(8,128)(2,1)}, bf16[3,32,16,128]{3,2,1,0:T(8,128)(2,1)}) custom-call(bf16[8,36,16,256]{3,2,1,0:T(8,128)(2,1)} %get-tuple-element.16.grad_h, bf16[8,36,2,256]{3,2,1,0:T(2,128)(2,1)} %copy-done.17, bf16[8,36,2,256]{3,2,1,0:T(2,128)(2,1)} %copy-done.16, bf16[3,768,256]{2,1,0:T(8,128)(2,1)} %bitcast.9), custom_call_target="tpu_custom_call" | custom-call | flops 1811939328 | bytes 3145728 | tf_op jit(solution)/shard_map/second/pallas_call | solution.py:181
  113.0 1.3 collective-permute-start.11
  114.3 0.4 broadcast_in_dim.3
  114.8 17.3 %collective-permute-done.11 = bf16[3,32,16,128]{3,2,1,0:T(8,128)(2,1)S(1)} collective-permute-done((bf16[3,32,16,128]{3,2,1,0:T(8,128)(2,1)}, bf16[3,32,16,128]{3,2,1,0:T(8,128)(2,1)S(1)}, u32[]{:S(2)}, u32[]{:S(2)}) %collective-permute-start.11) | collective-permute-done | bytes 393248 | tf_op jit(solution)/shard_map/ppermute | solution.py:25
  132.2 0.2 constant_dynamic-update-slice_fusion.4
  132.4 1.3 copy-done.6
  133.7 0.9 constant_dynamic-update-slice_fusion.3
  (41 shorter events, 0.4 us)
Async XLA Ops:
  0.0 15.1 %copy-start = (bf16[3,3,256,256]{3,2,1,0:T(8,128)(2,1)S(1)}, bf16[3,3,256,256]{3,2,1,0:T(8,128)(2,1)}, u32[]{:S(2)}) copy-start(bf16[3,3,256,256]{3,2,1,0:T(8,128)(2,1)} %param.6) | copy-start | bytes 3538948
  3.6 29.8 %collective-permute-start.1 = (bf16[4,32,16,128]{3,2,1,0:T(8,128)(2,1)}, bf16[4,32,16,128]{3,2,1,0:T(8,128)(2,1)S(1)}, u32[]{:S(2)}, u32[]{:S(2)}) collective-permute-start(bf16[4,32,16,128]{3,2,1,0:T(8,128)(2,1)} %constant_dynamic-slice_fusion.2), channel_id=1, source_target_pairs={{0,1},{1,0},{2,3},{3,2},{4,5},{5,4},{6,7},{7,6},{8,9},{9,8},{10,11... | collective-permute-start | bytes 1572872 | tf_op jit(solution)/shard_map/ppermute | solution.py:25
  9.1 24.3 %collective-permute-start = (bf16[4,32,16,128]{3,2,1,0:T(8,128)(2,1)}, bf16[4,32,16,128]{3,2,1,0:T(8,128)(2,1)S(1)}, u32[]{:S(2)}, u32[]{:S(2)}) collective-permute-start(bf16[4,32,16,128]{3,2,1,0:T(8,128)(2,1)} %constant_dynamic-slice_fusion.3), channel_id=1, source_target_pairs={{0,1},{1,0},{2,3},{3,2},{4,5},{5,4},{6,7},{7,6},{8,9},{9,8},{10,11... | collective-permute-start | bytes 1572872 | tf_op jit(solution)/shard_map/ppermute | solution.py:25
  9.1 22.8 %collective-permute-start.6 = (bf16[16,2,16,128]{3,2,1,0:T(8,128)(2,1)}, bf16[16,2,16,128]{3,2,1,0:T(8,128)(2,1)}, u32[]{:S(2)}, u32[]{:S(2)}) collective-permute-start(bf16[16,2,16,128]{3,2,1,0:T(8,128)(2,1)} %get-tuple-element.15), channel_id=1, source_target_pairs={{0,32},{32,64},{64,96},{1,33},{33,65},{65,97},{2,34},{34,66},{66,9... | collective-permute-start | bytes 393224 | tf_op jit(solution)/shard_map/ppermute | solution.py:16
  13.1 20.2 %collective-permute-start.7 = (bf16[16,2,16,128]{3,2,1,0:T(8,128)(2,1)}, bf16[16,2,16,128]{3,2,1,0:T(8,128)(2,1)S(1)}, u32[]{:S(2)}, u32[]{:S(2)}) collective-permute-start(bf16[16,2,16,128]{3,2,1,0:T(8,128)(2,1)} %get-tuple-element.25), channel_id=1, source_target_pairs={{32,0},{64,32},{96,64},{33,1},{65,33},{97,65},{34,2},{66,34},{98,6... | collective-permute-start | bytes 393224 | tf_op jit(solution)/shard_map/ppermute | solution.py:21
  15.2 17.7 %copy-start.4 = (bf16[16,32,16,128]{3,2,1,0:T(8,128)(2,1)S(1)}, bf16[16,32,16,128]{3,2,1,0:T(8,128)(2,1)}, u32[]{:S(2)}) copy-start(bf16[16,32,16,128]{3,2,1,0:T(8,128)(2,1)} %param.5) | copy-start | bytes 6291460
  33.4 22.3 %copy-start.11 = (bf16[16,36,16,128]{3,2,1,0:T(8,128)(2,1)}, bf16[16,36,16,128]{3,2,1,0:T(8,128)(2,1)S(1)}, u32[]{:S(2)}) copy-start(bf16[16,36,16,128]{3,2,1,0:T(8,128)(2,1)S(1)} %constant_dynamic-update-slice_fusion.gate_own) | copy-start | bytes 7077892
  33.4 0.8 copy-start.7
  33.5 1.0 copy-start.9
  34.4 7.7 %copy-start.1 = (bf16[3,3,256,256]{3,2,1,0:T(8,128)(2,1)S(1)}, bf16[3,3,256,256]{3,2,1,0:T(8,128)(2,1)}, u32[]{:S(2)}) copy-start(bf16[3,3,256,256]{3,2,1,0:T(8,128)(2,1)} %param.7) | copy-start | bytes 3538948
  34.4 11.2 %collective-permute-start.2 = (bf16[8,6,16,256]{3,2,1,0:T(8,128)(2,1)S(1)}, bf16[8,6,16,256]{3,2,1,0:T(8,128)(2,1)S(1)}, u32[]{:S(2)}, u32[]{:S(2)}) collective-permute-start(bf16[8,6,16,256]{3,2,1,0:T(8,128)(2,1)S(1)} %get-tuple-element.28), channel_id=1, source_target_pairs={{0,32},{32,64},{64,96},{1,33},{33,65},{65,97},{2,34},{34,66},{66,9... | collective-permute-start | bytes 1179656 | tf_op jit(solution)/shard_map/ppermute | solution.py:16
  39.0 13.7 %collective-permute-start.3 = (bf16[8,6,16,256]{3,2,1,0:T(8,128)(2,1)S(1)}, bf16[8,6,16,256]{3,2,1,0:T(8,128)(2,1)S(1)}, u32[]{:S(2)}, u32[]{:S(2)}) collective-permute-start(bf16[8,6,16,256]{3,2,1,0:T(8,128)(2,1)S(1)} %get-tuple-element.27), channel_id=1, source_target_pairs={{32,0},{64,32},{96,64},{33,1},{65,33},{97,65},{34,2},{66,34},{98,6... | collective-permute-start | bytes 1179656 | tf_op jit(solution)/shard_map/ppermute | solution.py:21
  42.1 10.6 %copy-start.8 = (bf16[4,32,16,128]{3,2,1,0:T(8,128)(2,1)S(1)}, bf16[4,32,16,128]{3,2,1,0:T(8,128)(2,1)}, u32[]{:S(2)}) copy-start(bf16[4,32,16,128]{3,2,1,0:T(8,128)(2,1)} %copy-done.7) | copy-start | bytes 1572868
  42.1 10.6 %copy-start.10 = (bf16[4,32,16,128]{3,2,1,0:T(8,128)(2,1)S(1)}, bf16[4,32,16,128]{3,2,1,0:T(8,128)(2,1)}, u32[]{:S(2)}) copy-start(bf16[4,32,16,128]{3,2,1,0:T(8,128)(2,1)} %copy-done.9) | copy-start | bytes 1572868
  42.1 27.4 %collective-permute-start.8 = (bf16[8,36,16,128]{3,2,1,0:T(8,128)(2,1)}, bf16[8,36,16,128]{3,2,1,0:T(8,128)(2,1)}, u32[]{:S(2)}, u32[]{:S(2)}) collective-permute-start(bf16[8,36,16,128]{3,2,1,0:T(8,128)(2,1)} %constant_dynamic-slice_fusion), channel_id=1, source_target_pairs={{0,1},{1,0},{2,3},{3,2},{4,5},{5,4},{6,7},{7,6},{8,9},{9,8},{10,11... | collective-permute-start | bytes 3538952 | tf_op jit(solution)/shard_map/ppermute | solution.py:25
  45.7 10.1 %copy-start.13 = (bf16[8,6,16,256]{3,2,1,0:T(8,128)(2,1)}, bf16[8,6,16,256]{3,2,1,0:T(8,128)(2,1)S(1)}, u32[]{:S(2)}) copy-start(bf16[8,6,16,256]{3,2,1,0:T(8,128)(2,1)S(1)} %collective-permute-done.2.top) | copy-start | bytes 1179652
  52.7 3.1 %copy-start.14 = (bf16[8,6,16,256]{3,2,1,0:T(8,128)(2,1)}, bf16[8,6,16,256]{3,2,1,0:T(8,128)(2,1)S(1)}, u32[]{:S(2)}) copy-start(bf16[8,6,16,256]{3,2,1,0:T(8,128)(2,1)S(1)} %collective-permute-done.3.bottom) | copy-start | bytes 1179652
  55.8 14.5 %collective-permute-start.4 = (bf16[8,44,4,256]{3,2,1,0:T(4,128)(2,1)}, bf16[8,44,4,256]{3,2,1,0:T(4,128)(2,1)}, u32[]{:S(2)}, u32[]{:S(2)}) collective-permute-start(bf16[8,44,4,256]{3,2,1,0:T(4,128)(2,1)} %get-tuple-element.24), channel_id=1, source_target_pairs={{0,2},{2,4},{4,6},{6,8},{8,10},{10,12},{12,14},{14,16},{16,18},{18... | collective-permute-start | bytes 2162696 | tf_op jit(solution)/shard_map/ppermute | solution.py:16
  58.9 12.8 %collective-permute-start.5 = (bf16[8,44,4,256]{3,2,1,0:T(4,128)(2,1)}, bf16[8,44,4,256]{3,2,1,0:T(4,128)(2,1)}, u32[]{:S(2)}, u32[]{:S(2)}) collective-permute-start(bf16[8,44,4,256]{3,2,1,0:T(4,128)(2,1)} %get-tuple-element.23), channel_id=1, source_target_pairs={{2,0},{4,2},{6,4},{8,6},{10,8},{12,10},{14,12},{16,14},{18,16},{20... | collective-permute-start | bytes 2162696 | tf_op jit(solution)/shard_map/ppermute | solution.py:21
  64.1 1.3 copy-start.2
  64.1 1.4 %copy-start.5 = (bf16[3,3,256,128]{3,2,1,0:T(8,128)(2,1)S(1)}, bf16[3,3,256,128]{3,2,1,0:T(8,128)(2,1)}, u32[]{:S(2)}) copy-start(bf16[3,3,256,128]{3,2,1,0:T(8,128)(2,1)} %fusion.4) | copy-start | bytes 1769476
  71.7 19.5 %copy-start.3 = (bf16[3,3,256,256]{3,2,1,0:T(8,128)(2,1)S(1)}, bf16[3,3,256,256]{3,2,1,0:T(8,128)(2,1)}, u32[]{:S(2)}) copy-start(bf16[3,3,256,256]{3,2,1,0:T(8,128)(2,1)} %get-tuple-element.33) | copy-start | bytes 3538948
  83.4 9.9 %collective-permute-start.10 = (bf16[8,36,2,256]{3,2,1,0:T(2,128)(2,1)}, bf16[8,36,2,256]{3,2,1,0:T(2,128)(2,1)S(1)}, u32[]{:S(2)}, u32[]{:S(2)}) collective-permute-start(bf16[8,36,2,256]{3,2,1,0:T(2,128)(2,1)} %get-tuple-element.18), channel_id=1, source_target_pairs={{2,0},{4,2},{6,4},{8,6},{10,8},{12,10},{14,12},{16,14},{18,16},{20... | collective-permute-start | bytes 884744 | tf_op jit(solution)/shard_map/ppermute | solution.py:21
  89.3 9.8 %collective-permute-start.9 = (bf16[8,36,2,256]{3,2,1,0:T(2,128)(2,1)}, bf16[8,36,2,256]{3,2,1,0:T(2,128)(2,1)S(1)}, u32[]{:S(2)}, u32[]{:S(2)}) collective-permute-start(bf16[8,36,2,256]{3,2,1,0:T(2,128)(2,1)} %get-tuple-element.17), channel_id=1, source_target_pairs={{0,2},{2,4},{4,6},{6,8},{8,10},{10,12},{12,14},{14,16},{16,18},{18... | collective-permute-start | bytes 884744 | tf_op jit(solution)/shard_map/ppermute | solution.py:16
  93.3 5.8 %copy-start.16 = (bf16[8,36,2,256]{3,2,1,0:T(2,128)(2,1)}, bf16[8,36,2,256]{3,2,1,0:T(2,128)(2,1)S(1)}, u32[]{:S(2)}) copy-start(bf16[8,36,2,256]{3,2,1,0:T(2,128)(2,1)S(1)} %collective-permute-done.10.right) | copy-start | bytes 884740
  99.1 0.7 copy-start.17
  106.5 25.8 %collective-permute-start.12 = (bf16[5,32,16,128]{3,2,1,0:T(8,128)(2,1)}, bf16[5,32,16,128]{3,2,1,0:T(8,128)(2,1)S(1)}, u32[]{:S(2)}, u32[]{:S(2)}) collective-permute-start(bf16[5,32,16,128]{3,2,1,0:T(8,128)(2,1)} %get-tuple-element.22), channel_id=1, source_target_pairs={{0,1},{1,0},{2,3},{3,2},{4,5},{5,4},{6,7},{7,6},{8,9},{9,8},{10,11... | collective-permute-start | bytes 1966088 | tf_op jit(solution)/shard_map/ppermute | solution.py:25
  113.0 1.7 %copy-start.15 = (bf16[3,32,16,128]{3,2,1,0:T(8,128)(2,1)S(1)}, bf16[3,32,16,128]{3,2,1,0:T(8,128)(2,1)}, u32[]{:S(2)}) copy-start(bf16[3,32,16,128]{3,2,1,0:T(8,128)(2,1)} %get-tuple-element.19) | copy-start | bytes 1179652
  113.0 19.1 %collective-permute-start.11 = (bf16[3,32,16,128]{3,2,1,0:T(8,128)(2,1)}, bf16[3,32,16,128]{3,2,1,0:T(8,128)(2,1)S(1)}, u32[]{:S(2)}, u32[]{:S(2)}) collective-permute-start(bf16[3,32,16,128]{3,2,1,0:T(8,128)(2,1)} %get-tuple-element.20), channel_id=1, source_target_pairs={{0,1},{1,0},{2,3},{3,2},{4,5},{5,4},{6,7},{7,6},{8,9},{9,8},{10,11... | collective-permute-start | bytes 1179656 | tf_op jit(solution)/shard_map/ppermute | solution.py:25
  114.3 17.9 %copy-start.12 = (bf16[5,32,16,128]{3,2,1,0:T(8,128)(2,1)S(1)}, bf16[5,32,16,128]{3,2,1,0:T(8,128)(2,1)}, u32[]{:S(2)}) copy-start(bf16[5,32,16,128]{3,2,1,0:T(8,128)(2,1)} %get-tuple-element.21) | copy-start | bytes 1966084
  132.3 1.3 copy-start.6
